TPU v7x, 128 devices: a whole 4x4x4 slice. The times are simulated.
128 devices in a mesh: gx: 4 (over z), gy: 4 (over y), gz: 8 (over x, core).
Axes of the slice: x: 4, y: 4, z: 4, core: 2. Of those that a mesh axis runs over, the one named last changes fastest.
Arguments:
- features: bfloat16 [32768, 1024], P(('gx', 'gy', 'gz')), may hold values from -6 to 6
- cotangent: bfloat16 [32768, 1024], P(('gx', 'gy', 'gz')), may hold values from -6 to 6
- leaf_device: int32 [32768, 1], P(('gx', 'gy', 'gz')), may hold values from 0 to 127; in each aligned block of 256 rows (0 to 255, 256 to 511, ...) at most 4 rows name the same one
- neighbours: int32 [16, 65536], P(None, ('gx', 'gy', 'gz')), may hold values from 0 to 511
- radial: float32 [64, 65536], P(None, ('gx', 'gy', 'gz')), may hold values from 0.25 to 2
- first_zero: bfloat16 [256, 256], replicated, may hold values from -0.375 to 0.375
- first_one: bfloat16 [192, 192], replicated, may hold values from -0.4375 to 0.4375
- first_two: bfloat16 [128, 128], replicated, may hold values from -0.5 to 0.5
- first_three: bfloat16 [64, 64], replicated, may hold values from -0.75 to 0.75
- second_zero: bfloat16 [256, 256], replicated, may hold values from -0.375 to 0.375
- second_one: bfloat16 [192, 192], replicated, may hold values from -0.4375 to 0.4375
- second_two: bfloat16 [128, 128], replicated, may hold values from -0.5 to 0.5
- second_three: bfloat16 [64, 64], replicated, may hold values from -0.75 to 0.75
- lift_leaf: float32 [8, 16, 16], replicated, may hold values from -0.5 to 0.5
- lift_branch: float32 [4, 16, 16], replicated, may hold values from -0.75 to 0.75
- couple_root: float32 [4, 4, 16, 16], replicated, may hold values from -0.75 to 0.75
- couple_branch: float32 [4, 4, 16, 16], replicated, may hold values from -0.75 to 0.75
- couple_leaf: float32 [8, 8, 16, 16], replicated, may hold values from -0.5 to 0.5
Outputs:
- updated: bfloat16 [32768, 1024], P(('gx', 'gy', 'gz'))
- radial_grad: float32 [64, 65536], P(None, ('gx', 'gy', 'gz'))
Inputs may be any that keep to these rules, and one draw needn't show every extreme that they name: `leaf_device`: among the 256 atoms of one brick at most 4 have the same leaf; every leaf holds at least one atom.
All inputs are finite; a program needn't handle non-finite values.
Results may differ from a plain program's by a relative error of at most 0.0037.
Values may be sent and summed in bfloat16 or wider, within the bound.
No kernel may reach another device: no remote copies, remote signals or barrier semaphores. Data moves between devices by JAX's collectives and lax.ppermute only.
A program may use at most 64 MiB of HBM per device.

v0:
```python
import math

import jax
import jax.numpy as jnp
import numpy as np
from jax import lax
from jax.sharding import PartitionSpec as P

DEGREES = (0, 1, 2, 3, 1, 2, 3, 1, 2, 3, 2, 3, 2, 3, 3, 3)
BLOCKS = ((0, 4, 0), (4, 7, 1), (7, 10, 1), (10, 12, 2), (12, 14, 2), (14, 15, 3), (15, 16, 3))


def degree_table(chans):
    table = np.zeros((4, 16 * chans), dtype=np.float32)
    for coef, degree in enumerate(DEGREES):
        table[degree, coef * chans : (coef + 1) * chans] = 1.0
    return jnp.asarray(table)


def mixing(values, mats, flip):
    chans = mats[3].shape[0]
    outs = []
    for first, last, which in BLOCKS:
        piece = values[:, first * chans : last * chans]
        weight = mats[which]
        if flip:
            result = lax.dot_general(
                piece, weight, (((1,), (1,)), ((), ())), preferred_element_type=jnp.float32
            )
        else:
            result = jnp.dot(piece, weight, preferred_element_type=jnp.float32)
        outs.append(result)
    return jnp.concatenate(outs, axis=1)


def shards(
    features,
    cotangent,
    leaf_device,
    neighbours,
    radial,
    first_zero,
    first_one,
    first_two,
    first_three,
    second_zero,
    second_one,
    second_two,
    second_three,
    lift_leaf,
    lift_branch,
    couple_root,
    couple_branch,
    couple_leaf,
):
    hp = lax.Precision.HIGHEST
    rows, width = features.shape
    chans = width // 16
    size_x = lax.axis_size("gx")
    size_y = lax.axis_size("gy")
    size_z = lax.axis_size("gz")
    devices = size_x * size_y * size_z
    pool = neighbours.shape[1]
    cap = pool // devices
    target = leaf_device[:, 0]
    onehot = (target[:, None] == jnp.arange(devices, dtype=jnp.int32)[None, :]).astype(jnp.int32)
    rank = jnp.sum(jnp.cumsum(onehot, axis=0) * onehot, axis=1) - 1
    slot = target * cap + rank
    send_feat = jnp.zeros((pool, width), jnp.bfloat16).at[slot].set(features)
    send_grad = jnp.zeros((pool, width), jnp.bfloat16).at[slot].set(cotangent)
    send_mask = jnp.zeros((pool,), jnp.bfloat16).at[slot].set(jnp.ones((rows,), jnp.bfloat16))
    flat_shape = (devices, cap * width)
    got_feat, got_grad, got_mask = (
        lax.all_to_all(
            send_feat.reshape(flat_shape),
            ("gx", "gy", "gz"),
            split_axis=0,
            concat_axis=0,
            tiled=True,
        ),
        lax.all_to_all(
            send_grad.reshape(flat_shape),
            ("gx", "gy", "gz"),
            split_axis=0,
            concat_axis=0,
            tiled=True,
        ),
        lax.all_to_all(
            send_mask.reshape(devices, cap),
            ("gx", "gy", "gz"),
            split_axis=0,
            concat_axis=0,
            tiled=True,
        ),
    )
    pool_feat = got_feat.reshape(pool, width)
    pool_grad = got_grad.reshape(pool, width)
    occ_int = got_mask.reshape(pool).astype(jnp.int32)
    occ = occ_int.astype(jnp.float32)
    order = jnp.argsort(1 - occ_int, stable=True)
    filled = jnp.sum(occ_int)
    leaf = jnp.sum(pool_feat, axis=0, dtype=jnp.float32).reshape(16, chans) / math.sqrt(rows)
    index_x = lax.axis_index("gx")
    index_y = lax.axis_index("gy")
    index_z = lax.axis_index("gz")
    sib_leaf = lax.all_gather(leaf[None], "gz", axis=0, tiled=True)
    middle = jnp.einsum("kpq,kqc->pc", lift_leaf, sib_leaf, precision=hp)
    sib_branch = lax.all_gather(middle[None], "gy", axis=0, tiled=True)
    topmost = jnp.einsum("kpq,kqc->pc", lift_branch, sib_branch, precision=hp)
    sib_root = lax.all_gather(topmost[None], "gx", axis=0, tiled=True)
    root_mask = couple_root * (1.0 - jnp.eye(size_x, dtype=jnp.float32))[:, :, None, None]
    branch_mask = couple_branch * (1.0 - jnp.eye(size_y, dtype=jnp.float32))[:, :, None, None]
    leaf_mask = couple_leaf * (1.0 - jnp.eye(size_z, dtype=jnp.float32))[:, :, None, None]
    local1 = jnp.einsum("jpq,jqc->pc", root_mask[index_x], sib_root, precision=hp)
    local2 = jnp.einsum("qp,qc->pc", lift_branch[index_y], local1, precision=hp) + jnp.einsum(
        "jpq,jqc->pc", branch_mask[index_y], sib_branch, precision=hp
    )
    local3 = jnp.einsum("qp,qc->pc", lift_leaf[index_z], local2, precision=hp) + jnp.einsum(
        "jpq,jqc->pc", leaf_mask[index_z], sib_leaf, precision=hp
    )
    firsts = (first_zero, first_one, first_two, first_three)
    seconds = (second_zero, second_one, second_two, second_three)
    table = degree_table(chans)
    trans = mixing(pool_grad, seconds, True)
    feat = pool_feat.astype(jnp.float32)

    def step(carry, item):
        choose, rad4 = item
        index = order[choose % filled]
        other = pool_feat[index]
        summed = feat + other.astype(jnp.float32)
        expand = lax.dot_general(rad4, table, (((0,), (0,)), ((), ())), precision=hp)
        zeta = (summed * expand).astype(jnp.bfloat16)
        upper = mixing(zeta, firsts, False)
        value = jax.nn.silu(upper).astype(jnp.bfloat16)
        message = mixing(value, seconds, False)
        sig = jax.nn.sigmoid(upper)
        grad_u = (sig * (1.0 + upper * (1.0 - sig)) * trans).astype(jnp.bfloat16)
        back = mixing(grad_u, firsts, True)
        dradial = (
            0.25
            * occ[None, :]
            * lax.dot_general(table, back * summed, (((1,), (1,)), ((), ())), precision=hp)
        )
        return (carry + message, dradial)

    near, grads = lax.scan(
        step, jnp.zeros((pool, width), jnp.float32), (neighbours, radial.reshape(-1, 4, pool))
    )
    near = 0.25 * occ[:, None] * near
    pool_out = (feat + near + feat * local3.reshape(1, width)).astype(jnp.bfloat16)
    returned = lax.all_to_all(
        pool_out.reshape(flat_shape), ("gx", "gy", "gz"), split_axis=0, concat_axis=0, tiled=True
    )
    updated = returned.reshape(pool, width)[slot]
    return (updated, grads.reshape(-1, pool))


def solution(mesh):
    placed = (
        P(("gx", "gy", "gz"), None),
        P(("gx", "gy", "gz"), None),
        P(("gx", "gy", "gz"), None),
        P(None, ("gx", "gy", "gz")),
        P(None, ("gx", "gy", "gz")),
        P(),
        P(),
        P(),
        P(),
        P(),
        P(),
        P(),
        P(),
        P(),
        P(),
        P(),
        P(),
        P(),
    )
    return jax.shard_map(
        shards,
        mesh=mesh,
        in_specs=placed,
        out_specs=(P(("gx", "gy", "gz"), None), P(None, ("gx", "gy", "gz"))),
        check_vma=False,
    )
```

profile of v0, /device:TPU:0, one launch (start us, length us, event | category | flops | bytes accessed | tf_op | source)
XLA Modules:
  0.0 868.3 jit_solution(5397576052168979461)
XLA Ops:
  6.3 11.2 %all-to-all-start.1 = ((bf16[128,1,4]{2,1,0:T(2,128)(2,1)}), bf16[128,1,4]{2,1,0:T(2,128)(2,1)S(1)}, u32[]{:S(2)}, u32[]{:S(2)}) async-start(bf16[128,1,4]{2,1,0:T(2,128)(2,1)} %all_to_all.33), calls=%async_computation.1 | async-start | bytes 131072 | tf_op jit(solution)/shard_map/all_to_all | solution.py:88
  21.3 7.0 reduce.13
  29.9 9.8 %all-to-all-start = ((bf16[128,2,2048]{2,1,0:T(2,128)(2,1)}), bf16[128,2,2048]{2,1,0:T(2,128)(2,1)S(1)}, u32[]{:S(2)}, u32[]{:S(2)}) async-start(bf16[128,2,2048]{2,1,0:T(2,128)(2,1)} %reshape.263), calls=%async_computation | async-start | bytes 2097152 | tf_op jit(solution)/shard_map/all_to_all | solution.py:74
  42.9 4.2 all_to_all.34
  47.1 8.0 reduce.14
  58.8 10.3 %all-to-all-start.2 = ((bf16[128,2,2048]{2,1,0:T(2,128)(2,1)}), bf16[128,2,2048]{2,1,0:T(2,128)(2,1)}, u32[]{:S(2)}, u32[]{:S(2)}) async-start(bf16[128,2,2048]{2,1,0:T(2,128)(2,1)} %reshape.265), calls=%async_computation.2 | async-start | bytes 2097152 | tf_op jit(solution)/shard_map/all_to_all | solution.py:81
  77.1 6.5 reshape.264
  83.6 7.7 reduce.2
  94.0 7.6 reshape.266
  101.7 8.7 %reduce.5 = bf16[128,4096]{1,0:T(8,128)(2,1)} reduce(bf16[128,1,4096]{2,1,0:T(2,128)(2,1)} %reshape.266, bf16[]{:T(256)} %constant.92), dimensions={1}, to_apply=%all_to_all.29.reduce_sub_computation | reduce | bytes 2097154 | tf_op jit(solution)/shard_map/all_to_all | solution.py:81
  119.0 652.3 %while.16 = (s32[]{:T(128)}, f32[512,1024]{0,1:T(8,128)}, f32[16,4,512]{2,1,0:T(4,128)}, s32[16,512]{1,0:T(8,128)}, s32[]{:T(128)}, /*index=5*/pred[]{:T(512)}, ...) while((s32[]{:T(128)}, f32[512,1024]{0,1:T(8,128)}, ...), condition=%wide.region_9.10_spmd.clone.clone, body=%wide.region_8.9_spmd.sunk.clone.clone.sunk | while | flops 614476800 | bytes 52811160 | solution.py:147
  144.6 4.7 fusion.223
  184.8 4.7 fusion.223
  225.6 4.7 fusion.223
  262.3 4.1 concatenate.29
  266.4 4.7 fusion.223
  303.1 4.1 concatenate.29
  307.2 4.7 fusion.223
  343.9 4.1 concatenate.29
  348.0 4.7 fusion.223
  384.7 4.1 concatenate.29
  388.8 4.7 fusion.223
  425.5 4.1 concatenate.29
  429.6 4.7 fusion.223
  466.3 4.1 concatenate.29
  470.4 4.7 fusion.223
  507.1 4.1 concatenate.29
  511.2 4.7 fusion.223
  547.9 4.1 concatenate.29
  552.0 4.7 fusion.223
  588.7 4.1 concatenate.29
  592.8 4.7 fusion.223
  629.5 4.1 concatenate.29
  633.6 4.7 fusion.223
  670.3 4.1 concatenate.29
  674.4 4.7 fusion.223
  711.1 4.1 concatenate.29
  715.2 4.7 fusion.223
  751.9 4.1 concatenate.29
  756.0 4.7 fusion.223
  773.4 12.7 %all_gather.9 = f32[8,16,64]{2,1,0:T(8,128)S(1)} all-gather(f32[1,16,64]{2,1,0:T(8,128)S(1)} %div.17), channel_id=1, replica_groups=mesh['gx'=4,'gy'=4,'gz'=8] {'gz'}, dimensions={0}, use_global_device_ids=true | all-gather | bytes 36864 | tf_op jit(solution)/shard_map/all_gather | solution.py:106
  786.5 12.1 %all-gather = f32[64,64]{1,0:T(8,128)S(1)} all-gather(f32[16,64]{1,0:T(8,128)S(1)} %convolution_bitcast_fusion.4), channel_id=2, replica_groups=mesh['gx'=4,'gy'=4,'gz'=8] {'gy'}, dimensions={0}, use_global_device_ids=true | all-gather | bytes 20480 | tf_op jit(solution)/shard_map/all_gather | solution.py:108
  798.8 12.8 %all-gather.1 = f32[64,64]{1,0:T(8,128)S(1)} all-gather(f32[16,64]{1,0:T(8,128)S(1)} %convolution_bitcast_fusion.3), channel_id=3, replica_groups=mesh['gx'=4,'gy'=4,'gz'=8] {'gx'}, dimensions={0}, use_global_device_ids=true | all-gather | bytes 20480 | tf_op jit(solution)/shard_map/all_gather | solution.py:110
  816.9 4.4 all_to_all.35
  821.3 7.0 reduce.15
  829.9 8.6 all-to-all-start.3
  839.3 18.4 %all-to-all-done.3 = bf16[128,2,2048]{2,1,0:T(2,128)(2,1)S(1)} async-done(((bf16[128,2,2048]{2,1,0:T(2,128)(2,1)}), bf16[128,2,2048]{2,1,0:T(2,128)(2,1)S(1)}, u32[]{:S(2)}, u32[]{:S(2)}) %all-to-all-start.3) | async-done | bytes 1048608 | tf_op jit(solution)/shard_map/all_to_all | solution.py:152
  858.7 6.4 reduce.6
  (827 shorter events, 571.2 us)
Async XLA Ops:
  0.6 785.6 %copy-start = (f32[8,16,16]{2,1,0:T(8,128)S(1)}, f32[8,16,16]{2,1,0:T(8,128)}, u32[]{:S(2)}) copy-start(f32[8,16,16]{2,1,0:T(8,128)} %param.34) | copy-start | bytes 24580
  3.3 36.4 %copy-start.21 = (s32[256,1]{0,1:T(1,128)}, s32[256,1]{0,1:T(1,128)S(1)}, u32[]{:S(2)}) copy-start(s32[256,1]{0,1:T(1,128)S(1)} %compare_select_fusion.2) | copy-start | bytes 3076
  6.3 23.6 %all-to-all-start.1 = ((bf16[128,1,4]{2,1,0:T(2,128)(2,1)}), bf16[128,1,4]{2,1,0:T(2,128)(2,1)S(1)}, u32[]{:S(2)}, u32[]{:S(2)}) async-start(bf16[128,1,4]{2,1,0:T(2,128)(2,1)} %all_to_all.33), calls=%async_computation.1 | async-start | bytes 131072 | tf_op jit(solution)/shard_map/all_to_all | solution.py:88
  29.9 28.9 %all-to-all-start = ((bf16[128,2,2048]{2,1,0:T(2,128)(2,1)}), bf16[128,2,2048]{2,1,0:T(2,128)(2,1)S(1)}, u32[]{:S(2)}, u32[]{:S(2)}) async-start(bf16[128,2,2048]{2,1,0:T(2,128)(2,1)} %reshape.263), calls=%async_computation | async-start | bytes 2097152 | tf_op jit(solution)/shard_map/all_to_all | solution.py:74
  47.0 10.7 %copy-start.16 = (f32[64,512]{1,0:T(8,128)S(1)}, f32[64,512]{1,0:T(8,128)}, u32[]{:S(2)}) copy-start(f32[64,512]{1,0:T(8,128)} %param.25) | copy-start | bytes 393220
  58.8 17.8 %copy-start.13 = (bf16[128,2,2048]{2,1,0:T(2,128)(2,1)}, bf16[128,2,2048]{2,1,0:T(2,128)(2,1)S(1)}, u32[]{:S(2)}) copy-start(bf16[128,2,2048]{2,1,0:T(2,128)(2,1)S(1)} %all-to-all-done) | copy-start | bytes 3145732
  58.8 35.3 %all-to-all-start.2 = ((bf16[128,2,2048]{2,1,0:T(2,128)(2,1)}), bf16[128,2,2048]{2,1,0:T(2,128)(2,1)}, u32[]{:S(2)}, u32[]{:S(2)}) async-start(bf16[128,2,2048]{2,1,0:T(2,128)(2,1)} %reshape.265), calls=%async_computation.2 | async-start | bytes 2097152 | tf_op jit(solution)/shard_map/all_to_all | solution.py:81
  112.9 6.1 copy-start.4
  112.9 6.1 copy-start.6
  144.6 4.7 copy-start.1
  149.3 5.0 copy-start.15
  184.8 4.7 copy-start.1
  189.5 5.0 copy-start.15
  225.5 4.7 copy-start.1
  230.3 5.0 copy-start.15
  266.3 4.7 copy-start.1
  271.1 5.0 copy-start.15
  307.1 4.7 copy-start.1
  311.9 5.0 copy-start.15
  347.9 4.7 copy-start.1
  352.7 5.0 copy-start.15
  388.7 4.7 copy-start.1
  393.5 5.0 copy-start.15
  429.5 4.7 copy-start.1
  434.3 5.0 copy-start.15
  470.3 4.7 copy-start.1
  475.1 5.0 copy-start.15
  511.1 4.7 copy-start.1
  515.9 5.0 copy-start.15
  551.9 4.7 copy-start.1
  556.7 5.0 copy-start.15
  592.7 4.7 copy-start.1
  597.5 5.0 copy-start.15
  633.5 4.7 copy-start.1
  638.3 5.0 copy-start.15
  674.3 4.7 copy-start.1
  679.1 5.0 copy-start.15
  715.1 4.7 copy-start.1
  719.9 5.0 copy-start.15
  760.7 5.0 copy-start.15
  771.4 27.2 %copy-start.18 = (f32[4,16,16]{2,1,0:T(8,128)S(1)}, f32[4,16,16]{2,1,0:T(8,128)}, u32[]{:S(2)}) copy-start(f32[4,16,16]{2,1,0:T(8,128)} %param.35) | copy-start | bytes 12292
  771.4 40.2 %copy-start.24 = (f32[1,4]{1,0:T(1,128)S(1)}, f32[1,4]{1,0:T(1,128)}, u32[]{:S(2)}) copy-start(f32[1,4]{1,0:T(1,128)} %get-tuple-element.430) | copy-start | bytes 52
  771.4 41.2 %copy-start.23 = (f32[1,4]{1,0:T(1,128)S(1)}, f32[1,4]{1,0:T(1,128)}, u32[]{:S(2)}) copy-start(f32[1,4]{1,0:T(1,128)} %get-tuple-element.429) | copy-start | bytes 52
  771.4 42.5 %copy-start.25 = (f32[1,8]{1,0:T(1,128)S(1)}, f32[1,8]{1,0:T(1,128)}, u32[]{:S(2)}) copy-start(f32[1,8]{1,0:T(1,128)} %constant_dynamic-slice_fusion) | copy-start | bytes 100
  771.4 44.0 %copy-start.20 = (f32[512]{0:T(512)S(1)}, f32[512]{0:T(512)}, u32[]{:S(2)}) copy-start(f32[512]{0:T(512)} %broadcast_multiply_fusion.2) | copy-start | bytes 6148
  828.3 10.2 %copy-start.22 = (s32[256,1]{0,1:T(1,128)S(1)}, s32[256,1]{0,1:T(1,128)}, u32[]{:S(2)}) copy-start(s32[256,1]{0,1:T(1,128)} %copy-done.21) | copy-start | bytes 3076
  828.3 10.3 %copy-start.17 = (f32[16,4,512]{2,1,0:T(4,128)S(1)}, f32[16,4,512]{2,1,0:T(4,128)}, u32[]{:S(2)}) copy-start(f32[16,4,512]{2,1,0:T(4,128)} %get-tuple-element.238) | copy-start | bytes 393220
  829.9 27.7 %all-to-all-start.3 = ((bf16[128,2,2048]{2,1,0:T(2,128)(2,1)}), bf16[128,2,2048]{2,1,0:T(2,128)(2,1)S(1)}, u32[]{:S(2)}, u32[]{:S(2)}) async-start(bf16[128,2,2048]{2,1,0:T(2,128)(2,1)} %reshape.267), calls=%async_computation.3 | async-start | bytes 2097152 | tf_op jit(solution)/shard_map/all_to_all | solution.py:152
  (87 other events, 215.8 us)
where the time goes:
time: 881 us; the launch traced here: 868 us
  matrix products  383 us (43%)
  local copies, waits for them, and re-layouts  219 us (25%)
  other arithmetic  164 us (19%)
  starting transfers between devices  39.9 us (5%)
  blocking collectives  37.6 us (4%)
  waiting for transfers between devices  18.8 us (2%)
    dot_general x224, matrix products, mixing(): result = jnp.dot(piece, weight, preferred_element_type=jnp.float32)  135 us
    dot_general x119, matrix products, mixing(): lax.dot_general(piece, weight, (((1,), (1,)), ((), ())), preferred_elemen...  117 us
    dot_general x16, matrix products, step(): lax.dot_general(table, back * summed, (((1,), (1,)), ((), ())), precision...  75.4 us
    concatenate x16, local copies, waits for them, and re-layouts, mixing(): return jnp.concatenate(outs, axis=1)  64.9 us
    add x16, other arithmetic, step(): return (carry + message, dradial)  63.5 us
    gather x16, local copies, waits for them, and re-layouts, step(): index = order[choose % filled]  55.9 us
    dot_general x16, matrix products, step(): lax.dot_general(rad4, table, (((0,), (0,)), ((), ())), precision=hp)  51.5 us
    gather x16, local copies, waits for them, and re-layouts, step(): other = pool_feat[index]  44.7 us
  transfers between devices with their start and end apart: 4, of which 2 were waited for; matrix products, arithmetic and copies ran while one was open for 6% of the time, Pallas kernels for 0%

commit v1 on v0

v1 whole, which is shorter than its diff:
```python
import math

import jax
import jax.numpy as jnp
import numpy as np
from jax import lax
from jax.experimental import pallas as pl
from jax.experimental.pallas import tpu as pltpu
from jax.sharding import PartitionSpec as P

BF16 = jnp.bfloat16
F32 = jnp.float32
HIGHEST = lax.Precision.HIGHEST
AXES = ("gx", "gy", "gz")
EMPTY = 1024.0
ROWS = 256
POOL = 512
WIDTH = 1024
NBR = 16
TILE = 256


def dot(a, b, **kw):
    return jnp.dot(a, b, preferred_element_type=F32, **kw)


def iota(shape, axis):
    return lax.broadcasted_iota(jnp.int32, shape, axis)


def row_of(col):
    n = col.shape[0]
    diag = jnp.where(iota((n, n), 0) == iota((n, n), 1), col.astype(F32), 0.0).astype(BF16)
    return dot(jnp.ones((8, n), BF16), diag)[0:1, :].astype(jnp.int32)


def pack_kernel(leaf_ref, feat_ref, grad_ref, send_ref):
    col = leaf_ref[...]
    row = row_of(col)
    n = ROWS
    same = (col == row) & (iota((n, n), 0) < iota((n, n), 1))
    rank = jnp.sum(jnp.where(same, 1.0, 0.0), axis=0, keepdims=True).astype(jnp.int32)
    slot = row * 8 + rank
    ones = jnp.ones((n, 128), BF16)
    for part in range(4):
        index = iota((n, n), 0) + part * n
        pick_f = jnp.where(index == slot, 1.0, 0.0).astype(BF16)
        pick_g = jnp.where(index == slot + 4, 1.0, 0.0).astype(BF16)
        there = dot(pick_f, ones)
        gone = (there < 0.5) & ((iota((n, 128), 0) & 7) < 4)
        out = dot(pick_f, feat_ref[...]) + dot(pick_g, grad_ref[...])
        send_ref[part * n : (part + 1) * n, 128:] = out[:, 128:].astype(BF16)
        send_ref[part * n : (part + 1) * n, :128] = jnp.where(gone, EMPTY, out[:, :128]).astype(BF16)


def pack(leaf_device, features, cotangent):
    return pl.pallas_call(
        pack_kernel,
        out_shape=jax.ShapeDtypeStruct((128 * 8, WIDTH), BF16),
        name="pack",
    )(leaf_device, features, cotangent)


def mix(x, w0, w1a, w1b, w2, w3):
    a = dot(x[:, 0:256], w0)
    b = dot(x[:, 256:512], w1a)
    c = dot(x[:, 384:640], w1b)
    d = dot(x[:, 640:896], w2)
    e = dot(x[:, 896:1024], w3)
    return [
        a[:, :128],
        a[:, 128:],
        b[:, :128],
        b[:, 128:] + c[:, :128],
        c[:, 128:],
        d[:, :128],
        d[:, 128:],
        e,
    ]


def gather_rows(perm_ref, m_ref, fc_ref, rows, k):
    size = rows.size
    shifted = pltpu.roll(m_ref[rows, :], (128 - k) % 128, 1)
    pick = jnp.broadcast_to(shifted[:, 0:1], (size, POOL))
    own = perm_ref[rows, :]
    hot = jnp.where(iota((size, POOL), 1).astype(F32) == pick, own + 1.0, own)
    return dot(hot.astype(BF16), fc_ref[...])


def scales(rad_ref, rows, k):
    size = rows.size
    shifted = pltpu.roll(rad_ref[rows, :], (128 - 4 * k) % 128, 1)
    r0, r1, r2, r3 = [jnp.broadcast_to(shifted[:, j : j + 1], (size, 128)) for j in range(4)]
    low = iota((size, 128), 1) < 64
    p01 = jnp.where(low, r0, r1)
    p23 = jnp.where(low, r2, r3)
    p12 = jnp.where(low, r1, r2)
    p31 = jnp.where(low, r3, r1)
    return [p01, p23, p12, p31, p23, p23, p23, r3]


def leaf_a_kernel(
    got_ref,
    nbr_ref,
    rad_ref,
    f0, f1a, f1b, f2, f3,
    s0, s1a, s1b, s2, s3,
    t0, t1a, t1b, t2, t3,
    gu_ref,
    back_ref,
    fc_ref,
    perm_ref,
    m_ref,
    acc_ref,
    half_t_ref,
):
    k = pl.program_id(0)

    @pl.when(k == 0)
    def _():
        first = jnp.where(iota((8, 128), 1) == 0, 1.0, 0.0).astype(BF16)
        got0 = got_ref[:, :, :, 0:128].reshape(1024, 128)
        lead = lax.dot_general(first, got0, (((1,), (1,)), ((), ())), preferred_element_type=F32)
        lane = iota((8, 1024), 1)
        occ = jnp.where((lead < 0.5 * EMPTY) & ((lane & 7) < 4), 1.0, 0.0)
        filled = jnp.sum(occ[0:1, :], axis=1, keepdims=True)
        before = jnp.where(iota((1024, 1024), 0) < iota((1024, 1024), 1), 1.0, 0.0).astype(BF16)
        rank = dot(occ.astype(BF16), before)
        rank = jnp.where(occ > 0.5, rank, -1.0)
        compact = jnp.where(iota((POOL, 1024), 0).astype(F32) == rank[0:1, :], 1.0, 0.0).astype(BF16)
        got = got_ref[...].reshape(1024, WIDTH)
        fc_ref[...] = dot(compact, got).astype(BF16)
        slot = iota((POOL, 1024), 0)
        where_from = (slot >> 2) * 8 + (slot & 3)
        pick = jnp.where(iota((POOL, 1024), 1) == where_from, 1.0, 0.0).astype(BF16)
        perm_ref[...] = lax.dot_general(
            pick, compact, (((1,), (1,)), ((), ())), preferred_element_type=F32
        )
        pick_t = jnp.where(iota((POOL, 1024), 1) == where_from + 4, 1.0, 0.0).astype(BF16)
        grad = dot(pick_t, got).astype(BF16)
        mixed = mix(grad, t0[...], t1a[...], t1b[...], t2[...], t3[...])
        half_t_ref[...] = 0.5 * jnp.concatenate(mixed, axis=1)
        choice = nbr_ref[...].astype(F32)
        turns = jnp.floor(choice / filled)
        left = choice - turns * filled
        left = jnp.where(left < 0.0, left + filled, left)
        m_ref[...] = jnp.where(left >= filled, left - filled, left)
        acc_ref[...] = jnp.zeros_like(acc_ref)

    for part in range(POOL // TILE):
        rows = pl.ds(part * TILE, TILE)
        y = gather_rows(perm_ref, m_ref, fc_ref, rows, k)
        pats = scales(rad_ref, rows, k)
        z = jnp.concatenate([(y[:, g * 128 : (g + 1) * 128] * pats[g]).astype(BF16) for g in range(8)], axis=1)
        w = mix(z, f0[...], f1a[...], f1b[...], f2[...], f3[...])
        for g in range(8):
            cols = slice(g * 128, (g + 1) * 128)
            h = jnp.tanh(w[g])
            up = 1.0 + h
            v = w[g] * up
            acc_ref[rows, cols] += v
            gu_ref[0, rows, cols] = ((up + v * (1.0 - h)) * half_t_ref[rows, cols]).astype(BF16)

    @pl.when(k == NBR - 1)
    def _():
        total = acc_ref[...]
        high = total.astype(BF16)
        low = (total - high.astype(F32)).astype(BF16)
        wts = (s0[...], s1a[...], s1b[...], s2[...], s3[...])
        near = [0.25 * (a + b) for a, b in zip(mix(high, *wts), mix(low, *wts))]
        half = iota((64, 8, 512), 1) < 4
        lo = jnp.concatenate(near[:4], axis=1)
        hi = jnp.concatenate(near[4:], axis=1)
        lo_r = pltpu.roll(lo.reshape(64, 8, 512), 4, 1)
        hi_r = pltpu.roll(hi.reshape(64, 8, 512), 4, 1)
        lo = lo.reshape(64, 8, 512)
        hi = hi.reshape(64, 8, 512)
        back_ref[:, 0, :, :512] = jnp.where(half, lo, hi_r).astype(BF16)
        back_ref[:, 1, :, :512] = jnp.where(half, lo_r, hi).astype(BF16)
        tile = jnp.sum(fc_ref[...].astype(F32), axis=0, keepdims=True) / math.sqrt(ROWS)
        body = jnp.concatenate([tile[:, r * 128 : (r + 1) * 128] for r in range(8)], axis=0)
        body = jnp.broadcast_to(body[None, None], (64, 2, 8, 128)).astype(BF16)
        back_ref[:, :, :, 512:] = body


def leaf_a(got, nbr, rad, firsts, seconds, trans):
    full = lambda x: pl.BlockSpec(x.shape, lambda k, n=len(x.shape): (0,) * n)
    args = (got, nbr, rad, *firsts, *seconds, *trans)
    return pl.pallas_call(
        leaf_a_kernel,
        grid=(NBR,),
        in_specs=[full(x) for x in args],
        out_specs=[
            pl.BlockSpec((1, POOL, WIDTH), lambda k: (k, 0, 0)),
            pl.BlockSpec((64, 2, 8, 640), lambda k: (0, 0, 0, 0)),
            pl.BlockSpec((POOL, WIDTH), lambda k: (0, 0)),
            pl.BlockSpec((POOL, POOL), lambda k: (0, 0)),
            pl.BlockSpec((POOL, 128), lambda k: (0, 0)),
        ],
        out_shape=[
            jax.ShapeDtypeStruct((NBR, POOL, WIDTH), BF16),
            jax.ShapeDtypeStruct((64, 2, 8, 640), BF16),
            jax.ShapeDtypeStruct((POOL, WIDTH), BF16),
            jax.ShapeDtypeStruct((POOL, POOL), F32),
            jax.ShapeDtypeStruct((POOL, 128), F32),
        ],
        scratch_shapes=[pltpu.VMEM((POOL, WIDTH), F32), pltpu.VMEM((POOL, WIDTH), F32)],
        compiler_params=pltpu.CompilerParams(vmem_limit_bytes=56 << 20),
        cost_estimate=pl.CostEstimate(flops=12 << 30, bytes_accessed=24 << 20, transcendentals=8 << 20),
        name="leaf_a",
    )(*args)


PATTERN = ((0, 1), (2, 3), (1, 2), (3, 1), (3, 3))


def leaf_b_kernel(gu_ref, fc_ref, perm_ref, m_ref, t0, t1a, t1b, t2, t3, table_ref, out_ref, acc_ref):
    k = pl.program_id(0)

    @pl.when(k == 0)
    def _():
        acc_ref[...] = jnp.zeros_like(acc_ref)

    for part in range(POOL // TILE):
        rows = pl.ds(part * TILE, TILE)
        y = gather_rows(perm_ref, m_ref, fc_ref, rows, k)
        s = mix(gu_ref[0, rows, :], t0[...], t1a[...], t1b[...], t2[...], t3[...])
        p = [s[g] * y[:, g * 128 : (g + 1) * 128] for g in range(8)]
        q = jnp.concatenate([p[0], (p[1] + p[4]) + (p[5] + p[6]), p[2], p[3], p[7]], axis=1)
        high = q.astype(BF16)
        low = (q - high.astype(F32)).astype(BF16)
        sums = dot(high, table_ref[...]) + dot(low, table_ref[...])
        mine = (iota((TILE, 128), 1) >> 2) == k
        acc_ref[rows, :] += jnp.where(mine, sums, 0.0)

    @pl.when(k == NBR - 1)
    def _():
        occ = dot(perm_ref[...].astype(BF16), jnp.ones((POOL, 128), BF16))
        out_ref[...] = jnp.transpose(0.5 * occ * acc_ref[...])[0:64, :]


def leaf_b(gu, fc, perm, m, trans, table):
    full = lambda x: pl.BlockSpec(x.shape, lambda k, n=len(x.shape): (0,) * n)
    args = (fc, perm, m, *trans, table)
    return pl.pallas_call(
        leaf_b_kernel,
        grid=(NBR,),
        in_specs=[pl.BlockSpec((1, POOL, WIDTH), lambda k: (k, 0, 0))] + [full(x) for x in args],
        out_specs=pl.BlockSpec((64, POOL), lambda k: (0, 0)),
        out_shape=jax.ShapeDtypeStruct((64, POOL), F32),
        scratch_shapes=[pltpu.VMEM((POOL, 128), F32)],
        compiler_params=pltpu.CompilerParams(vmem_limit_bytes=40 << 20),
        cost_estimate=pl.CostEstimate(flops=12 << 30, bytes_accessed=24 << 20, transcendentals=0),
        name="leaf_b",
    )(gu, *args)


def block_swap(tiles):
    low = iota((8, 128), 1) < 64
    out = [[None] * 8 for _ in range(16)]
    for pair in range(8):
        for g in range(8):
            a, b = tiles[2 * pair][g], tiles[2 * pair + 1][g]
            out[2 * g][pair] = jnp.where(low, a, pltpu.roll(b, 64, 1))
            out[2 * g + 1][pair] = jnp.where(low, pltpu.roll(a, 64, 1), b)
    return out


def own_block(x):
    which = (iota((16, 1024), 1) >> 6) & 3
    out = x[0:16]
    for b in range(1, 4):
        out = jnp.where(which == b, x[b * 16 : (b + 1) * 16], out)
    return out


def finish_kernel(ret_ref, feat_ref, leaf_ref, up2_ref, up1_ref, root_ref, mid_ref, low_ref, out_ref, tile_ref):
    tile_ref[...] = ret_ref[:, 512:640].astype(F32)
    tiles = [[tile_ref[pl.ds(ab * 64 + g, 8, stride=8), :] for g in range(8)] for ab in range(16)]
    swapped = block_swap(tiles)
    s2 = jnp.concatenate([jnp.concatenate(row, axis=1) for row in swapped], axis=0)
    m2 = dot(up2_ref[...], s2, precision=HIGHEST)
    v = own_block(dot(up1_ref[...], m2, precision=HIGHEST))
    parts = []
    for a in range(4):
        s = v[:, a * 256 : a * 256 + 128] + v[:, a * 256 + 128 : a * 256 + 256]
        s = s + pltpu.roll(s, 64, 1)
        parts.append(jnp.concatenate([s, s], axis=1))
    m1 = jnp.concatenate(parts, axis=0)
    l1 = dot(root_ref[...], m1, precision=HIGHEST)
    l1 = jnp.concatenate([l1[a * 16 : (a + 1) * 16] for a in range(4)], axis=1)
    stack = [l1]
    for shift in range(1, 4):
        stack.append(
            jnp.concatenate(
                [pltpu.roll(m2[:, a * 256 : (a + 1) * 256], 256 - 64 * shift, 1) for a in range(4)], axis=1
            )
        )
    l2 = own_block(dot(mid_ref[...], jnp.concatenate(stack, axis=0), precision=HIGHEST))
    l3 = dot(low_ref[:, :128], s2, precision=HIGHEST) + dot(low_ref[:, 128:144], l2, precision=HIGHEST)
    swapped = block_swap([[l3[q * 8 : (q + 1) * 8, g * 128 : (g + 1) * 128] for g in range(8)] for q in range(16)])
    l3 = jnp.concatenate([jnp.concatenate(row, axis=1) for row in swapped], axis=0)
    l3_high = l3.astype(BF16)
    l3_low = (l3 - l3_high.astype(F32)).astype(BF16)

    n = ROWS
    col = leaf_ref[...]
    row = row_of(col)
    same = jnp.where((col == row) & (iota((n, n), 1) < iota((n, n), 0)), 1.0, 0.0).astype(BF16)
    rank = dot(same, jnp.ones((n, 128), BF16))[:, 0:1].astype(jnp.int32)
    slot = col * 8 + rank
    lane = iota((n, 1024), 1)
    near_lo = dot(jnp.where(lane == slot, 1.0, 0.0).astype(BF16), ret_ref[:, :512])
    near_hi = dot(jnp.where(lane == slot + 4, 1.0, 0.0).astype(BF16), ret_ref[:, :512])
    mine = jnp.where(iota((n, 128), 1) == col, 1.0, 0.0).astype(BF16)
    local = dot(mine, l3_high) + dot(mine, l3_low)
    feat = feat_ref[...].astype(F32)
    near = jnp.concatenate([near_lo, near_hi], axis=1)
    out_ref[...] = (feat + near + feat * local).astype(BF16)


def finish(ret, features, leaf_device, mats):
    return pl.pallas_call(
        finish_kernel,
        out_shape=jax.ShapeDtypeStruct((ROWS, WIDTH), BF16),
        scratch_shapes=[pltpu.VMEM((1024, 128), F32)],
        name="finish",
    )(ret, features, leaf_device, *mats)


def blocks(mats, scale, flip):
    m0, m1, m2, m3 = [(m.T if flip else m) * jnp.asarray(scale, m.dtype) for m in mats]
    w1a = jnp.pad(m1, ((0, 64), (0, 64)))
    w1b = jnp.pad(m1, ((64, 0), (64, 0)))
    w2 = jnp.pad(m2, ((0, 128), (0, 128))) + jnp.pad(m2, ((128, 0), (128, 0)))
    w3 = jnp.pad(m3, ((0, 64), (0, 64))) + jnp.pad(m3, ((64, 0), (64, 0)))
    return m0, w1a, w1b, w2, w3


def tree_mats(lift_leaf, lift_branch, couple_root, couple_branch, couple_leaf):
    up2 = lift_leaf.transpose(1, 2, 0).reshape(16, 128)
    up1 = lift_branch.reshape(64, 16)
    keep4 = (1.0 - jnp.eye(4, dtype=F32))[:, :, None, None]
    keep8 = (1.0 - jnp.eye(8, dtype=F32))[:, :, None, None]
    root = (couple_root * keep4).transpose(0, 2, 1, 3).reshape(64, 64)
    mid = [lift_branch.transpose(0, 2, 1).reshape(64, 16)]
    for shift in range(1, 4):
        mid.append(jnp.stack([couple_branch[b, (b + shift) % 4] for b in range(4)]).reshape(64, 16))
    mid = jnp.concatenate(mid, axis=1)
    low = (couple_leaf * keep8).transpose(2, 0, 3, 1).reshape(128, 128)
    lift = lift_leaf.transpose(2, 0, 1).reshape(128, 16)
    return up2, up1, root, mid, jnp.concatenate([low, lift], axis=1)


def degree_table():
    table = np.zeros((640, 128), np.float32)
    for group, pair in enumerate(PATTERN):
        for half, degree in enumerate(pair):
            table[group * 128 + half * 64 : group * 128 + (half + 1) * 64, degree::4] = 1.0
    return jnp.asarray(table, BF16)


def swap(x):
    return lax.all_to_all(x, AXES, split_axis=0, concat_axis=0, tiled=True)


def shards(
    features,
    cotangent,
    leaf_device,
    neighbours,
    radial,
    first_zero,
    first_one,
    first_two,
    first_three,
    second_zero,
    second_one,
    second_two,
    second_three,
    lift_leaf,
    lift_branch,
    couple_root,
    couple_branch,
    couple_leaf,
):
    send = pack(leaf_device, features, cotangent)
    got = swap(send.reshape(128, 8, WIDTH))
    nbr = jnp.pad(neighbours.T, ((0, 0), (0, 112)))
    rad = jnp.pad(radial.T, ((0, 0), (0, 64)))
    firsts = (first_zero, first_one, first_two, first_three)
    seconds = (second_zero, second_one, second_two, second_three)
    gu, back, fc, perm, m = leaf_a(
        got.reshape(64, 2, 8, WIDTH),
        nbr,
        rad,
        blocks(firsts, 0.5, False),
        blocks(seconds, 1.0, False),
        blocks(seconds, 1.0, True),
    )
    ret = swap(back.reshape(128, 8, 640))
    grads = leaf_b(gu, fc, perm, m, blocks(firsts, 0.5, True), degree_table())
    mats = tree_mats(lift_leaf, lift_branch, couple_root, couple_branch, couple_leaf)
    updated = finish(ret.reshape(1024, 640), features, leaf_device, mats)
    return updated, grads


def solution(mesh):
    spread = P(AXES, None)
    across = P(None, AXES)
    return jax.shard_map(
        shards,
        mesh=mesh,
        in_specs=(spread, spread, spread, across, across) + (P(),) * 13,
        out_specs=(spread, across),
        check_vma=False,
    )
```

time: 881 us -> 129 us (0.15); the launches traced: 868 us -> 128 us
  matrix products: 383 us -> 0 us
  local copies, waits for them, and re-layouts: 219 us -> 11.3 us
  other arithmetic: 164 us -> 3.25 us
  Pallas kernels: 0 us -> 77.6 us
  blocking collectives: 37.6 us -> 0 us
  starting transfers between devices: 39.9 us -> 17.7 us
    dot_general x382 -> x0, matrix products: 383 us -> none  [the longest x224 135 us: mixing(): result = jnp.dot(piece, weight, preferred_element_type=jnp.float32)]
    gather x33 -> x0, local copies, waits for them, and re-layouts: 103 us -> none  [the longest x16 55.9 us: step(): index = order[choose % filled]]
    pallas_call x0 -> x4, Pallas kernels: none -> 77.6 us  [the longest x1 37.6 us: leaf_a(): pl.pallas_call(leaf_a_kernel, grid=(NBR,), in_specs=[full(x) for x in arg...]
    concatenate x16 -> x0, local copies, waits for them, and re-layouts: 64.9 us -> none  [mixing(): return jnp.concatenate(outs, axis=1)]
    add x16 -> x6, other arithmetic: 63.5 us -> 1.6 us  [the longest x3 0.86 us: blocks(): w3 = jnp.pad(m3, ((0, 64), (0, 64))) + jnp.pad(m3, ((64, 0), (64, 0)))]
    all_to_all x6 -> x0, other arithmetic: 44.8 us -> none  [the longest x2 16.7 us: shards(): lax.all_to_all(send_grad.reshape(flat_shape), ('gx', 'gy', 'gz'), split_a...]
    all_gather x3 -> x0, blocking collectives: 37.6 us -> none  [the longest x1 12.8 us: shards(): sib_root = lax.all_gather(topmost[None], 'gx', axis=0, tiled=True)]
    convert_element_type x19 -> x0, other arithmetic: 32.4 us -> none  [the longest x16 30.4 us: step(): grad_u = (sig * (1.0 + upper * (1.0 - sig)) * trans).astype(jnp.bfloat16)]
  transfers between devices with their start and end apart: 4 -> 2, of which waited for: 2 -> 1; matrix products, arithmetic and copies ran while one was open for 6% -> 10% of each run, Pallas kernels for 0% -> 23%
where the time goes in v1:
time: 129 us; the launch traced here: 128 us
  Pallas kernels  77.6 us (60%)
  starting transfers between devices  17.7 us (14%)
  waiting for transfers between devices  17.3 us (13%)
  local copies, waits for them, and re-layouts  11.3 us (9%)
  other arithmetic  3.25 us (3%)
    pallas_call x1, Pallas kernels, leaf_a(): pl.pallas_call(leaf_a_kernel, grid=(NBR,), in_specs=[full(x) for x in arg...  37.6 us
    pallas_call x1, Pallas kernels, leaf_b(): pl.pallas_call(leaf_b_kernel, grid=(NBR,), in_specs=[pl.BlockSpec((1, POO...  29.9 us
    all_to_all x2, starting transfers between devices, swap(): return lax.all_to_all(x, AXES, split_axis=0, concat_axis=0, tiled=True)  17.7 us
    all_to_all x2, waiting for transfers between devices, swap(): return lax.all_to_all(x, AXES, split_axis=0, concat_axis=0, tiled=True)  17.3 us
    pallas_call x1, Pallas kernels, finish(): pl.pallas_call(finish_kernel, out_shape=jax.ShapeDtypeStruct((ROWS, WIDTH...  5.74 us
    pallas_call x1, Pallas kernels, pack(): pl.pallas_call(pack_kernel, out_shape=jax.ShapeDtypeStruct((128 * 8, WIDT...  4.29 us
    unnamed x50, local copies, waits for them, and re-layouts  3.37 us
  transfers between devices with their start and end apart: 2, of which 1 were waited for; matrix products, arithmetic and copies ran while one was open for 10% of the time, Pallas kernels for 23%

profile of v1, /device:TPU:0, one launch (start us, length us, event | category | flops | bytes accessed | tf_op | source)
XLA Modules:
  0.0 128.2 jit_solution(10941793024699978816)
XLA Ops:
  0.6 1.5 %copy.43.leaf_ref = s32[256,1]{1,0:T(8,128)} copy(s32[256,1]{0,1:T(1,128)} %param.21) | data formatting | bytes 2048 | tf_op args[2]
  2.1 4.3 %pack.1 = bf16[1024,1024]{1,0:T(8,128)(2,1)} custom-call(s32[256,1]{1,0:T(8,128)} %copy.43.leaf_ref, bf16[256,1024]{1,0:T(8,128)(2,1)} %feat_ref.3, bf16[256,1024]{1,0:T(8,128)(2,1)} %grad_ref.1), custom_call_target="tpu_custom_call" | custom-call | tf_op jit(solution)/shard_map/pack/pallas_call | solution.py:57
  6.4 11.7 %all-to-all-start = ((bf16[128,8,1024]{2,1,0:T(8,128)(2,1)}), bf16[128,8,1024]{2,1,0:T(8,128)(2,1)}, u32[]{:S(2)}, u32[]{:S(2)}) async-start(bf16[128,8,1024]{2,1,0:T(8,128)(2,1)} %bitcast.58), calls=%async_computation | async-start | bytes 4194304 | tf_op jit(solution)/shard_map/all_to_all | solution.py:365
  18.1 0.0 copy-start.9
  18.1 0.0 copy-start.18
  18.2 0.0 copy-start.8
  18.2 0.0 copy-start.12
  18.2 0.1 copy.47
  18.4 0.1 copy.66
  18.5 0.1 copy.51
  18.6 0.1 copy.46
  18.7 0.8 copy.54.f0
  19.5 0.1 copy.48
  19.6 0.8 copy.57.f2
  20.4 0.1 copy.52
  20.5 0.1 copy.49
  20.6 0.1 pad_add_fusion.7
  20.7 0.7 copy.58.f3
  21.4 0.1 copy.53
  21.5 0.1 copy.44
  21.7 0.1 copy.45
  21.8 0.0 copy-start.6
  21.8 0.8 copy.50
  22.6 0.1 copy.61
  22.7 0.1 multiply_bitcast_fusion
  22.8 0.4 copy.62
  23.2 0.5 reshape.72
  23.7 0.1 copy.63
  23.8 0.1 multiply_bitcast_fusion.1
  23.9 0.1 copy.60
  24.0 0.7 reshape.67.root_ref
  24.7 0.1 copy.59
  24.8 0.7 copy.65.up2_ref
  25.5 0.7 pad.86.nbr_ref
  26.2 0.7 pad.87.rad_ref
  26.9 0.1 pad_add_fusion.4.t3
  27.0 0.7 pad_add_fusion.5
  27.8 0.7 pad_maximum_fusion.low_ref
  28.4 0.7 pad_add_fusion.1
  29.1 0.9 fusion.6
  30.0 0.8 fusion.4
  30.8 17.3 %all-to-all-done = bf16[128,8,1024]{2,1,0:T(8,128)(2,1)} async-done(((bf16[128,8,1024]{2,1,0:T(8,128)(2,1)}), bf16[128,8,1024]{2,1,0:T(8,128)(2,1)}, u32[]{:S(2)}, u32[]{:S(2)}) %all-to-all-start) | async-done | bytes 2097184 | tf_op jit(solution)/shard_map/all_to_all | solution.py:365
  48.1 37.6 %leaf_a.1 = (bf16[16,512,1024]{2,1,0:T(8,128)(2,1)}, bf16[64,2,8,640]{3,2,1,0:T(8,128)(2,1)}, bf16[512,1024]{1,0:T(8,128)(2,1)}, f32[512,512]{1,0:T(8,128)}, f32[512,128]{1,0:T(8,128)}) custom-call(bf16[64,2,8,1024]{3,2,1,0:T(8,128)(2,1)} %bitcast.1.got_ref, s32[512,128]{1,0:T(8,128)} %pad.86.nbr_ref, f32[512,128]{1,0:T(8,128)} %pad.87.rad_ref, ...), custom_call_target="tpu_custom_call" | custom-call | flops 12884901888 | bytes 25165824 | tf_op jit(solution)/shard_map/leaf_a/pallas_call | solution.py:190
  85.7 0.0 copy-start
  85.7 6.0 %all-to-all-start.1 = ((bf16[128,8,640]{2,1,0:T(8,128)(2,1)}), bf16[128,8,640]{2,1,0:T(8,128)(2,1)}, u32[]{:S(2)}, u32[]{:S(2)}) async-start(bf16[128,8,640]{2,1,0:T(8,128)(2,1)} %bitcast.59), calls=%async_computation.1 | async-start | bytes 2621440 | tf_op jit(solution)/shard_map/all_to_all | solution.py:365
  91.8 0.7 pad_maximum_fusion.4.mid_ref
  92.5 29.9 %leaf_b.1 = f32[64,512]{1,0:T(8,128)} custom-call(bf16[16,512,1024]{2,1,0:T(8,128)(2,1)} %get-tuple-element.8.gu_ref, bf16[512,1024]{1,0:T(8,128)(2,1)S(1)} %copy-done.1, f32[512,512]{1,0:T(8,128)S(1)} %copy-done.2, f32[512,128]{1,0:T(8,128)S(1)} %copy-done.3, bf16[256,256]{1,0:T(8,128)(2,1)S(1)} %get-tuple-element.12.t0, ...), custom_call_target="tpu_custom_call" | custom-call | flops 12884901888 | bytes 25165824 | tf_op jit(solution)/shard_map/leaf_b/pallas_call | solution.py:246
  122.4 5.7 %finish.1 = bf16[256,1024]{1,0:T(8,128)(2,1)} custom-call(bf16[1024,640]{1,0:T(8,128)(2,1)} %bitcast.9.ret_ref, bf16[256,1024]{1,0:T(8,128)(2,1)} %feat_ref.3, s32[256,1]{1,0:T(8,128)} %copy.43.leaf_ref, f32[16,128]{1,0:T(8,128)} %copy.65.up2_ref, f32[64,16]{1,0:T(8,128)} %bitcast.67, f32[64,64]{1,0:T(8,128)} %reshape.67.root_ref, ...), custom_call_target="tpu_custom_call" | custom-call | tf_op jit(solution)/shard_map/finish/pallas_call | solution.py:324
  (44 shorter events, 0.2 us)
Async XLA Ops:
  6.4 11.7 %copy-start.13 = (bf16[192,192]{1,0:T(8,128)(2,1)S(1)}, bf16[192,192]{1,0:T(8,128)(2,1)}, u32[]{:S(2)}) copy-start(bf16[192,192]{1,0:T(8,128)(2,1)} %param.25) | copy-start | bytes 221188
  6.4 12.1 %copy-start.5 = (bf16[192,192]{1,0:T(8,128)(2,1)S(1)}, bf16[192,192]{1,0:T(8,128)(2,1)}, u32[]{:S(2)}) copy-start(bf16[192,192]{1,0:T(8,128)(2,1)} %param.29) | copy-start | bytes 221188
  6.4 12.2 %copy-start.10 = (bf16[256,256]{1,0:T(8,128)(2,1)S(1)}, bf16[256,256]{1,0:T(8,128)(2,1)}, u32[]{:S(2)}) copy-start(bf16[256,256]{1,0:T(8,128)(2,1)} %param.24) | copy-start | bytes 393220
  6.4 13.1 %copy-start.17 = (bf16[128,128]{1,0:T(8,128)(2,1)S(1)}, bf16[128,128]{1,0:T(8,128)(2,1)}, u32[]{:S(2)}) copy-start(bf16[128,128]{1,0:T(8,128)(2,1)} %param.26) | copy-start | bytes 98308
  6.4 41.6 %all-to-all-start = ((bf16[128,8,1024]{2,1,0:T(8,128)(2,1)}), bf16[128,8,1024]{2,1,0:T(8,128)(2,1)}, u32[]{:S(2)}, u32[]{:S(2)}) async-start(bf16[128,8,1024]{2,1,0:T(8,128)(2,1)} %bitcast.58), calls=%async_computation | async-start | bytes 4194304 | tf_op jit(solution)/shard_map/all_to_all | solution.py:365
  18.1 2.3 %copy-start.9 = (bf16[128,128]{1,0:T(8,128)(2,1)S(1)}, bf16[128,128]{1,0:T(8,128)(2,1)}, u32[]{:S(2)}) copy-start(bf16[128,128]{1,0:T(8,128)(2,1)} %param.30) | copy-start | bytes 98308
  18.1 2.4 %copy-start.18 = (bf16[64,64]{1,0:T(8,128)(2,1)S(1)}, bf16[64,64]{1,0:T(8,128)(2,1)}, u32[]{:S(2)}) copy-start(bf16[64,64]{1,0:T(8,128)(2,1)} %param.27) | copy-start | bytes 24580
  18.2 3.3 %copy-start.15 = (bf16[64,64]{1,0:T(8,128)(2,1)S(1)}, bf16[64,64]{1,0:T(8,128)(2,1)}, u32[]{:S(2)}) copy-start(bf16[64,64]{1,0:T(8,128)(2,1)} %param.31) | copy-start | bytes 24580
  18.2 3.4 %copy-start.16 = (s32[16,512]{1,0:T(8,128)S(1)}, s32[16,512]{1,0:T(8,128)}, u32[]{:S(2)}) copy-start(s32[16,512]{1,0:T(8,128)} %param.22) | copy-start | bytes 98308
  18.2 3.5 %copy-start.8 = (f32[64,512]{1,0:T(8,128)S(1)}, f32[64,512]{1,0:T(8,128)}, u32[]{:S(2)}) copy-start(f32[64,512]{1,0:T(8,128)} %param.23) | copy-start | bytes 393220
  18.2 3.6 %copy-start.12 = (bf16[256,256]{1,0:T(8,128)(2,1)S(1)}, bf16[256,256]{1,0:T(8,128)(2,1)}, u32[]{:S(2)}) copy-start(bf16[256,256]{1,0:T(8,128)(2,1)} %s0.1) | copy-start | bytes 393220
  18.2 4.4 %copy-start.7 = (f32[4,16,16]{2,1,0:T(8,128)S(1)}, f32[4,16,16]{2,1,0:T(8,128)}, u32[]{:S(2)}) copy-start(f32[4,16,16]{2,1,0:T(8,128)} %param.33) | copy-start | bytes 12292
  18.2 4.5 %copy-start.4 = (f32[8,8,16,16]{3,2,1,0:T(8,128)S(1)}, f32[8,8,16,16]{3,2,1,0:T(8,128)}, u32[]{:S(2)}) copy-start(f32[8,8,16,16]{3,2,1,0:T(8,128)} %param.36) | copy-start | bytes 196612
  21.8 1.9 %copy-start.6 = (f32[8,16,16]{2,1,0:T(8,128)S(1)}, f32[8,16,16]{2,1,0:T(8,128)}, u32[]{:S(2)}) copy-start(f32[8,16,16]{2,1,0:T(8,128)} %param.32) | copy-start | bytes 24580
  21.8 2.0 %copy-start.11 = (f32[4,4,16,16]{3,2,1,0:T(8,128)S(1)}, f32[4,4,16,16]{3,2,1,0:T(8,128)}, u32[]{:S(2)}) copy-start(f32[4,4,16,16]{3,2,1,0:T(8,128)} %param.34) | copy-start | bytes 49156
  22.8 4.2 %copy-start.14 = (f32[4,4,16,16]{3,2,1,0:T(8,128)S(1)}, f32[4,4,16,16]{3,2,1,0:T(8,128)}, u32[]{:S(2)}) copy-start(f32[4,4,16,16]{3,2,1,0:T(8,128)} %param.35) | copy-start | bytes 49156
  85.7 6.8 %copy-start = (bf16[640,128]{1,0:T(8,128)(2,1)S(1)}, bf16[640,128]{1,0:T(8,128)(2,1)}, u32[]{:S(2)}) copy-start(bf16[640,128]{1,0:T(8,128)(2,1)} %constant.16.clone.table_ref) | copy-start | bytes 491524
  85.7 6.8 %copy-start.1 = (bf16[512,1024]{1,0:T(8,128)(2,1)S(1)}, bf16[512,1024]{1,0:T(8,128)(2,1)}, u32[]{:S(2)}) copy-start(bf16[512,1024]{1,0:T(8,128)(2,1)} %get-tuple-element.9.fc_ref) | copy-start | bytes 3145732
  85.7 6.8 %copy-start.2 = (f32[512,512]{1,0:T(8,128)S(1)}, f32[512,512]{1,0:T(8,128)}, u32[]{:S(2)}) copy-start(f32[512,512]{1,0:T(8,128)} %get-tuple-element.10.perm_ref) | copy-start | bytes 3145732
  85.7 6.8 %copy-start.3 = (f32[512,128]{1,0:T(8,128)S(1)}, f32[512,128]{1,0:T(8,128)}, u32[]{:S(2)}) copy-start(f32[512,128]{1,0:T(8,128)} %get-tuple-element.11.m_ref) | copy-start | bytes 786436
  85.7 36.7 %all-to-all-start.1 = ((bf16[128,8,640]{2,1,0:T(8,128)(2,1)}), bf16[128,8,640]{2,1,0:T(8,128)(2,1)}, u32[]{:S(2)}, u32[]{:S(2)}) async-start(bf16[128,8,640]{2,1,0:T(8,128)(2,1)} %bitcast.59), calls=%async_computation.1 | async-start | bytes 2621440 | tf_op jit(solution)/shard_map/all_to_all | solution.py:365

commit v2 on v1

v2 whole, which is shorter than its diff:
```python
import math

import jax
import jax.numpy as jnp
import numpy as np
from jax import lax
from jax.experimental import pallas as pl
from jax.experimental.pallas import tpu as pltpu
from jax.sharding import PartitionSpec as P

BF16 = jnp.bfloat16
F32 = jnp.float32
AXES = ("gx", "gy", "gz")
EMPTY = 1024.0
ROWS = 256
POOL = 512
WIDTH = 1024
NBR = 16
TILE = 256


def dot(a, b, **kw):
    return jnp.dot(a, b, preferred_element_type=F32, **kw)


def iota(shape, axis):
    return lax.broadcasted_iota(jnp.int32, shape, axis)


def col_of(row):
    n = row.shape[1]
    diag = jnp.where(iota((n, n), 0) == iota((n, n), 1), row.astype(F32), 0.0).astype(BF16)
    return dot(diag, jnp.ones((n, 128), BF16)).astype(jnp.int32)


def split(x):
    high = x.astype(BF16)
    return high, (x - high.astype(F32)).astype(BF16)


def pack_kernel(leaf_ref, feat_ref, grad_ref, send_ref):
    row = leaf_ref[...]
    col = col_of(row)[:, 0:1]
    n = ROWS
    same = (col == row) & (iota((n, n), 0) < iota((n, n), 1))
    rank = jnp.sum(jnp.where(same, 1.0, 0.0), axis=0, keepdims=True).astype(jnp.int32)
    slot = row * 8 + rank
    ones = jnp.ones((n, 128), BF16)
    for part in range(4):
        index = iota((n, n), 0) + part * n
        pick_f = jnp.where(index == slot, 1.0, 0.0).astype(BF16)
        pick_g = jnp.where(index == slot + 4, 1.0, 0.0).astype(BF16)
        there = dot(pick_f, ones)
        gone = (there < 0.5) & ((iota((n, 128), 0) & 7) < 4)
        out = dot(pick_f, feat_ref[...]) + dot(pick_g, grad_ref[...])
        send_ref[part * n : (part + 1) * n, 128:] = out[:, 128:].astype(BF16)
        send_ref[part * n : (part + 1) * n, :128] = jnp.where(gone, EMPTY, out[:, :128]).astype(BF16)


def pack(leaf_row, features, cotangent):
    return pl.pallas_call(
        pack_kernel,
        out_shape=jax.ShapeDtypeStruct((128 * 8, WIDTH), BF16),
        name="pack",
    )(leaf_row, features, cotangent)


def mix(x, w0, w1a, w1b, w2, w3):
    a = dot(x[:, 0:256], w0)
    b = dot(x[:, 256:512], w1a)
    c = dot(x[:, 384:640], w1b)
    d = dot(x[:, 640:896], w2)
    e = dot(x[:, 896:1024], w3)
    return [
        a[:, :128],
        a[:, 128:],
        b[:, :128],
        b[:, 128:] + c[:, :128],
        c[:, 128:],
        d[:, :128],
        d[:, 128:],
        e,
    ]


def gather(index, own_ref, table_ref, out_ref, first, last, tiled):
    for i in range(first, last):
        start = pl.multiple_of(index[i >> 7, i & 127], 8)
        row = own_ref[i * 8 : (i + 1) * 8, :] + table_ref[pl.ds(start, 8), :]
        if tiled:
            out_ref[i >> 3, pl.ds(i & 7, 8, stride=8), :] = row
        else:
            out_ref[i * 8 : (i + 1) * 8, :] = row


def fetch(index_ref, k, index_smem, sem):
    return pltpu.make_async_copy(index_ref.at[jnp.minimum(k, NBR - 1)], index_smem, sem)


def scales(rad_ref, rows, k):
    size = rows.size
    shifted = pltpu.roll(rad_ref[rows, :], (128 - 4 * k) % 128, 1)
    r0, r1, r2, r3 = [jnp.broadcast_to(shifted[:, j : j + 1], (size, 128)) for j in range(4)]
    low = iota((size, 128), 1) < 64
    p01 = jnp.where(low, r0, r1)
    p23 = jnp.where(low, r2, r3)
    p12 = jnp.where(low, r1, r2)
    p31 = jnp.where(low, r3, r1)
    return [p01, p23, p12, p31, p23, p23, p23, r3]


def mix_blocks(piece, w0, w1a, w1b, w2, w3, use):
    out = dot(jnp.concatenate([piece(0), piece(1)], axis=1), w0[...])
    use(0, out[:, :128])
    use(1, out[:, 128:])
    middle = piece(3)
    a = dot(jnp.concatenate([piece(2), middle], axis=1), w1a[...])
    b = dot(jnp.concatenate([middle, piece(4)], axis=1), w1b[...])
    use(2, a[:, :128])
    use(3, a[:, 128:] + b[:, :128])
    use(4, b[:, 128:])
    out = dot(jnp.concatenate([piece(5), piece(6)], axis=1), w2[...])
    use(5, out[:, :128])
    use(6, out[:, 128:])
    use(7, dot(piece(7), w3[...]))


def leaf_a_kernel(
    got_ref,
    nbr_ref,
    rad_ref,
    f0, f1a, f1b, f2, f3,
    s0, s1a, s1b, s2, s3,
    u_ref,
    back_ref,
    own_ref,
    table_ref,
    index_ref,
    occ_ref,
    acc_ref,
    tile_ref,
    buf0_ref,
    buf1_ref,
    rank_ref,
    rank_smem,
    first_smem,
    odd_smem,
    even_smem,
    sem0,
    sem1,
    sem2,
    sem3,
):
    step = pl.program_id(0)

    @pl.when(step == 0)
    def _():
        first = jnp.where(iota((8, 128), 1) == 0, 1.0, 0.0).astype(BF16)
        got0 = got_ref[:, :, :, 0:128].reshape(1024, 128)
        lead = lax.dot_general(first, got0, (((1,), (1,)), ((), ())), preferred_element_type=F32)
        lane = iota((8, 1024), 1)
        occ = jnp.where((lead < 0.5 * EMPTY) & ((lane & 7) < 4), 1.0, 0.0)
        occ8 = jnp.concatenate([occ[0:1, r * 128 : (r + 1) * 128] for r in range(8)], axis=0)
        occ_ref[...] = occ8
        occ8_low = occ8.astype(BF16)
        before = jnp.where(iota((128, 128), 0) < iota((128, 128), 1), 1.0, 0.0).astype(BF16)
        sums = dot(occ8_low, jnp.ones((128, 128), BF16))
        above = jnp.where(iota((8, 8), 1) < iota((8, 8), 0), 1.0, 0.0).astype(BF16)
        rank = dot(occ8_low, before) + dot(above, sums.astype(BF16))
        filled = jnp.sum(sums, axis=0, keepdims=True)
        rank_ref[...] = 8 * jnp.where(occ8 > 0.5, rank, float(POOL)).astype(jnp.int32)
        to_smem = pltpu.make_async_copy(rank_ref, rank_smem, sem0)
        to_smem.start()
        choice = nbr_ref[...].astype(F32)
        filled = jnp.concatenate([filled] * 4, axis=1)
        left = choice - jnp.floor(choice / filled) * filled
        left = jnp.where(left < 0.0, left + filled, left)
        left = 8 * jnp.where(left >= filled, left - filled, left).astype(jnp.int32)
        for r in range(4):
            index_ref[:, r, :] = left[:, r * 128 : (r + 1) * 128]
        fetch(index_ref, 0, first_smem, sem1).start()
        fetch(index_ref, 1, odd_smem, sem2).start()
        fetch(index_ref, 2, even_smem, sem3).start()
        sums = dot(occ.astype(BF16), got_ref[...].reshape(1024, WIDTH))
        tile_ref[...] = sums * (1.0 / math.sqrt(ROWS))
        for pair in range(64):
            for half in range(2):
                block = got_ref[pair, half].astype(F32)
                at = (pair * 2 + half) * 4
                for g in range(8):
                    own_ref[pl.ds(at * 8 + g, 4, stride=8), :] = block[0:4, g * 128 : (g + 1) * 128]
        acc_ref[...] = jnp.zeros_like(acc_ref)
        to_smem.wait()
        for i in range(POOL):
            s = (i >> 2) * 8 + (i & 3)
            to = pl.multiple_of(rank_smem[s >> 7, s & 127], 8)
            table_ref[pl.ds(to, 8), :] = own_ref[i * 8 : (i + 1) * 8, :]
        fetch(index_ref, 0, first_smem, sem1).wait()
        gather(first_smem, own_ref, table_ref, buf0_ref, 0, POOL, False)

    turns = ((buf0_ref, buf1_ref, odd_smem, sem2), (buf1_ref, buf0_ref, even_smem, sem3))
    for half, (buf, other, index_smem, sem) in enumerate(turns):
        k = step * 2 + half
        fetch(index_ref, k + 1, index_smem, sem).wait()
        for part in range(POOL // TILE):
            rows = pl.ds(part * TILE, TILE)
            gather(index_smem, own_ref, table_ref, other, part * TILE, (part + 1) * TILE, False)
            pats = scales(rad_ref, rows, k)

            def piece(g):
                y = buf[pl.ds(part * TILE * 8 + g, TILE, stride=8), :]
                return (y * pats[g]).astype(BF16)

            def use(g, w):
                cols = slice(g * 128, (g + 1) * 128)
                acc_ref[rows, cols] += w + w * jnp.tanh(w)
                u_ref[half, rows, cols] = w

            mix_blocks(piece, f0, f1a, f1b, f2, f3, use)

        @pl.when(step < NBR // 2 - 1)
        def _():
            fetch(index_ref, k + 3, index_smem, sem).start()

    @pl.when(step == NBR // 2 - 1)
    def _():
        total = acc_ref[...]
        high, low = split(total)
        wts = (s0[...], s1a[...], s1b[...], s2[...], s3[...])
        near = [0.25 * (a + b) for a, b in zip(mix(high, *wts), mix(low, *wts))]
        half = iota((64, 8, 512), 1) < 4
        lo = jnp.concatenate(near[:4], axis=1)
        hi = jnp.concatenate(near[4:], axis=1)
        lo_r = pltpu.roll(lo.reshape(64, 8, 512), 4, 1)
        hi_r = pltpu.roll(hi.reshape(64, 8, 512), 4, 1)
        lo = lo.reshape(64, 8, 512)
        hi = hi.reshape(64, 8, 512)
        back_ref[:, 0, :, :512] = jnp.where(half, lo, hi_r).astype(BF16)
        back_ref[:, 1, :, :512] = jnp.where(half, lo_r, hi).astype(BF16)
        tile = tile_ref[...]
        body = jnp.concatenate([tile[0:1, r * 128 : (r + 1) * 128] for r in range(8)], axis=0)
        body = jnp.broadcast_to(body[None, None], (64, 2, 8, 128)).astype(BF16)
        back_ref[:, :, :, 512:] = body


def full(x):
    return pl.BlockSpec(x.shape, lambda k, n=len(x.shape): (0,) * n)


def leaf_a(got, nbr, rad, firsts, seconds):
    args = (got, nbr, rad, *firsts, *seconds)
    out_shape = [
        jax.ShapeDtypeStruct((NBR, POOL, WIDTH), F32),
        jax.ShapeDtypeStruct((64, 2, 8, 640), BF16),
        jax.ShapeDtypeStruct((POOL * 8, 128), F32),
        jax.ShapeDtypeStruct((POOL * 8 + 8, 128), F32),
        jax.ShapeDtypeStruct((NBR, 4, 128), jnp.int32),
        jax.ShapeDtypeStruct((8, 128), F32),
    ]
    return pl.pallas_call(
        leaf_a_kernel,
        grid=(NBR // 2,),
        in_specs=[full(x) for x in args],
        out_specs=[pl.BlockSpec((2, POOL, WIDTH), lambda k: (k, 0, 0))] + [full(x) for x in out_shape[1:]],
        out_shape=out_shape,
        scratch_shapes=[
            pltpu.VMEM((POOL, WIDTH), F32),
            pltpu.VMEM((8, WIDTH), F32),
            pltpu.VMEM((POOL * 8, 128), F32),
            pltpu.VMEM((POOL * 8, 128), F32),
            pltpu.VMEM((8, 128), jnp.int32),
            pltpu.SMEM((8, 128), jnp.int32),
            pltpu.SMEM((4, 128), jnp.int32),
            pltpu.SMEM((4, 128), jnp.int32),
            pltpu.SMEM((4, 128), jnp.int32),
            pltpu.SemaphoreType.DMA,
            pltpu.SemaphoreType.DMA,
            pltpu.SemaphoreType.DMA,
            pltpu.SemaphoreType.DMA,
        ],
        compiler_params=pltpu.CompilerParams(vmem_limit_bytes=56 << 20),
        cost_estimate=pl.CostEstimate(flops=6 << 30, bytes_accessed=24 << 20, transcendentals=8 << 20),
        name="leaf_a",
    )(*args)


def leaf_b_kernel(
    index_ref, u_ref, got_ref, own_ref, table_ref, occ_ref,
    t0, t1a, t1b, t2, t3,
    s0, s1a, s1b, s2, s3,
    sum_ref, out_ref, acc_ref, half_t_ref, buf0_ref, buf1_ref,
    first_smem, odd_smem, even_smem, sem1, sem2, sem3,
):
    step = pl.program_id(0)

    @pl.when(step == 0)
    def _():
        fetch(index_ref, 0, first_smem, sem1).start()
        fetch(index_ref, 1, odd_smem, sem2).start()
        fetch(index_ref, 2, even_smem, sem3).start()
        acc_ref[...] = jnp.zeros_like(acc_ref)
        top = iota((8, WIDTH), 0) < 4
        for part in range(POOL // TILE):
            grad = []
            for pair in range(part * TILE // 8, (part + 1) * TILE // 8):
                a = pltpu.roll(got_ref[pair, 0].astype(F32), 4, 0)
                grad.append(jnp.where(top, a, got_ref[pair, 1].astype(F32)))
            grad = jnp.concatenate(grad, axis=0).astype(BF16)
            rows = slice(part * TILE, (part + 1) * TILE)

            def use(g, value):
                half_t_ref[rows, g * 128 : (g + 1) * 128] = 0.5 * value

            mix_blocks(lambda g: grad[:, g * 128 : (g + 1) * 128], s0, s1a, s1b, s2, s3, use)
        fetch(index_ref, 0, first_smem, sem1).wait()
        gather(first_smem, own_ref, table_ref, buf0_ref, 0, POOL, True)

    turns = ((buf0_ref, buf1_ref, odd_smem, sem2), (buf1_ref, buf0_ref, even_smem, sem3))
    for half, (buf, other, index_smem, sem) in enumerate(turns):
        k = step * 2 + half
        fetch(index_ref, k + 1, index_smem, sem).wait()
        for part in range(POOL // TILE):
            rows = pl.ds(part * TILE, TILE)
            gather(index_smem, own_ref, table_ref, other, part * TILE, (part + 1) * TILE, True)
            prods = {}

            def piece(g):
                cols = slice(g * 128, (g + 1) * 128)
                w = u_ref[half, rows, cols]
                h = jnp.tanh(w)
                up = 1.0 + h
                return ((up + (w * up) * (1.0 - h)) * half_t_ref[rows, cols]).astype(BF16)

            def use(g, s):
                tiles = slice(part * TILE // 8, (part + 1) * TILE // 8)
                prods[g] = s * buf[tiles, g * 8 : (g + 1) * 8, :].reshape(TILE, 128)

            mix_blocks(piece, t0, t1a, t1b, t2, t3, use)
            low = iota((TILE, 128), 1) < 64
            ones = jnp.where(low, prods[2], prods[3])
            ones = ones + pltpu.roll(ones, 64, 1)
            threes = prods[7] + pltpu.roll(prods[7], 64, 1)
            cross = pltpu.roll(jnp.where(low, prods[3], prods[2]), 64, 1)
            x01 = prods[0] + jnp.where(low, 0.0, ones)
            x23 = (prods[1] + prods[4]) + (prods[5] + prods[6]) + cross + jnp.where(low, 0.0, threes)
            sums = dot(jnp.concatenate([x01, x23], axis=1).astype(BF16), sum_ref[...])
            mine = (iota((TILE, 128), 1) >> 2) == k
            acc_ref[rows, :] = jnp.where(mine, sums, acc_ref[rows, :])

        @pl.when(step < NBR // 2 - 1)
        def _():
            fetch(index_ref, k + 3, index_smem, sem).start()

    @pl.when(step == NBR // 2 - 1)
    def _():
        occ = []
        for r in range(8):
            pick = iota((128, 64), 0) == (iota((128, 64), 1) >> 2) * 8 + (iota((128, 64), 1) & 3)
            occ.append(dot(occ_ref[r : r + 1, :].astype(BF16), jnp.where(pick, 1.0, 0.0).astype(BF16)))
        occ = jnp.concatenate(occ, axis=1)
        out_ref[...] = 0.5 * occ * jnp.transpose(acc_ref[...])[0:64, :]


def leaf_b(index, u, got, own, table, occ, trans, seconds_t, sums):
    args = (got, own, table, occ, *trans, *seconds_t, sums)
    return pl.pallas_call(
        leaf_b_kernel,
        grid=(NBR // 2,),
        in_specs=[
            full(index),
            pl.BlockSpec((2, POOL, WIDTH), lambda k: (k, 0, 0)),
        ]
        + [full(x) for x in args],
        out_specs=pl.BlockSpec((64, POOL), lambda k: (0, 0)),
        out_shape=jax.ShapeDtypeStruct((64, POOL), F32),
        scratch_shapes=[
            pltpu.VMEM((POOL, 128), F32),
            pltpu.VMEM((POOL, WIDTH), F32),
            pltpu.VMEM((64, 64, 128), F32),
            pltpu.VMEM((64, 64, 128), F32),
            pltpu.SMEM((4, 128), jnp.int32),
            pltpu.SMEM((4, 128), jnp.int32),
            pltpu.SMEM((4, 128), jnp.int32),
            pltpu.SemaphoreType.DMA,
            pltpu.SemaphoreType.DMA,
            pltpu.SemaphoreType.DMA,
        ],
        compiler_params=pltpu.CompilerParams(vmem_limit_bytes=48 << 20),
        cost_estimate=pl.CostEstimate(flops=6 << 30, bytes_accessed=24 << 20, transcendentals=8 << 20),
        name="leaf_b",
    )(index, u, *args)


def block_swap(tiles):
    low = iota((8, 128), 1) < 64
    out = [[None] * 8 for _ in range(16)]
    for pair in range(8):
        for g in range(8):
            a, b = tiles[2 * pair][g], tiles[2 * pair + 1][g]
            out[2 * g][pair] = jnp.where(low, a, pltpu.roll(b, 64, 1))
            out[2 * g + 1][pair] = jnp.where(low, pltpu.roll(a, 64, 1), b)
    return out


def own_block(x):
    which = (iota((16, 1024), 1) >> 6) & 3
    out = x[0:16]
    for b in range(1, 4):
        out = jnp.where(which == b, x[b * 16 : (b + 1) * 16], out)
    return out


def dot2(a, b):
    high, low = split(a)
    return dot(high, b) + dot(low, b)


def dot3(a, b):
    high, low = split(b)
    return dot2(a, high) + dot(a.astype(BF16), low)


def finish_kernel(ret_ref, feat_ref, leaf_ref, up2_ref, up1_ref, root_ref, mid_ref, low_ref, out_ref, tile_ref):
    tile_ref[...] = ret_ref[:, 512:640].astype(F32)
    tiles = [[tile_ref[pl.ds(ab * 64 + g, 8, stride=8), :] for g in range(8)] for ab in range(16)]
    swapped = block_swap(tiles)
    s2 = jnp.concatenate([jnp.concatenate(row, axis=1) for row in swapped], axis=0)
    s2 = s2.astype(BF16)
    m2 = dot2(up2_ref[...], s2)
    v = own_block(dot3(up1_ref[...], m2))
    parts = []
    for a in range(4):
        s = v[:, a * 256 : a * 256 + 128] + v[:, a * 256 + 128 : a * 256 + 256]
        s = s + pltpu.roll(s, 64, 1)
        parts.append(jnp.concatenate([s, s], axis=1))
    m1 = jnp.concatenate(parts, axis=0)
    l1 = dot3(root_ref[...], m1)
    l1 = jnp.concatenate([l1[a * 16 : (a + 1) * 16] for a in range(4)], axis=1)
    stack = [l1]
    for shift in range(1, 4):
        stack.append(
            jnp.concatenate(
                [pltpu.roll(m2[:, a * 256 : (a + 1) * 256], 256 - 64 * shift, 1) for a in range(4)], axis=1
            )
        )
    l2 = own_block(dot3(mid_ref[...], jnp.concatenate(stack, axis=0)))
    l3 = dot2(low_ref[:, :128], s2) + dot3(low_ref[:, 128:144], l2)
    swapped = block_swap([[l3[q * 8 : (q + 1) * 8, g * 128 : (g + 1) * 128] for g in range(8)] for q in range(16)])
    l3 = jnp.concatenate([jnp.concatenate(row, axis=1) for row in swapped], axis=0)
    l3_high, l3_low = split(l3)

    n = ROWS
    row = leaf_ref[...]
    col = col_of(row)[:, 0:1]
    same = jnp.where((col == row) & (iota((n, n), 1) < iota((n, n), 0)), 1.0, 0.0).astype(BF16)
    rank = dot(same, jnp.ones((n, 128), BF16))[:, 0:1].astype(jnp.int32)
    slot = col * 8 + rank
    lane = iota((n, 1024), 1)
    near_lo = dot(jnp.where(lane == slot, 1.0, 0.0).astype(BF16), ret_ref[:, :512])
    near_hi = dot(jnp.where(lane == slot + 4, 1.0, 0.0).astype(BF16), ret_ref[:, :512])
    mine = jnp.where(iota((n, 128), 1) == col, 1.0, 0.0).astype(BF16)
    local = dot(mine, l3_high) + dot(mine, l3_low)
    feat = feat_ref[...].astype(F32)
    near = jnp.concatenate([near_lo, near_hi], axis=1)
    out_ref[...] = (feat + near + feat * local).astype(BF16)


def finish(ret, features, leaf_row, mats):
    return pl.pallas_call(
        finish_kernel,
        out_shape=jax.ShapeDtypeStruct((ROWS, WIDTH), BF16),
        scratch_shapes=[pltpu.VMEM((1024, 128), F32)],
        name="finish",
    )(ret, features, leaf_row, *mats)


def blocks(mats, scale, flip):
    m0, m1, m2, m3 = [(m.T if flip else m) * jnp.asarray(scale, m.dtype) for m in mats]
    w1a = jnp.pad(m1, ((0, 64), (0, 64)))
    w1b = jnp.pad(m1, ((64, 0), (64, 0)))
    w2 = jnp.pad(m2, ((0, 128), (0, 128))) + jnp.pad(m2, ((128, 0), (128, 0)))
    w3 = jnp.pad(m3, ((0, 64), (0, 64))) + jnp.pad(m3, ((64, 0), (64, 0)))
    return m0, w1a, w1b, w2, w3


def tree_mats(lift_leaf, lift_branch, couple_root, couple_branch, couple_leaf):
    up2 = lift_leaf.transpose(1, 2, 0).reshape(16, 128)
    up1 = lift_branch.reshape(64, 16)
    keep4 = (1.0 - jnp.eye(4, dtype=F32))[:, :, None, None]
    keep8 = (1.0 - jnp.eye(8, dtype=F32))[:, :, None, None]
    root = (couple_root * keep4).transpose(0, 2, 1, 3).reshape(64, 64)
    mid = [lift_branch.transpose(0, 2, 1).reshape(64, 16)]
    for shift in range(1, 4):
        mid.append(jnp.stack([couple_branch[b, (b + shift) % 4] for b in range(4)]).reshape(64, 16))
    mid = jnp.concatenate(mid, axis=1)
    low = (couple_leaf * keep8).transpose(2, 0, 3, 1).reshape(128, 128)
    lift = lift_leaf.transpose(2, 0, 1).reshape(128, 16)
    return up2, up1, root, mid, jnp.concatenate([low, lift], axis=1)


def degree_table():
    table = np.zeros((256, 128), np.float32)
    for degree in range(4):
        table[degree * 64 : (degree + 1) * 64, degree::4] = 1.0
    return jnp.asarray(table, BF16)


def swap(x):
    return lax.all_to_all(x, AXES, split_axis=0, concat_axis=0, tiled=True)


def shards(
    features,
    cotangent,
    leaf_device,
    neighbours,
    radial,
    first_zero,
    first_one,
    first_two,
    first_three,
    second_zero,
    second_one,
    second_two,
    second_three,
    lift_leaf,
    lift_branch,
    couple_root,
    couple_branch,
    couple_leaf,
):
    leaf_row = leaf_device.reshape(1, ROWS)
    send = pack(leaf_row, features, cotangent)
    got = swap(send.reshape(128, 8, WIDTH))
    rad = jnp.pad(radial.T, ((0, 0), (0, 64)))
    firsts = (first_zero, first_one, first_two, first_three)
    seconds = (second_zero, second_one, second_two, second_three)
    got = got.reshape(64, 2, 8, WIDTH)
    u, back, own, table, index, occ = leaf_a(
        got, neighbours, rad, blocks(firsts, 0.5, False), blocks(seconds, 1.0, False)
    )
    ret = swap(back.reshape(128, 8, 640))
    grads = leaf_b(
        index, u, got, own, table, occ, blocks(firsts, 0.5, True), blocks(seconds, 1.0, True), degree_table()
    )
    mats = tree_mats(lift_leaf, lift_branch, couple_root, couple_branch, couple_leaf)
    updated = finish(ret.reshape(1024, 640), features, leaf_row, mats)
    return updated, grads


def solution(mesh):
    spread = P(AXES, None)
    across = P(None, AXES)
    return jax.shard_map(
        shards,
        mesh=mesh,
        in_specs=(spread, spread, spread, across, across) + (P(),) * 13,
        out_specs=(spread, across),
        check_vma=False,
    )
```

time: 129 us -> 123 us (0.953)
  waiting for transfers between devices: 17.3 us -> 7 us
  local copies, waits for them, and re-layouts: 11.3 us -> 21 us
  Pallas kernels: 77.6 us -> 69.3 us
  other arithmetic: 3.25 us -> 6.8 us
    all_to_all x2, waiting for transfers between devices: 17.3 us -> 7 us  [swap(): return lax.all_to_all(x, AXES, split_axis=0, concat_axis=0, tiled=True)]
    pallas_call x2, Pallas kernels: 67.6 us -> 60.1 us  [the longest x1 31.5 us: leaf_a(): pl.pallas_call(leaf_a_kernel, grid=(NBR // 2,), in_specs=[full(x) for x i...]
    unnamed x50 -> x60, local copies, waits for them, and re-layouts: 3.37 us -> 8.7 us
    mul x4, other arithmetic: 0.05 us -> 1.93 us  [blocks(): (m.T if flip else m) * jnp.asarray(scale, m.dtype)]
  transfers between devices with their start and end apart: 2 -> 2, of which waited for: 1 -> 1; matrix products, arithmetic and copies ran while one was open for 10% -> 20% of each run, Pallas kernels for 23% -> 23%
where the time goes in v2:
time: 123 us; the launch traced here: 122 us
  Pallas kernels  69.3 us (56%)
  local copies, waits for them, and re-layouts  21 us (17%)
  starting transfers between devices  17.2 us (14%)
  waiting for transfers between devices  7 us (6%)
  other arithmetic  6.8 us (6%)
    pallas_call x1, Pallas kernels, leaf_a(): pl.pallas_call(leaf_a_kernel, grid=(NBR // 2,), in_specs=[full(x) for x i...  31.5 us
    pallas_call x1, Pallas kernels, leaf_b(): pl.pallas_call(leaf_b_kernel, grid=(NBR // 2,), in_specs=[full(index), pl...  28.6 us
    all_to_all x2, starting transfers between devices, swap(): return lax.all_to_all(x, AXES, split_axis=0, concat_axis=0, tiled=True)  17.2 us
    unnamed x60, local copies, waits for them, and re-layouts  8.7 us
    all_to_all x2, waiting for transfers between devices, swap(): return lax.all_to_all(x, AXES, split_axis=0, concat_axis=0, tiled=True)  7 us
    pallas_call x1, Pallas kernels, finish(): pl.pallas_call(finish_kernel, out_shape=jax.ShapeDtypeStruct((ROWS, WIDTH...  4.95 us
    pallas_call x1, Pallas kernels, pack(): pl.pallas_call(pack_kernel, out_shape=jax.ShapeDtypeStruct((128 * 8, WIDT...  4.26 us
  transfers between devices with their start and end apart: 2, of which 1 were waited for; matrix products, arithmetic and copies ran while one was open for 20% of the time, Pallas kernels for 23%

profile of v2, /device:TPU:0, one launch (start us, length us, event | category | flops | bytes accessed | tf_op | source)
XLA Modules:
  0.0 122.3 jit_solution(14883757386518360867)
XLA Ops:
  0.6 4.3 %pack.1 = bf16[1024,1024]{1,0:T(8,128)(2,1)} custom-call(s32[1,256]{1,0:T(1,128)} %bitcast.77, bf16[256,1024]{1,0:T(8,128)(2,1)} %feat_ref.3, bf16[256,1024]{1,0:T(8,128)(2,1)} %grad_ref.1), custom_call_target="tpu_custom_call" | custom-call | tf_op jit(solution)/shard_map/pack/pallas_call | solution.py:61
  4.9 11.2 %all-to-all-start = ((bf16[128,8,1024]{2,1,0:T(8,128)(2,1)}), bf16[128,8,1024]{2,1,0:T(8,128)(2,1)S(1)}, u32[]{:S(2)}, u32[]{:S(2)}) async-start(bf16[128,8,1024]{2,1,0:T(8,128)(2,1)} %bitcast.61), calls=%async_computation | async-start | bytes 4194304 | tf_op jit(solution)/shard_map/all_to_all | solution.py:509
  16.1 0.0 copy-start.13
  16.1 0.0 copy-start.7
  16.2 0.1 copy.42
  16.3 0.7 fusion.2
  16.9 0.7 copy.60
  17.7 0.1 copy.41
  17.8 0.8 copy.45.f0
  18.6 0.9 copy.43
  19.4 0.6 fusion.1
  20.1 0.8 copy.48.f2
  20.8 0.8 copy.44
  21.6 0.6 fusion
  22.3 0.1 pad_add_fusion.7
  22.3 0.7 copy.49.f3
  23.0 0.8 copy.40
  23.9 0.7 copy.57
  24.6 0.7 copy.58
  25.3 0.7 copy.59
  26.0 0.1 copy.56
  26.2 0.7 copy.52
  26.9 0.9 multiply_bitcast_fusion
  27.8 1.4 %copy.53 = f32[16,8,16,8]{3,2,1,0:T(8,128)S(1)} copy(f32[16,8,16,8]{2,0,3,1:T(8,128)} %multiply_bitcast_fusion) | data formatting | bytes 131072 | tf_op jit(solution)/shard_map/transpose | solution.py:496
  29.2 1.1 reshape.76
  30.3 1.0 copy.54
  31.3 1.0 multiply_bitcast_fusion.1
  32.3 0.1 copy.51
  32.3 0.7 reshape.71.root_ref
  33.0 0.9 copy.50
  34.0 0.7 copy.55.up2_ref
  34.6 1.7 %pad.82.rad_ref = f32[512,128]{1,0:T(8,128)} pad(f32[512,64]{1,0:T(8,128)} %bitcast.63, f32[]{:T(128)} %constant.5.clone.1), padding=0_0x0_64 | pad | bytes 393220 | tf_op jit(solution)/shard_map/jit(_pad)/pad | solution.py:535
  36.3 0.7 pad_add_fusion.6.s3
  37.0 0.9 slice_bitcast_fusion.11
  37.9 0.7 pad_add_fusion.2.s2
  38.5 0.9 fusion.6
  39.4 7.0 %all-to-all-done = bf16[128,8,1024]{2,1,0:T(8,128)(2,1)S(1)} async-done(((bf16[128,8,1024]{2,1,0:T(8,128)(2,1)}), bf16[128,8,1024]{2,1,0:T(8,128)(2,1)S(1)}, u32[]{:S(2)}, u32[]{:S(2)}) %all-to-all-start) | async-done | bytes 2097184 | tf_op jit(solution)/shard_map/all_to_all | solution.py:509
  46.4 1.3 %copy-done = bf16[128,8,1024]{2,1,0:T(8,128)(2,1)} copy-done((bf16[128,8,1024]{2,1,0:T(8,128)(2,1)}, bf16[128,8,1024]{2,1,0:T(8,128)(2,1)S(1)}, u32[]{:S(2)}) %copy-start) | copy-done | bytes 2097176
  47.8 31.5 %leaf_a.1 = (f32[16,512,1024]{2,1,0:T(8,128)}, bf16[64,2,8,640]{3,2,1,0:T(8,128)(2,1)}, f32[4096,128]{1,0:T(8,128)}, f32[4104,128]{1,0:T(8,128)}, s32[16,4,128]{2,1,0:T(4,128)}, /*index=5*/f32[8,128]{1,0:T(8,128)}) custom-call(bf16[64,2,8,1024]{3,2,1,0:T(8,128)(2,1)} %bitcast.58, s32[16,512]{1,0:T(8,128)} %nbr_ref.1, f32[512,128]{1,0:T(8,128)} %pad.82.rad_ref, ...), custom_call_target="tpu_custom_call" | custom-call | flops 6442450944 | bytes 25165824 | tf_op jit(solution)/shard_map/leaf_a/pallas_call | solution.py:260
  79.4 0.0 copy-start.3
  79.4 6.0 %all-to-all-start.1 = ((bf16[128,8,640]{2,1,0:T(8,128)(2,1)}), bf16[128,8,640]{2,1,0:T(8,128)(2,1)}, u32[]{:S(2)}, u32[]{:S(2)}) async-start(bf16[128,8,640]{2,1,0:T(8,128)(2,1)} %bitcast.62), calls=%async_computation.1 | async-start | bytes 2621440 | tf_op jit(solution)/shard_map/all_to_all | solution.py:509
  85.5 0.7 pad_maximum_fusion.4.mid_ref
  86.2 0.1 pad_add_fusion.4
  86.3 0.7 pad_maximum_fusion.low_ref
  87.0 0.1 fusion.4
  87.2 1.6 %copy-done.2 = f32[4096,128]{1,0:T(8,128)S(1)} copy-done((f32[4096,128]{1,0:T(8,128)S(1)}, f32[4096,128]{1,0:T(8,128)}, u32[]{:S(2)}) %copy-start.2) | copy-done | bytes 2097176
  88.8 28.6 %leaf_b.1 = f32[64,512]{1,0:T(8,128)} custom-call(s32[16,4,128]{2,1,0:T(4,128)S(1)} %copy-done.4, f32[16,512,1024]{2,1,0:T(8,128)} %get-tuple-element.10.u_ref, bf16[64,2,8,1024]{3,2,1,0:T(8,128)(2,1)S(1)} %bitcast.59, f32[4096,128]{1,0:T(8,128)S(1)} %copy-done.2, f32[4104,128]{1,0:T(8,128)} %get-tuple-element.12.table_ref, f32[8,128]{1,0:T(8,128)S(1)} %copy-done.5, ...), custom_call_target="tpu_custom_call" | custom-call | flops 6442450944 | bytes 25165824 | tf_op jit(solution)/shard_map/leaf_b/pallas_call | solution.py:366
  117.3 5.0 %finish.1 = bf16[256,1024]{1,0:T(8,128)(2,1)} custom-call(bf16[1024,640]{1,0:T(8,128)(2,1)} %bitcast.5.ret_ref, bf16[256,1024]{1,0:T(8,128)(2,1)} %feat_ref.3, s32[1,256]{1,0:T(1,128)} %bitcast.78, f32[16,128]{1,0:T(8,128)} %copy.55.up2_ref, f32[64,16]{1,0:T(8,128)} %bitcast.69, f32[64,64]{1,0:T(8,128)} %reshape.71.root_ref, ...), custom_call_target="tpu_custom_call" | custom-call | tf_op jit(solution)/shard_map/finish/pallas_call | solution.py:469
  (53 shorter events, 0.2 us)
Async XLA Ops:
  4.9 11.2 %copy-start.21 = (bf16[192,192]{1,0:T(8,128)(2,1)S(1)}, bf16[192,192]{1,0:T(8,128)(2,1)}, u32[]{:S(2)}) copy-start(bf16[192,192]{1,0:T(8,128)(2,1)} %param.25) | copy-start | bytes 221188
  4.9 12.8 %copy-start.19 = (bf16[256,256]{1,0:T(8,128)(2,1)S(1)}, bf16[256,256]{1,0:T(8,128)(2,1)}, u32[]{:S(2)}) copy-start(bf16[256,256]{1,0:T(8,128)(2,1)} %param.24) | copy-start | bytes 393220
  4.9 41.5 %all-to-all-start = ((bf16[128,8,1024]{2,1,0:T(8,128)(2,1)}), bf16[128,8,1024]{2,1,0:T(8,128)(2,1)S(1)}, u32[]{:S(2)}, u32[]{:S(2)}) async-start(bf16[128,8,1024]{2,1,0:T(8,128)(2,1)} %bitcast.61), calls=%async_computation | async-start | bytes 4194304 | tf_op jit(solution)/shard_map/all_to_all | solution.py:509
  16.1 7.0 %copy-start.13 = (f32[64,512]{1,0:T(8,128)S(1)}, f32[64,512]{1,0:T(8,128)}, u32[]{:S(2)}) copy-start(f32[64,512]{1,0:T(8,128)} %param.23) | copy-start | bytes 393220
  16.1 7.8 %copy-start.7 = (bf16[192,192]{1,0:T(8,128)(2,1)S(1)}, bf16[192,192]{1,0:T(8,128)(2,1)}, u32[]{:S(2)}) copy-start(bf16[192,192]{1,0:T(8,128)(2,1)} %param.29) | copy-start | bytes 221188
  16.1 8.5 %copy-start.15 = (bf16[128,128]{1,0:T(8,128)(2,1)S(1)}, bf16[128,128]{1,0:T(8,128)(2,1)}, u32[]{:S(2)}) copy-start(bf16[128,128]{1,0:T(8,128)(2,1)} %param.30) | copy-start | bytes 98308
  16.1 9.2 %copy-start.22 = (bf16[64,64]{1,0:T(8,128)(2,1)S(1)}, bf16[64,64]{1,0:T(8,128)(2,1)}, u32[]{:S(2)}) copy-start(bf16[64,64]{1,0:T(8,128)(2,1)} %param.31) | copy-start | bytes 24580
  16.1 9.9 %copy-start.20 = (bf16[256,256]{1,0:T(8,128)(2,1)S(1)}, bf16[256,256]{1,0:T(8,128)(2,1)}, u32[]{:S(2)}) copy-start(bf16[256,256]{1,0:T(8,128)(2,1)} %s0.1) | copy-start | bytes 393220
  16.1 10.0 %copy-start.12 = (f32[4,16,16]{2,1,0:T(8,128)S(1)}, f32[4,16,16]{2,1,0:T(8,128)}, u32[]{:S(2)}) copy-start(f32[4,16,16]{2,1,0:T(8,128)} %param.33) | copy-start | bytes 12292
  16.1 10.7 %copy-start.6 = (f32[8,8,16,16]{3,2,1,0:T(8,128)S(1)}, f32[8,8,16,16]{3,2,1,0:T(8,128)}, u32[]{:S(2)}) copy-start(f32[8,8,16,16]{3,2,1,0:T(8,128)} %param.36) | copy-start | bytes 196612
  27.8 10.1 %copy-start.16 = (bf16[128,128]{1,0:T(8,128)(2,1)S(1)}, bf16[128,128]{1,0:T(8,128)(2,1)}, u32[]{:S(2)}) copy-start(bf16[128,128]{1,0:T(8,128)(2,1)} %param.30) | copy-start | bytes 98308
  30.3 8.3 %copy-start.9 = (bf16[192,192]{1,0:T(8,128)(2,1)S(1)}, bf16[192,192]{1,0:T(8,128)(2,1)}, u32[]{:S(2)}) copy-start(bf16[192,192]{1,0:T(8,128)(2,1)} %copy.60) | copy-start | bytes 221188
  46.4 1.3 %copy-start = (bf16[128,8,1024]{2,1,0:T(8,128)(2,1)}, bf16[128,8,1024]{2,1,0:T(8,128)(2,1)S(1)}, u32[]{:S(2)}) copy-start(bf16[128,8,1024]{2,1,0:T(8,128)(2,1)S(1)} %all-to-all-done) | copy-start | bytes 6291460
  79.3 6.2 %copy-start.18 = (f32[4,16,16]{2,1,0:T(8,128)S(1)}, f32[4,16,16]{2,1,0:T(8,128)}, u32[]{:S(2)}) copy-start(f32[4,16,16]{2,1,0:T(8,128)} %copy.52) | copy-start | bytes 12292
  79.3 6.9 %copy-start.23 = (bf16[64,64]{1,0:T(8,128)(2,1)S(1)}, bf16[64,64]{1,0:T(8,128)(2,1)}, u32[]{:S(2)}) copy-start(bf16[64,64]{1,0:T(8,128)(2,1)} %get-tuple-element.40) | copy-start | bytes 24580
  79.3 6.9 %copy-start.24 = (bf16[64,64]{0,1:T(8,128)(2,1)S(1)}, bf16[64,64]{0,1:T(8,128)(2,1)}, u32[]{:S(2)}) copy-start(bf16[64,64]{0,1:T(8,128)(2,1)} %copy.59) | copy-start | bytes 24580
  79.3 7.0 %copy-start.11 = (f32[128,128]{1,0:T(8,128)S(1)}, f32[128,128]{1,0:T(8,128)}, u32[]{:S(2)}) copy-start(f32[128,128]{1,0:T(8,128)} %reshape.76) | copy-start | bytes 196612
  79.3 7.6 %copy-start.14 = (bf16[128,128]{1,0:T(8,128)(2,1)S(1)}, bf16[128,128]{1,0:T(8,128)(2,1)}, u32[]{:S(2)}) copy-start(bf16[128,128]{1,0:T(8,128)(2,1)} %get-tuple-element.38) | copy-start | bytes 98308
  79.3 7.6 %copy-start.17 = (bf16[128,128]{0,1:T(8,128)(2,1)S(1)}, bf16[128,128]{0,1:T(8,128)(2,1)}, u32[]{:S(2)}) copy-start(bf16[128,128]{0,1:T(8,128)(2,1)} %copy.58) | copy-start | bytes 98308
  79.3 7.6 %copy-start.8 = (bf16[192,192]{0,1:T(8,128)(2,1)S(1)}, bf16[192,192]{0,1:T(8,128)(2,1)}, u32[]{:S(2)}) copy-start(bf16[192,192]{0,1:T(8,128)(2,1)} %copy.57) | copy-start | bytes 221188
  79.4 7.6 %copy-start.10 = (bf16[192,192]{1,0:T(8,128)(2,1)S(1)}, bf16[192,192]{1,0:T(8,128)(2,1)}, u32[]{:S(2)}) copy-start(bf16[192,192]{1,0:T(8,128)(2,1)} %get-tuple-element.32) | copy-start | bytes 221188
  79.4 7.8 %copy-start.1 = (bf16[128,8,1024]{2,1,0:T(8,128)(2,1)S(1)}, bf16[128,8,1024]{2,1,0:T(8,128)(2,1)}, u32[]{:S(2)}) copy-start(bf16[128,8,1024]{2,1,0:T(8,128)(2,1)} %copy-done) | copy-start | bytes 6291460
  79.4 7.8 %copy-start.3 = (bf16[256,128]{1,0:T(8,128)(2,1)S(1)}, bf16[256,128]{1,0:T(8,128)(2,1)}, u32[]{:S(2)}) copy-start(bf16[256,128]{1,0:T(8,128)(2,1)} %constant.4.clone.sum_ref) | copy-start | bytes 196612
  79.4 7.8 %copy-start.4 = (s32[16,4,128]{2,1,0:T(4,128)S(1)}, s32[16,4,128]{2,1,0:T(4,128)}, u32[]{:S(2)}) copy-start(s32[16,4,128]{2,1,0:T(4,128)} %get-tuple-element.9.index_ref) | copy-start | bytes 98308
  79.4 7.8 %copy-start.5 = (f32[8,128]{1,0:T(8,128)S(1)}, f32[8,128]{1,0:T(8,128)}, u32[]{:S(2)}) copy-start(f32[8,128]{1,0:T(8,128)} %get-tuple-element.13.occ_ref) | copy-start | bytes 12292
  79.4 37.9 %all-to-all-start.1 = ((bf16[128,8,640]{2,1,0:T(8,128)(2,1)}), bf16[128,8,640]{2,1,0:T(8,128)(2,1)}, u32[]{:S(2)}, u32[]{:S(2)}) async-start(bf16[128,8,640]{2,1,0:T(8,128)(2,1)} %bitcast.62), calls=%async_computation.1 | async-start | bytes 2621440 | tf_op jit(solution)/shard_map/all_to_all | solution.py:509
  87.2 1.6 %copy-start.2 = (f32[4096,128]{1,0:T(8,128)S(1)}, f32[4096,128]{1,0:T(8,128)}, u32[]{:S(2)}) copy-start(f32[4096,128]{1,0:T(8,128)} %get-tuple-element.11.own_ref) | copy-start | bytes 6291460

commit v3 on v2

--- a/solution.py
+++ b/solution.py
@@ -16,7 +16,7 @@
 POOL = 512
 WIDTH = 1024
 NBR = 16
-TILE = 256
+TILE = 128
 
 
 def dot(a, b, **kw):
@@ -83,25 +83,26 @@
     ]
 
 
-def gather(index, own_ref, table_ref, out_ref, first, last, tiled):
-    for i in range(first, last):
-        start = pl.multiple_of(index[i >> 7, i & 127], 8)
-        row = own_ref[i * 8 : (i + 1) * 8, :] + table_ref[pl.ds(start, 8), :]
-        if tiled:
-            out_ref[i >> 3, pl.ds(i & 7, 8, stride=8), :] = row
-        else:
-            out_ref[i * 8 : (i + 1) * 8, :] = row
-
-
-def fetch(index_ref, k, index_smem, sem):
-    return pltpu.make_async_copy(index_ref.at[jnp.minimum(k, NBR - 1)], index_smem, sem)
-
-
-def scales(rad_ref, rows, k):
-    size = rows.size
-    shifted = pltpu.roll(rad_ref[rows, :], (128 - 4 * k) % 128, 1)
-    r0, r1, r2, r3 = [jnp.broadcast_to(shifted[:, j : j + 1], (size, 128)) for j in range(4)]
-    low = iota((size, 128), 1) < 64
+def gather(index_ref, pair, part, own_ref, table_ref, out_ref):
+    index = [index_ref.at[2 * pair], index_ref.at[2 * pair + 1]]
+    for j in range(TILE):
+        i = part * TILE + j
+        own = own_ref[i * 8 : (i + 1) * 8, :]
+        for which in range(2):
+            start = pl.multiple_of(index[which][i >> 7, i & 127], 8)
+            row = own + table_ref[pl.ds(start, 8), :]
+            out_ref[(which * TILE + j) >> 3, pl.ds(j & 7, 8, stride=8), :] = row
+
+
+def both(a, b):
+    return jnp.concatenate([a, b], axis=0)
+
+
+def scales(rad_ref, rows, pair):
+    shifted = pltpu.roll(rad_ref[rows, :], (128 - 8 * pair) % 128, 1)
+    r = [jnp.broadcast_to(shifted[:, j : j + 1], (TILE, 128)) for j in range(8)]
+    r0, r1, r2, r3 = [both(r[j], r[j + 4]) for j in range(4)]
+    low = iota((2 * TILE, 128), 1) < 64
     p01 = jnp.where(low, r0, r1)
     p23 = jnp.where(low, r2, r3)
     p12 = jnp.where(low, r1, r2)
@@ -139,17 +140,15 @@
     occ_ref,
     acc_ref,
     tile_ref,
-    buf0_ref,
-    buf1_ref,
+    buf0,
+    buf1,
+    buf2,
+    buf3,
     rank_ref,
     rank_smem,
-    first_smem,
-    odd_smem,
-    even_smem,
+    index_smem,
     sem0,
     sem1,
-    sem2,
-    sem3,
 ):
     step = pl.program_id(0)
 
@@ -178,9 +177,8 @@
         left = 8 * jnp.where(left >= filled, left - filled, left).astype(jnp.int32)
         for r in range(4):
             index_ref[:, r, :] = left[:, r * 128 : (r + 1) * 128]
-        fetch(index_ref, 0, first_smem, sem1).start()
-        fetch(index_ref, 1, odd_smem, sem2).start()
-        fetch(index_ref, 2, even_smem, sem3).start()
+        index_to_smem = pltpu.make_async_copy(index_ref, index_smem, sem1)
+        index_to_smem.start()
         sums = dot(occ.astype(BF16), got_ref[...].reshape(1024, WIDTH))
         tile_ref[...] = sums * (1.0 / math.sqrt(ROWS))
         for pair in range(64):
@@ -195,32 +193,28 @@
             s = (i >> 2) * 8 + (i & 3)
             to = pl.multiple_of(rank_smem[s >> 7, s & 127], 8)
             table_ref[pl.ds(to, 8), :] = own_ref[i * 8 : (i + 1) * 8, :]
-        fetch(index_ref, 0, first_smem, sem1).wait()
-        gather(first_smem, own_ref, table_ref, buf0_ref, 0, POOL, False)
-
-    turns = ((buf0_ref, buf1_ref, odd_smem, sem2), (buf1_ref, buf0_ref, even_smem, sem3))
-    for half, (buf, other, index_smem, sem) in enumerate(turns):
-        k = step * 2 + half
-        fetch(index_ref, k + 1, index_smem, sem).wait()
-        for part in range(POOL // TILE):
-            rows = pl.ds(part * TILE, TILE)
-            gather(index_smem, own_ref, table_ref, other, part * TILE, (part + 1) * TILE, False)
-            pats = scales(rad_ref, rows, k)
-
-            def piece(g):
-                y = buf[pl.ds(part * TILE * 8 + g, TILE, stride=8), :]
-                return (y * pats[g]).astype(BF16)
-
-            def use(g, w):
-                cols = slice(g * 128, (g + 1) * 128)
-                acc_ref[rows, cols] += w + w * jnp.tanh(w)
-                u_ref[half, rows, cols] = w
-
-            mix_blocks(piece, f0, f1a, f1b, f2, f3, use)
-
-        @pl.when(step < NBR // 2 - 1)
-        def _():
-            fetch(index_ref, k + 3, index_smem, sem).start()
+        index_to_smem.wait()
+        gather(index_smem, 0, 0, own_ref, table_ref, buf0)
+
+    bufs = (buf0, buf1, buf2, buf3)
+    for turn in range(4):
+        after = jnp.minimum(step + (turn + 1) // 4, NBR // 2 - 1)
+        gather(index_smem, after, (turn + 1) % 4, own_ref, table_ref, bufs[(turn + 1) % 4])
+        rows = pl.ds(turn * TILE, TILE)
+        pats = scales(rad_ref, rows, step)
+
+        def piece(g):
+            y = bufs[turn][:, g * 8 : (g + 1) * 8, :].reshape(2 * TILE, 128)
+            return (y * pats[g]).astype(BF16)
+
+        def use(g, w):
+            cols = slice(g * 128, (g + 1) * 128)
+            v = w + w * jnp.tanh(w)
+            acc_ref[rows, cols] += v[:TILE] + v[TILE:]
+            u_ref[0, rows, cols] = w[:TILE]
+            u_ref[1, rows, cols] = w[TILE:]
+
+        mix_blocks(piece, f0, f1a, f1b, f2, f3, use)
 
     @pl.when(step == NBR // 2 - 1)
     def _():
@@ -243,8 +237,7 @@
         back_ref[:, :, :, 512:] = body
 
 
-def full(x):
-    return pl.BlockSpec(x.shape, lambda k, n=len(x.shape): (0,) * n)
+WHOLE = pl.BlockSpec(memory_space=pltpu.VMEM)
 
 
 def leaf_a(got, nbr, rad, firsts, seconds):
@@ -260,25 +253,22 @@
     return pl.pallas_call(
         leaf_a_kernel,
         grid=(NBR // 2,),
-        in_specs=[full(x) for x in args],
-        out_specs=[pl.BlockSpec((2, POOL, WIDTH), lambda k: (k, 0, 0))] + [full(x) for x in out_shape[1:]],
+        in_specs=[WHOLE] * len(args),
+        out_specs=[pl.BlockSpec((2, POOL, WIDTH), lambda k: (k, 0, 0))] + [WHOLE] * (len(out_shape) - 1),
         out_shape=out_shape,
         scratch_shapes=[
             pltpu.VMEM((POOL, WIDTH), F32),
             pltpu.VMEM((8, WIDTH), F32),
-            pltpu.VMEM((POOL * 8, 128), F32),
-            pltpu.VMEM((POOL * 8, 128), F32),
+        ]
+        + [pltpu.VMEM((TILE // 4, 64, 128), F32)] * 4
+        + [
             pltpu.VMEM((8, 128), jnp.int32),
             pltpu.SMEM((8, 128), jnp.int32),
-            pltpu.SMEM((4, 128), jnp.int32),
-            pltpu.SMEM((4, 128), jnp.int32),
-            pltpu.SMEM((4, 128), jnp.int32),
-            pltpu.SemaphoreType.DMA,
-            pltpu.SemaphoreType.DMA,
+            pltpu.SMEM((NBR, 4, 128), jnp.int32),
             pltpu.SemaphoreType.DMA,
             pltpu.SemaphoreType.DMA,
         ],
-        compiler_params=pltpu.CompilerParams(vmem_limit_bytes=56 << 20),
+        compiler_params=pltpu.CompilerParams(vmem_limit_bytes=40 << 20),
         cost_estimate=pl.CostEstimate(flops=6 << 30, bytes_accessed=24 << 20, transcendentals=8 << 20),
         name="leaf_a",
     )(*args)
@@ -288,16 +278,12 @@
     index_ref, u_ref, got_ref, own_ref, table_ref, occ_ref,
     t0, t1a, t1b, t2, t3,
     s0, s1a, s1b, s2, s3,
-    sum_ref, out_ref, acc_ref, half_t_ref, buf0_ref, buf1_ref,
-    first_smem, odd_smem, even_smem, sem1, sem2, sem3,
+    sum_ref, out_ref, acc_ref, half_t_ref, buf0, buf1, buf2, buf3,
 ):
     step = pl.program_id(0)
 
     @pl.when(step == 0)
     def _():
-        fetch(index_ref, 0, first_smem, sem1).start()
-        fetch(index_ref, 1, odd_smem, sem2).start()
-        fetch(index_ref, 2, even_smem, sem3).start()
         acc_ref[...] = jnp.zeros_like(acc_ref)
         top = iota((8, WIDTH), 0) < 4
         for part in range(POOL // TILE):
@@ -312,44 +298,41 @@
                 half_t_ref[rows, g * 128 : (g + 1) * 128] = 0.5 * value
 
             mix_blocks(lambda g: grad[:, g * 128 : (g + 1) * 128], s0, s1a, s1b, s2, s3, use)
-        fetch(index_ref, 0, first_smem, sem1).wait()
-        gather(first_smem, own_ref, table_ref, buf0_ref, 0, POOL, True)
-
-    turns = ((buf0_ref, buf1_ref, odd_smem, sem2), (buf1_ref, buf0_ref, even_smem, sem3))
-    for half, (buf, other, index_smem, sem) in enumerate(turns):
-        k = step * 2 + half
-        fetch(index_ref, k + 1, index_smem, sem).wait()
-        for part in range(POOL // TILE):
-            rows = pl.ds(part * TILE, TILE)
-            gather(index_smem, own_ref, table_ref, other, part * TILE, (part + 1) * TILE, True)
-            prods = {}
-
-            def piece(g):
-                cols = slice(g * 128, (g + 1) * 128)
-                w = u_ref[half, rows, cols]
+        gather(index_ref, 0, 0, own_ref, table_ref, buf0)
+
+    bufs = (buf0, buf1, buf2, buf3)
+    for turn in range(4):
+        after = jnp.minimum(step + (turn + 1) // 4, NBR // 2 - 1)
+        gather(index_ref, after, (turn + 1) % 4, own_ref, table_ref, bufs[(turn + 1) % 4])
+        rows = pl.ds(turn * TILE, TILE)
+        prods = {}
+
+        def piece(g):
+            cols = slice(g * 128, (g + 1) * 128)
+            half_t = half_t_ref[rows, cols]
+            out = []
+            for which in range(2):
+                w = u_ref[which, rows, cols]
                 h = jnp.tanh(w)
                 up = 1.0 + h
-                return ((up + (w * up) * (1.0 - h)) * half_t_ref[rows, cols]).astype(BF16)
-
-            def use(g, s):
-                tiles = slice(part * TILE // 8, (part + 1) * TILE // 8)
-                prods[g] = s * buf[tiles, g * 8 : (g + 1) * 8, :].reshape(TILE, 128)
-
-            mix_blocks(piece, t0, t1a, t1b, t2, t3, use)
-            low = iota((TILE, 128), 1) < 64
-            ones = jnp.where(low, prods[2], prods[3])
-            ones = ones + pltpu.roll(ones, 64, 1)
-            threes = prods[7] + pltpu.roll(prods[7], 64, 1)
-            cross = pltpu.roll(jnp.where(low, prods[3], prods[2]), 64, 1)
-            x01 = prods[0] + jnp.where(low, 0.0, ones)
-            x23 = (prods[1] + prods[4]) + (prods[5] + prods[6]) + cross + jnp.where(low, 0.0, threes)
-            sums = dot(jnp.concatenate([x01, x23], axis=1).astype(BF16), sum_ref[...])
-            mine = (iota((TILE, 128), 1) >> 2) == k
-            acc_ref[rows, :] = jnp.where(mine, sums, acc_ref[rows, :])
-
-        @pl.when(step < NBR // 2 - 1)
-        def _():
-            fetch(index_ref, k + 3, index_smem, sem).start()
+                out.append(((up + (w * up) * (1.0 - h)) * half_t).astype(BF16))
+            return both(*out)
+
+        def use(g, s):
+            prods[g] = s * bufs[turn][:, g * 8 : (g + 1) * 8, :].reshape(2 * TILE, 128)
+
+        mix_blocks(piece, t0, t1a, t1b, t2, t3, use)
+        low = iota((2 * TILE, 128), 1) < 64
+        ones = jnp.where(low, prods[2], prods[3])
+        ones = ones + pltpu.roll(ones, 64, 1)
+        threes = prods[7] + pltpu.roll(prods[7], 64, 1)
+        cross = pltpu.roll(jnp.where(low, prods[3], prods[2]), 64, 1)
+        x01 = prods[0] + jnp.where(low, 0.0, ones)
+        x23 = (prods[1] + prods[4]) + (prods[5] + prods[6]) + cross + jnp.where(low, 0.0, threes)
+        sums = dot(jnp.concatenate([x01, x23], axis=1).astype(BF16), sum_ref[...])
+        owner = iota((TILE, 128), 1) >> 2
+        kept = jnp.where(owner == 2 * step, sums[:TILE], acc_ref[rows, :])
+        acc_ref[rows, :] = jnp.where(owner == 2 * step + 1, sums[TILE:], kept)
 
     @pl.when(step == NBR // 2 - 1)
     def _():
@@ -367,25 +350,18 @@
         leaf_b_kernel,
         grid=(NBR // 2,),
         in_specs=[
-            full(index),
+            pl.BlockSpec(memory_space=pltpu.SMEM),
             pl.BlockSpec((2, POOL, WIDTH), lambda k: (k, 0, 0)),
         ]
-        + [full(x) for x in args],
+        + [WHOLE] * len(args),
         out_specs=pl.BlockSpec((64, POOL), lambda k: (0, 0)),
         out_shape=jax.ShapeDtypeStruct((64, POOL), F32),
         scratch_shapes=[
             pltpu.VMEM((POOL, 128), F32),
             pltpu.VMEM((POOL, WIDTH), F32),
-            pltpu.VMEM((64, 64, 128), F32),
-            pltpu.VMEM((64, 64, 128), F32),
-            pltpu.SMEM((4, 128), jnp.int32),
-            pltpu.SMEM((4, 128), jnp.int32),
-            pltpu.SMEM((4, 128), jnp.int32),
-            pltpu.SemaphoreType.DMA,
-            pltpu.SemaphoreType.DMA,
-            pltpu.SemaphoreType.DMA,
-        ],
-        compiler_params=pltpu.CompilerParams(vmem_limit_bytes=48 << 20),
+        ]
+        + [pltpu.VMEM((TILE // 4, 64, 128), F32)] * 4,
+        compiler_params=pltpu.CompilerParams(vmem_limit_bytes=32 << 20),
         cost_estimate=pl.CostEstimate(flops=6 << 30, bytes_accessed=24 << 20, transcendentals=8 << 20),
         name="leaf_b",
     )(index, u, *args)

time: 123 us -> 121 us (0.984)
  Pallas kernels: 69.3 us -> 60.7 us
  local copies, waits for them, and re-layouts: 21 us -> 25 us
  waiting for transfers between devices: 7 us -> 9.51 us
    pallas_call x2, Pallas kernels: 60.1 us -> 51.5 us  [the longest x1 26.6 us: leaf_b(): pl.pallas_call(leaf_b_kernel, grid=(NBR // 2,), in_specs=[pl.BlockSpec(me...]
    unnamed x60 -> x84, local copies, waits for them, and re-layouts: 8.7 us -> 13.3 us
    all_to_all x2, waiting for transfers between devices: 7 us -> 9.51 us  [swap(): return lax.all_to_all(x, AXES, split_axis=0, concat_axis=0, tiled=True)]
    pad x1, local copies, waits for them, and re-layouts: 1.67 us -> 0.02 us  [shards(): rad = jnp.pad(radial.T, ((0, 0), (0, 64)))]
  transfers between devices with their start and end apart: 2 -> 2, of which waited for: 1 -> 1; matrix products, arithmetic and copies ran while one was open for 20% -> 18% of each run, Pallas kernels for 23% -> 22%
where the time goes in v3:
time: 121 us; the launch traced here: 120 us
  Pallas kernels  60.7 us (50%)
  local copies, waits for them, and re-layouts  25 us (21%)
  starting transfers between devices  17.2 us (14%)
  waiting for transfers between devices  9.51 us (8%)
  other arithmetic  6.97 us (6%)
    pallas_call x1, Pallas kernels, leaf_b(): pl.pallas_call(leaf_b_kernel, grid=(NBR // 2,), in_specs=[pl.BlockSpec(me...  26.6 us
    pallas_call x1, Pallas kernels, leaf_a(): pl.pallas_call(leaf_a_kernel, grid=(NBR // 2,), in_specs=[WHOLE] * len(ar...  24.9 us
    all_to_all x2, starting transfers between devices, swap(): return lax.all_to_all(x, AXES, split_axis=0, concat_axis=0, tiled=True)  17.2 us
    unnamed x84, local copies, waits for them, and re-layouts  13.3 us
    all_to_all x2, waiting for transfers between devices, swap(): return lax.all_to_all(x, AXES, split_axis=0, concat_axis=0, tiled=True)  9.51 us
    pallas_call x1, Pallas kernels, finish(): pl.pallas_call(finish_kernel, out_shape=jax.ShapeDtypeStruct((ROWS, WIDTH...  4.94 us
    pallas_call x1, Pallas kernels, pack(): pl.pallas_call(pack_kernel, out_shape=jax.ShapeDtypeStruct((128 * 8, WIDT...  4.24 us
  transfers between devices with their start and end apart: 2, of which 1 were waited for; matrix products, arithmetic and copies ran while one was open for 18% of the time, Pallas kernels for 22%

profile of v3, /device:TPU:0, one launch (start us, length us, event | category | flops | bytes accessed | tf_op | source)
XLA Modules:
  0.0 120.5 jit_solution(3654131151833683106)
XLA Ops:
  0.6 4.2 %pack.1 = bf16[1024,1024]{1,0:T(8,128)(2,1)} custom-call(s32[1,256]{1,0:T(1,128)} %bitcast.76, bf16[256,1024]{1,0:T(8,128)(2,1)} %feat_ref.3, bf16[256,1024]{1,0:T(8,128)(2,1)} %grad_ref.1), custom_call_target="tpu_custom_call" | custom-call | tf_op jit(solution)/shard_map/pack/pallas_call | solution.py:61
  4.9 11.2 %all-to-all-start = ((bf16[128,8,1024]{2,1,0:T(8,128)(2,1)}), bf16[128,8,1024]{2,1,0:T(8,128)(2,1)S(1)}, u32[]{:S(2)}, u32[]{:S(2)}) async-start(bf16[128,8,1024]{2,1,0:T(8,128)(2,1)} %bitcast.61), calls=%async_computation | async-start | bytes 4194304 | tf_op jit(solution)/shard_map/all_to_all | solution.py:485
  16.1 0.1 copy.42
  16.2 0.7 fusion.2
  16.9 0.7 copy.60
  17.6 0.1 copy.41
  17.8 0.1 copy.45.f0
  17.9 0.1 copy.43
  18.0 0.6 fusion.1
  18.7 0.1 copy.48.f2
  18.8 0.1 copy.44
  18.9 0.6 fusion
  19.6 0.7 copy.49.f3
  20.3 0.1 copy.40
  20.4 0.7 copy.57
  21.2 0.7 copy.58
  21.9 0.7 copy.59
  22.6 0.1 copy.56
  22.7 0.7 copy.52
  23.4 1.2 multiply_bitcast_fusion
  24.5 1.4 %copy.53 = f32[16,8,16,8]{3,2,1,0:T(8,128)} copy(f32[16,8,16,8]{2,0,3,1:T(8,128)S(1)} %multiply_bitcast_fusion) | data formatting | bytes 131072 | tf_op jit(solution)/shard_map/transpose | solution.py:472
  25.9 2.3 %reshape.76 = f32[128,128]{1,0:T(8,128)} reshape(f32[16,8,16,8]{3,2,1,0:T(8,128)} %copy.53) | data formatting | bytes 131072 | tf_op jit(solution)/shard_map/reshape | solution.py:472
  28.2 1.6 %copy.54 = f32[16,8,16]{2,1,0:T(8,128)} copy(f32[16,8,16]{0,2,1:T(8,128)} %bitcast.64) | data formatting | bytes 16384 | tf_op jit(solution)/shard_map/transpose | solution.py:473
  29.8 1.0 multiply_bitcast_fusion.1
  30.8 0.7 reshape.71.root_ref
  31.5 0.9 copy.50
  32.5 0.7 copy.55.up2_ref
  33.2 0.7 pad_add_fusion.6.s3
  33.8 0.6 slice_bitcast_fusion.11
  34.4 0.6 pad_maximum_fusion.1
  35.1 1.8 %fusion.6 = (bf16[256,256]{1,0:T(8,128)(2,1)S(1)}, bf16[256,256]{1,0:T(8,128)(2,1)S(1)}, bf16[256,256]{1,0:T(8,128)(2,1)S(1)}, bf16[256,256]{1,0:T(8,128)(2,1)}) fusion(bf16[192,192]{1,0:T(8,128)(2,1)} %param.29, bf16[192,192]{1,0:T(8,128)(2,1)} %copy.60), kind=kLoop, calls=%fused_computation.41 | loop fusion | bytes 671744 | tf_op jit(solution)/shard_map/jit(_pad)/pad | solution.py:456
  36.9 9.5 %all-to-all-done = bf16[128,8,1024]{2,1,0:T(8,128)(2,1)S(1)} async-done(((bf16[128,8,1024]{2,1,0:T(8,128)(2,1)}), bf16[128,8,1024]{2,1,0:T(8,128)(2,1)S(1)}, u32[]{:S(2)}, u32[]{:S(2)}) %all-to-all-start) | async-done | bytes 2097184 | tf_op jit(solution)/shard_map/all_to_all | solution.py:485
  46.4 0.9 copy-done.5
  47.3 0.8 copy-done.9
  48.1 0.8 copy-done.10
  48.8 0.8 copy-done.11
  49.6 24.9 %leaf_a.1 = (f32[16,512,1024]{2,1,0:T(8,128)}, bf16[64,2,8,640]{3,2,1,0:T(8,128)(2,1)}, f32[4096,128]{1,0:T(8,128)S(1)}, f32[4104,128]{1,0:T(8,128)S(1)}, s32[16...) custom-call(bf16[64,2,8,1024]{3,2,1,0:T(8,128)(2,1)S(1)} %bitcast.58, s32[16,512]{1,0:T(8,128)S(1)} %copy-done.11, ...), custom_call_target="tpu_custom_call" | custom-call | flops 6442450944 | bytes 25165824 | tf_op jit(solution)/shard_map/leaf_a/pallas_call | solution.py:253
  74.5 1.3 %copy-done = f32[4104,128]{1,0:T(8,128)} copy-done((f32[4104,128]{1,0:T(8,128)}, f32[4104,128]{1,0:T(8,128)S(1)}, u32[]{:S(2)}) %copy-start) | copy-done | bytes 2101272
  75.8 1.4 %copy-done.2 = f32[4096,128]{1,0:T(8,128)} copy-done((f32[4096,128]{1,0:T(8,128)}, f32[4096,128]{1,0:T(8,128)S(1)}, u32[]{:S(2)}) %copy-start.2) | copy-done | bytes 2097176
  77.2 0.6 copy-done.7
  77.9 6.0 %all-to-all-start.1 = ((bf16[128,8,640]{2,1,0:T(8,128)(2,1)}), bf16[128,8,640]{2,1,0:T(8,128)(2,1)}, u32[]{:S(2)}, u32[]{:S(2)}) async-start(bf16[128,8,640]{2,1,0:T(8,128)(2,1)} %bitcast.4), calls=%async_computation.1 | async-start | bytes 2621440 | tf_op jit(solution)/shard_map/all_to_all | solution.py:485
  84.0 0.7 pad_maximum_fusion.4.mid_ref
  84.8 0.7 pad_maximum_fusion.low_ref
  85.5 0.1 fusion.4
  85.7 1.6 %copy-done.1 = f32[4104,128]{1,0:T(8,128)S(1)} copy-done((f32[4104,128]{1,0:T(8,128)S(1)}, f32[4104,128]{1,0:T(8,128)}, u32[]{:S(2)}) %copy-start.1) | copy-done | bytes 2101272
  87.3 1.6 %copy-done.3 = f32[4096,128]{1,0:T(8,128)S(1)} copy-done((f32[4096,128]{1,0:T(8,128)S(1)}, f32[4096,128]{1,0:T(8,128)}, u32[]{:S(2)}) %copy-start.3) | copy-done | bytes 2097176
  88.9 26.6 %leaf_b.1 = f32[64,512]{1,0:T(8,128)} custom-call(s32[16,4,128]{2,1,0:T(4,128)S(1)} %copy-done.8, f32[16,512,1024]{2,1,0:T(8,128)} %get-tuple-element.10.u_ref, bf16[64,2,8,1024]{3,2,1,0:T(8,128)(2,1)S(1)} %bitcast.59, f32[4096,128]{1,0:T(8,128)S(1)} %copy-done.3, f32[4104,128]{1,0:T(8,128)S(1)} %copy-done.1, f32[8,128]{1,0:T(8,128)S(1)} %get-tuple-element.13.occ_ref, ...), custom_call_target="tpu_custom_call" | custom-call | flops 6442450944 | bytes 25165824 | tf_op jit(solution)/shard_map/leaf_b/pallas_call | solution.py:349
  115.5 4.9 %finish.1 = bf16[256,1024]{1,0:T(8,128)(2,1)} custom-call(bf16[1024,640]{1,0:T(8,128)(2,1)} %bitcast.5.ret_ref, bf16[256,1024]{1,0:T(8,128)(2,1)} %feat_ref.3, s32[1,256]{1,0:T(1,128)} %bitcast.77, f32[16,128]{1,0:T(8,128)} %copy.55.up2_ref, f32[64,16]{1,0:T(8,128)} %bitcast.68, f32[64,64]{1,0:T(8,128)} %reshape.71.root_ref, ...), custom_call_target="tpu_custom_call" | custom-call | tf_op jit(solution)/shard_map/finish/pallas_call | solution.py:445
  (77 shorter events, 0.5 us)
Async XLA Ops:
  4.9 11.2 %copy-start.27 = (bf16[192,192]{1,0:T(8,128)(2,1)S(1)}, bf16[192,192]{1,0:T(8,128)(2,1)}, u32[]{:S(2)}) copy-start(bf16[192,192]{1,0:T(8,128)(2,1)} %param.25) | copy-start | bytes 221188
  4.9 12.8 %copy-start.24 = (bf16[256,256]{1,0:T(8,128)(2,1)S(1)}, bf16[256,256]{1,0:T(8,128)(2,1)}, u32[]{:S(2)}) copy-start(bf16[256,256]{1,0:T(8,128)(2,1)} %param.24) | copy-start | bytes 393220
  4.9 13.0 %copy-start.32 = (bf16[128,128]{1,0:T(8,128)(2,1)S(1)}, bf16[128,128]{1,0:T(8,128)(2,1)}, u32[]{:S(2)}) copy-start(bf16[128,128]{1,0:T(8,128)(2,1)} %param.26) | copy-start | bytes 98308
  4.9 41.5 %all-to-all-start = ((bf16[128,8,1024]{2,1,0:T(8,128)(2,1)}), bf16[128,8,1024]{2,1,0:T(8,128)(2,1)S(1)}, u32[]{:S(2)}, u32[]{:S(2)}) async-start(bf16[128,8,1024]{2,1,0:T(8,128)(2,1)} %bitcast.61), calls=%async_computation | async-start | bytes 4194304 | tf_op jit(solution)/shard_map/all_to_all | solution.py:485
  16.1 2.7 %copy-start.36 = (bf16[64,64]{1,0:T(8,128)(2,1)S(1)}, bf16[64,64]{1,0:T(8,128)(2,1)}, u32[]{:S(2)}) copy-start(bf16[64,64]{1,0:T(8,128)(2,1)} %param.27) | copy-start | bytes 24580
  16.1 4.2 %copy-start.18 = (f32[64,512]{1,0:T(8,128)S(1)}, f32[64,512]{1,0:T(8,128)}, u32[]{:S(2)}) copy-start(f32[64,512]{1,0:T(8,128)} %param.23) | copy-start | bytes 393220
  16.1 4.3 %copy-start.12 = (bf16[192,192]{1,0:T(8,128)(2,1)S(1)}, bf16[192,192]{1,0:T(8,128)(2,1)}, u32[]{:S(2)}) copy-start(bf16[192,192]{1,0:T(8,128)(2,1)} %param.29) | copy-start | bytes 221188
  16.1 5.1 %copy-start.20 = (bf16[128,128]{1,0:T(8,128)(2,1)S(1)}, bf16[128,128]{1,0:T(8,128)(2,1)}, u32[]{:S(2)}) copy-start(bf16[128,128]{1,0:T(8,128)(2,1)} %param.30) | copy-start | bytes 98308
  16.1 5.8 %copy-start.29 = (bf16[64,64]{1,0:T(8,128)(2,1)S(1)}, bf16[64,64]{1,0:T(8,128)(2,1)}, u32[]{:S(2)}) copy-start(bf16[64,64]{1,0:T(8,128)(2,1)} %param.31) | copy-start | bytes 24580
  16.1 6.5 %copy-start.4 = (bf16[256,256]{1,0:T(8,128)(2,1)S(1)}, bf16[256,256]{1,0:T(8,128)(2,1)}, u32[]{:S(2)}) copy-start(bf16[256,256]{1,0:T(8,128)(2,1)} %s0.1) | copy-start | bytes 393220
  16.1 6.5 %copy-start.17 = (f32[4,16,16]{2,1,0:T(8,128)S(1)}, f32[4,16,16]{2,1,0:T(8,128)}, u32[]{:S(2)}) copy-start(f32[4,16,16]{2,1,0:T(8,128)} %param.33) | copy-start | bytes 12292
  25.9 7.9 %copy-start.28 = (f32[4,4,16,16]{3,2,1,0:T(8,128)S(1)}, f32[4,4,16,16]{3,2,1,0:T(8,128)}, u32[]{:S(2)}) copy-start(f32[4,4,16,16]{3,2,1,0:T(8,128)} %param.35) | copy-start | bytes 49156
  25.9 9.2 %copy-start.21 = (bf16[128,128]{1,0:T(8,128)(2,1)S(1)}, bf16[128,128]{1,0:T(8,128)(2,1)}, u32[]{:S(2)}) copy-start(bf16[128,128]{1,0:T(8,128)(2,1)} %param.30) | copy-start | bytes 98308
  46.4 0.9 copy-start.5
  47.3 0.8 copy-start.9
  48.1 0.8 copy-start.10
  48.8 0.8 copy-start.11
  74.5 1.3 %copy-start = (f32[4104,128]{1,0:T(8,128)}, f32[4104,128]{1,0:T(8,128)S(1)}, u32[]{:S(2)}) copy-start(f32[4104,128]{1,0:T(8,128)S(1)} %get-tuple-element.12.table_ref) | copy-start | bytes 6303748
  75.8 1.4 %copy-start.2 = (f32[4096,128]{1,0:T(8,128)}, f32[4096,128]{1,0:T(8,128)S(1)}, u32[]{:S(2)}) copy-start(f32[4096,128]{1,0:T(8,128)S(1)} %get-tuple-element.11.own_ref) | copy-start | bytes 6291460
  77.2 0.6 copy-start.7
  77.8 6.2 %copy-start.33 = (f32[1,16,16]{2,1,0:T(8,128)S(1)}, f32[1,16,16]{2,1,0:T(8,128)}, u32[]{:S(2)}) copy-start(f32[1,16,16]{2,1,0:T(8,128)} %get-tuple-element.18) | copy-start | bytes 3076
  77.8 6.2 %copy-start.34 = (f32[1,16,16]{2,1,0:T(8,128)S(1)}, f32[1,16,16]{2,1,0:T(8,128)}, u32[]{:S(2)}) copy-start(f32[1,16,16]{2,1,0:T(8,128)} %get-tuple-element.26) | copy-start | bytes 3076
  77.8 6.2 %copy-start.35 = (f32[1,16,16]{2,1,0:T(8,128)S(1)}, f32[1,16,16]{2,1,0:T(8,128)}, u32[]{:S(2)}) copy-start(f32[1,16,16]{2,1,0:T(8,128)} %get-tuple-element.27) | copy-start | bytes 3076
  77.8 6.2 %copy-start.23 = (f32[4,16,16]{2,1,0:T(8,128)S(1)}, f32[4,16,16]{2,1,0:T(8,128)}, u32[]{:S(2)}) copy-start(f32[4,16,16]{2,1,0:T(8,128)} %copy.52) | copy-start | bytes 12292
  77.8 6.2 %copy-start.25 = (f32[4,16,16]{2,1,0:T(8,128)S(1)}, f32[4,16,16]{2,1,0:T(8,128)}, u32[]{:S(2)}) copy-start(f32[4,16,16]{2,1,0:T(8,128)} %get-tuple-element.46) | copy-start | bytes 12292
  77.8 6.2 %copy-start.26 = (f32[4,16,16]{2,1,0:T(8,128)S(1)}, f32[4,16,16]{2,1,0:T(8,128)}, u32[]{:S(2)}) copy-start(f32[4,16,16]{2,1,0:T(8,128)} %get-tuple-element.47) | copy-start | bytes 12292
  77.8 6.9 %copy-start.30 = (bf16[64,64]{1,0:T(8,128)(2,1)S(1)}, bf16[64,64]{1,0:T(8,128)(2,1)}, u32[]{:S(2)}) copy-start(bf16[64,64]{1,0:T(8,128)(2,1)} %get-tuple-element.40) | copy-start | bytes 24580
  77.8 6.9 %copy-start.31 = (bf16[64,64]{0,1:T(8,128)(2,1)S(1)}, bf16[64,64]{0,1:T(8,128)(2,1)}, u32[]{:S(2)}) copy-start(bf16[64,64]{0,1:T(8,128)(2,1)} %copy.59) | copy-start | bytes 24580
  77.8 7.0 %copy-start.15 = (f32[128,128]{1,0:T(8,128)S(1)}, f32[128,128]{1,0:T(8,128)}, u32[]{:S(2)}) copy-start(f32[128,128]{1,0:T(8,128)} %reshape.76) | copy-start | bytes 196612
  77.9 7.0 %copy-start.16 = (f32[16,8,16]{2,1,0:T(8,128)S(1)}, f32[16,8,16]{2,1,0:T(8,128)}, u32[]{:S(2)}) copy-start(f32[16,8,16]{2,1,0:T(8,128)} %copy.54) | copy-start | bytes 24580
  77.9 7.6 %copy-start.19 = (bf16[128,128]{1,0:T(8,128)(2,1)S(1)}, bf16[128,128]{1,0:T(8,128)(2,1)}, u32[]{:S(2)}) copy-start(bf16[128,128]{1,0:T(8,128)(2,1)} %get-tuple-element.38) | copy-start | bytes 98308
  77.9 7.6 %copy-start.22 = (bf16[128,128]{0,1:T(8,128)(2,1)S(1)}, bf16[128,128]{0,1:T(8,128)(2,1)}, u32[]{:S(2)}) copy-start(bf16[128,128]{0,1:T(8,128)(2,1)} %copy.58) | copy-start | bytes 98308
  77.9 7.7 %copy-start.13 = (bf16[192,192]{0,1:T(8,128)(2,1)S(1)}, bf16[192,192]{0,1:T(8,128)(2,1)}, u32[]{:S(2)}) copy-start(bf16[192,192]{0,1:T(8,128)(2,1)} %copy.57) | copy-start | bytes 221188
  77.9 7.7 %copy-start.14 = (bf16[192,192]{1,0:T(8,128)(2,1)S(1)}, bf16[192,192]{1,0:T(8,128)(2,1)}, u32[]{:S(2)}) copy-start(bf16[192,192]{1,0:T(8,128)(2,1)} %get-tuple-element.32) | copy-start | bytes 221188
  77.9 7.8 %copy-start.6 = (bf16[256,128]{1,0:T(8,128)(2,1)S(1)}, bf16[256,128]{1,0:T(8,128)(2,1)}, u32[]{:S(2)}) copy-start(bf16[256,128]{1,0:T(8,128)(2,1)} %constant.4.clone.sum_ref) | copy-start | bytes 196612
  77.9 7.8 %copy-start.8 = (s32[16,4,128]{2,1,0:T(4,128)S(1)}, s32[16,4,128]{2,1,0:T(4,128)}, u32[]{:S(2)}) copy-start(s32[16,4,128]{2,1,0:T(4,128)} %copy-done.7) | copy-start | bytes 98308
  77.9 37.6 %all-to-all-start.1 = ((bf16[128,8,640]{2,1,0:T(8,128)(2,1)}), bf16[128,8,640]{2,1,0:T(8,128)(2,1)}, u32[]{:S(2)}, u32[]{:S(2)}) async-start(bf16[128,8,640]{2,1,0:T(8,128)(2,1)} %bitcast.4), calls=%async_computation.1 | async-start | bytes 2621440 | tf_op jit(solution)/shard_map/all_to_all | solution.py:485
  85.7 1.6 %copy-start.1 = (f32[4104,128]{1,0:T(8,128)S(1)}, f32[4104,128]{1,0:T(8,128)}, u32[]{:S(2)}) copy-start(f32[4104,128]{1,0:T(8,128)} %copy-done) | copy-start | bytes 6303748
  87.3 1.6 %copy-start.3 = (f32[4096,128]{1,0:T(8,128)S(1)}, f32[4096,128]{1,0:T(8,128)}, u32[]{:S(2)}) copy-start(f32[4096,128]{1,0:T(8,128)} %copy-done.2) | copy-start | bytes 6291460

commit v4 on v3

--- a/solution.py
+++ b/solution.py
@@ -91,7 +91,7 @@
         for which in range(2):
             start = pl.multiple_of(index[which][i >> 7, i & 127], 8)
             row = own + table_ref[pl.ds(start, 8), :]
-            out_ref[(which * TILE + j) >> 3, pl.ds(j & 7, 8, stride=8), :] = row
+            out_ref[0, part, (which * TILE + j) >> 3, pl.ds(j & 7, 8, stride=8), :] = row
 
 
 def both(a, b):
@@ -127,23 +127,21 @@
 
 
 def leaf_a_kernel(
-    got_ref,
+    got_hbm,
     nbr_ref,
     rad_ref,
     f0, f1a, f1b, f2, f3,
     s0, s1a, s1b, s2, s3,
     u_ref,
+    y_ref,
     back_ref,
+    occ_ref,
+    got_ref,
     own_ref,
     table_ref,
     index_ref,
-    occ_ref,
     acc_ref,
     tile_ref,
-    buf0,
-    buf1,
-    buf2,
-    buf3,
     rank_ref,
     rank_smem,
     index_smem,
@@ -154,6 +152,7 @@
 
     @pl.when(step == 0)
     def _():
+        pltpu.sync_copy(got_hbm, got_ref)
         first = jnp.where(iota((8, 128), 1) == 0, 1.0, 0.0).astype(BF16)
         got0 = got_ref[:, :, :, 0:128].reshape(1024, 128)
         lead = lax.dot_general(first, got0, (((1,), (1,)), ((), ())), preferred_element_type=F32)
@@ -194,25 +193,24 @@
             to = pl.multiple_of(rank_smem[s >> 7, s & 127], 8)
             table_ref[pl.ds(to, 8), :] = own_ref[i * 8 : (i + 1) * 8, :]
         index_to_smem.wait()
-        gather(index_smem, 0, 0, own_ref, table_ref, buf0)
-
-    bufs = (buf0, buf1, buf2, buf3)
+
+    gather(index_smem, step, 0, own_ref, table_ref, y_ref)
     for turn in range(4):
-        after = jnp.minimum(step + (turn + 1) // 4, NBR // 2 - 1)
-        gather(index_smem, after, (turn + 1) % 4, own_ref, table_ref, bufs[(turn + 1) % 4])
+        if turn < 3:
+            gather(index_smem, step, turn + 1, own_ref, table_ref, y_ref)
         rows = pl.ds(turn * TILE, TILE)
         pats = scales(rad_ref, rows, step)
 
         def piece(g):
-            y = bufs[turn][:, g * 8 : (g + 1) * 8, :].reshape(2 * TILE, 128)
+            y = y_ref[0, turn, :, g * 8 : (g + 1) * 8, :].reshape(2 * TILE, 128)
             return (y * pats[g]).astype(BF16)
 
         def use(g, w):
             cols = slice(g * 128, (g + 1) * 128)
             v = w + w * jnp.tanh(w)
             acc_ref[rows, cols] += v[:TILE] + v[TILE:]
-            u_ref[0, rows, cols] = w[:TILE]
-            u_ref[1, rows, cols] = w[TILE:]
+            u_ref[0, rows, cols] = w[:TILE].astype(BF16)
+            u_ref[1, rows, cols] = w[TILE:].astype(BF16)
 
         mix_blocks(piece, f0, f1a, f1b, f2, f3, use)
 
@@ -237,53 +235,63 @@
         back_ref[:, :, :, 512:] = body
 
 
-WHOLE = pl.BlockSpec(memory_space=pltpu.VMEM)
+def full(x):
+    return pl.BlockSpec(x.shape, lambda k, n=len(x.shape): (0,) * n)
+
+
+HBM = pl.BlockSpec(memory_space=pltpu.HBM)
+Y_BLOCK = (1, 4, TILE // 4, 64, 128)
 
 
 def leaf_a(got, nbr, rad, firsts, seconds):
-    args = (got, nbr, rad, *firsts, *seconds)
+    args = (nbr, rad, *firsts, *seconds)
     out_shape = [
-        jax.ShapeDtypeStruct((NBR, POOL, WIDTH), F32),
+        jax.ShapeDtypeStruct((NBR, POOL, WIDTH), BF16),
+        jax.ShapeDtypeStruct((NBR // 2,) + Y_BLOCK[1:], F32),
         jax.ShapeDtypeStruct((64, 2, 8, 640), BF16),
-        jax.ShapeDtypeStruct((POOL * 8, 128), F32),
-        jax.ShapeDtypeStruct((POOL * 8 + 8, 128), F32),
-        jax.ShapeDtypeStruct((NBR, 4, 128), jnp.int32),
         jax.ShapeDtypeStruct((8, 128), F32),
     ]
     return pl.pallas_call(
         leaf_a_kernel,
         grid=(NBR // 2,),
-        in_specs=[WHOLE] * len(args),
-        out_specs=[pl.BlockSpec((2, POOL, WIDTH), lambda k: (k, 0, 0))] + [WHOLE] * (len(out_shape) - 1),
+        in_specs=[HBM] + [full(x) for x in args],
+        out_specs=[
+            pl.BlockSpec((2, POOL, WIDTH), lambda k: (k, 0, 0)),
+            pl.BlockSpec(Y_BLOCK, lambda k: (k, 0, 0, 0, 0)),
+            full(out_shape[2]),
+            full(out_shape[3]),
+        ],
         out_shape=out_shape,
         scratch_shapes=[
+            pltpu.VMEM((64, 2, 8, WIDTH), BF16),
+            pltpu.VMEM((POOL * 8, 128), F32),
+            pltpu.VMEM((POOL * 8 + 8, 128), F32),
+            pltpu.VMEM((NBR, 4, 128), jnp.int32),
             pltpu.VMEM((POOL, WIDTH), F32),
             pltpu.VMEM((8, WIDTH), F32),
-        ]
-        + [pltpu.VMEM((TILE // 4, 64, 128), F32)] * 4
-        + [
             pltpu.VMEM((8, 128), jnp.int32),
             pltpu.SMEM((8, 128), jnp.int32),
             pltpu.SMEM((NBR, 4, 128), jnp.int32),
             pltpu.SemaphoreType.DMA,
             pltpu.SemaphoreType.DMA,
         ],
-        compiler_params=pltpu.CompilerParams(vmem_limit_bytes=40 << 20),
-        cost_estimate=pl.CostEstimate(flops=6 << 30, bytes_accessed=24 << 20, transcendentals=8 << 20),
+        compiler_params=pltpu.CompilerParams(vmem_limit_bytes=56 << 20),
+        cost_estimate=pl.CostEstimate(flops=6 << 30, bytes_accessed=50 << 20, transcendentals=8 << 20),
         name="leaf_a",
-    )(*args)
+    )(got, *args)
 
 
 def leaf_b_kernel(
-    index_ref, u_ref, got_ref, own_ref, table_ref, occ_ref,
+    u_ref, y_ref, got_hbm, occ_ref,
     t0, t1a, t1b, t2, t3,
     s0, s1a, s1b, s2, s3,
-    sum_ref, out_ref, acc_ref, half_t_ref, buf0, buf1, buf2, buf3,
+    sum_ref, out_ref, acc_ref, half_t_ref, got_ref,
 ):
     step = pl.program_id(0)
 
     @pl.when(step == 0)
     def _():
+        pltpu.sync_copy(got_hbm, got_ref)
         acc_ref[...] = jnp.zeros_like(acc_ref)
         top = iota((8, WIDTH), 0) < 4
         for part in range(POOL // TILE):
@@ -298,12 +306,8 @@
                 half_t_ref[rows, g * 128 : (g + 1) * 128] = 0.5 * value
 
             mix_blocks(lambda g: grad[:, g * 128 : (g + 1) * 128], s0, s1a, s1b, s2, s3, use)
-        gather(index_ref, 0, 0, own_ref, table_ref, buf0)
-
-    bufs = (buf0, buf1, buf2, buf3)
+
     for turn in range(4):
-        after = jnp.minimum(step + (turn + 1) // 4, NBR // 2 - 1)
-        gather(index_ref, after, (turn + 1) % 4, own_ref, table_ref, bufs[(turn + 1) % 4])
         rows = pl.ds(turn * TILE, TILE)
         prods = {}
 
@@ -312,14 +316,14 @@
             half_t = half_t_ref[rows, cols]
             out = []
             for which in range(2):
-                w = u_ref[which, rows, cols]
+                w = u_ref[which, rows, cols].astype(F32)
                 h = jnp.tanh(w)
                 up = 1.0 + h
                 out.append(((up + (w * up) * (1.0 - h)) * half_t).astype(BF16))
             return both(*out)
 
         def use(g, s):
-            prods[g] = s * bufs[turn][:, g * 8 : (g + 1) * 8, :].reshape(2 * TILE, 128)
+            prods[g] = s * y_ref[0, turn, :, g * 8 : (g + 1) * 8, :].reshape(2 * TILE, 128)
 
         mix_blocks(piece, t0, t1a, t1b, t2, t3, use)
         low = iota((2 * TILE, 128), 1) < 64
@@ -344,27 +348,28 @@
         out_ref[...] = 0.5 * occ * jnp.transpose(acc_ref[...])[0:64, :]
 
 
-def leaf_b(index, u, got, own, table, occ, trans, seconds_t, sums):
-    args = (got, own, table, occ, *trans, *seconds_t, sums)
+def leaf_b(u, y, got, occ, firsts_t, seconds_t, sums):
+    args = (occ, *firsts_t, *seconds_t, sums)
     return pl.pallas_call(
         leaf_b_kernel,
         grid=(NBR // 2,),
         in_specs=[
-            pl.BlockSpec(memory_space=pltpu.SMEM),
             pl.BlockSpec((2, POOL, WIDTH), lambda k: (k, 0, 0)),
+            pl.BlockSpec(Y_BLOCK, lambda k: (k, 0, 0, 0, 0)),
+            HBM,
         ]
-        + [WHOLE] * len(args),
+        + [full(x) for x in args],
         out_specs=pl.BlockSpec((64, POOL), lambda k: (0, 0)),
         out_shape=jax.ShapeDtypeStruct((64, POOL), F32),
         scratch_shapes=[
             pltpu.VMEM((POOL, 128), F32),
             pltpu.VMEM((POOL, WIDTH), F32),
-        ]
-        + [pltpu.VMEM((TILE // 4, 64, 128), F32)] * 4,
-        compiler_params=pltpu.CompilerParams(vmem_limit_bytes=32 << 20),
-        cost_estimate=pl.CostEstimate(flops=6 << 30, bytes_accessed=24 << 20, transcendentals=8 << 20),
+            pltpu.VMEM((64, 2, 8, WIDTH), BF16),
+        ],
+        compiler_params=pltpu.CompilerParams(vmem_limit_bytes=56 << 20),
+        cost_estimate=pl.CostEstimate(flops=6 << 30, bytes_accessed=50 << 20, transcendentals=8 << 20),
         name="leaf_b",
-    )(index, u, *args)
+    )(u, y, got, *args)
 
 
 def block_swap(tiles):
@@ -512,12 +517,12 @@
     firsts = (first_zero, first_one, first_two, first_three)
     seconds = (second_zero, second_one, second_two, second_three)
     got = got.reshape(64, 2, 8, WIDTH)
-    u, back, own, table, index, occ = leaf_a(
+    u, y, back, occ = leaf_a(
         got, neighbours, rad, blocks(firsts, 0.5, False), blocks(seconds, 1.0, False)
     )
     ret = swap(back.reshape(128, 8, 640))
     grads = leaf_b(
-        index, u, got, own, table, occ, blocks(firsts, 0.5, True), blocks(seconds, 1.0, True), degree_table()
+        u, y, got, occ, blocks(firsts, 0.5, True), blocks(seconds, 1.0, True), degree_table()
     )
     mats = tree_mats(lift_leaf, lift_branch, couple_root, couple_branch, couple_leaf)
     updated = finish(ret.reshape(1024, 640), features, leaf_row, mats)

time: 121 us -> 118 us (0.975)
  local copies, waits for them, and re-layouts: 25 us -> 17.6 us
  Pallas kernels: 60.7 us -> 63.7 us
  other arithmetic: 6.97 us -> 8.18 us
    unnamed x84 -> x46, local copies, waits for them, and re-layouts: 13.3 us -> 6.42 us
    pallas_call x2, Pallas kernels: 51.5 us -> 54.5 us  [the longest x1 28.5 us: leaf_a(): pl.pallas_call(leaf_a_kernel, grid=(NBR // 2,), in_specs=[HBM] + [full(x)...]
    add x3, other arithmetic: 0.05 us -> 1.42 us  [blocks(): w2 = jnp.pad(m2, ((0, 128), (0, 128))) + jnp.pad(m2, ((128, 0), (128, 0)))]
    reshape x1, local copies, waits for them, and re-layouts: 2.29 us -> 1.08 us  [tree_mats(): low = (couple_leaf * keep8).transpose(2, 0, 3, 1).reshape(128, 128)]
  transfers between devices with their start and end apart: 2 -> 2, of which waited for: 1 -> 1; matrix products, arithmetic and copies ran while one was open for 18% -> 20% of each run, Pallas kernels for 22% -> 22%
where the time goes in v4:
time: 118 us; the launch traced here: 117 us
  Pallas kernels  63.7 us (54%)
  local copies, waits for them, and re-layouts  17.6 us (15%)
  starting transfers between devices  16.1 us (14%)
  waiting for transfers between devices  10.4 us (9%)
  other arithmetic  8.18 us (7%)
    pallas_call x1, Pallas kernels, leaf_a(): pl.pallas_call(leaf_a_kernel, grid=(NBR // 2,), in_specs=[HBM] + [full(x)...  28.5 us
    pallas_call x1, Pallas kernels, leaf_b(): pl.pallas_call(leaf_b_kernel, grid=(NBR // 2,), in_specs=[pl.BlockSpec((2...  26 us
    all_to_all x2, starting transfers between devices, swap(): return lax.all_to_all(x, AXES, split_axis=0, concat_axis=0, tiled=True)  16.1 us
    all_to_all x2, waiting for transfers between devices, swap(): return lax.all_to_all(x, AXES, split_axis=0, concat_axis=0, tiled=True)  10.4 us
    unnamed x46, local copies, waits for them, and re-layouts  6.42 us
    pallas_call x1, Pallas kernels, finish(): pl.pallas_call(finish_kernel, out_shape=jax.ShapeDtypeStruct((ROWS, WIDTH...  4.96 us
    pallas_call x1, Pallas kernels, pack(): pl.pallas_call(pack_kernel, out_shape=jax.ShapeDtypeStruct((128 * 8, WIDT...  4.26 us
  transfers between devices with their start and end apart: 2, of which 1 were waited for; matrix products, arithmetic and copies ran while one was open for 20% of the time, Pallas kernels for 22%

profile of v4, /device:TPU:0, one launch (start us, length us, event | category | flops | bytes accessed | tf_op | source)
XLA Modules:
  0.0 117.0 jit_solution(12519023612439338586)
XLA Ops:
  0.6 4.3 %pack.1 = bf16[1024,1024]{1,0:T(8,128)(2,1)} custom-call(s32[1,256]{1,0:T(1,128)} %bitcast.78, bf16[256,1024]{1,0:T(8,128)(2,1)} %feat_ref.3, bf16[256,1024]{1,0:T(8,128)(2,1)} %grad_ref.1), custom_call_target="tpu_custom_call" | custom-call | tf_op jit(solution)/shard_map/pack/pallas_call | solution.py:61
  4.9 11.2 %all-to-all-start = ((bf16[128,8,1024]{2,1,0:T(8,128)(2,1)}), bf16[128,8,1024]{2,1,0:T(8,128)(2,1)S(1)}, u32[]{:S(2)}, u32[]{:S(2)}) async-start(bf16[128,8,1024]{2,1,0:T(8,128)(2,1)} %bitcast.58), calls=%async_computation | async-start | bytes 4194304 | tf_op jit(solution)/shard_map/all_to_all | solution.py:490
  16.1 0.0 copy-start.17
  16.1 0.0 copy-start.8
  16.1 0.0 copy-start.2
  16.1 0.7 copy.52
  16.8 0.1 copy.42
  16.9 0.7 fusion.2
  17.6 0.7 copy.60
  18.3 0.1 copy.41
  18.4 0.7 fusion.3
  19.1 0.8 copy.45.f0
  19.9 0.1 copy.43
  20.0 0.8 copy.48.f2
  20.8 0.1 copy.44
  20.9 0.6 fusion
  21.5 0.1 pad_add_fusion.7
  21.6 0.7 copy.49.f3
  22.3 0.1 copy.40
  22.5 0.9 multiply_bitcast_fusion
  23.4 1.4 %copy.53 = f32[16,8,16,8]{3,2,1,0:T(8,128)S(1)} copy(f32[16,8,16,8]{2,0,3,1:T(8,128)} %multiply_bitcast_fusion) | data formatting | bytes 131072 | tf_op jit(solution)/shard_map/transpose | solution.py:477
  24.8 1.1 reshape.76
  25.9 1.0 copy.54
  26.9 1.0 multiply_bitcast_fusion.1
  27.9 0.1 copy.51
  28.0 0.7 reshape.71.root_ref
  28.7 0.9 copy.50
  29.6 0.7 copy.55.up2_ref
  30.3 0.1 copy.57
  30.4 0.9 copy.58
  31.3 0.1 copy.59
  31.4 1.7 %copy.56 = bf16[256,256]{0,1:T(8,128)(2,1)} copy(bf16[256,256]{1,0:T(8,128)(2,1)} %s0.1) | data formatting | bytes 262144 | tf_op args[9]
  33.0 0.7 pad.82.rad_ref
  33.8 0.7 pad_add_fusion.6.s3
  34.5 0.7 pad_add_fusion.2.s2
  35.2 0.9 fusion.6
  36.0 10.4 %all-to-all-done = bf16[128,8,1024]{2,1,0:T(8,128)(2,1)S(1)} async-done(((bf16[128,8,1024]{2,1,0:T(8,128)(2,1)}), bf16[128,8,1024]{2,1,0:T(8,128)(2,1)S(1)}, u32[]{:S(2)}, u32[]{:S(2)}) %all-to-all-start) | async-done | bytes 2097184 | tf_op jit(solution)/shard_map/all_to_all | solution.py:490
  46.4 1.3 %copy-done = bf16[128,8,1024]{2,1,0:T(8,128)(2,1)} copy-done((bf16[128,8,1024]{2,1,0:T(8,128)(2,1)}, bf16[128,8,1024]{2,1,0:T(8,128)(2,1)S(1)}, u32[]{:S(2)}) %copy-start) | copy-done | bytes 2097176
  47.7 28.5 %leaf_a.1 = (bf16[16,512,1024]{2,1,0:T(8,128)(2,1)}, f32[8,4,32,64,128]{4,3,2,1,0:T(8,128)}, bf16[64,2,8,640]{3,2,1,0:T(8,128)(2,1)}, f32[8,128]{1,0:T(8,128)}) custom-call(bf16[64,2,8,1024]{3,2,1,0:T(8,128)(2,1)} %bitcast.59, s32[16,512]{1,0:T(8,128)} %nbr_ref.1, f32[512,128]{1,0:T(8,128)} %pad.82.rad_ref, bf16[256,256]{1,0:T(8,128)(2,1)} %copy.45.f0, ...), custom_call_target="tpu_custom_call" | custom-call | flops 6442450944 | bytes 52428800 | tf_op jit(solution)/shard_map/leaf_a/pallas_call | solution.py:254
  76.3 5.0 %all-to-all-start.1 = ((bf16[128,8,640]{2,1,0:T(8,128)(2,1)}), bf16[128,8,640]{2,1,0:T(8,128)(2,1)S(1)}, u32[]{:S(2)}, u32[]{:S(2)}) async-start(bf16[128,8,640]{2,1,0:T(8,128)(2,1)} %bitcast.62), calls=%async_computation.1 | async-start | bytes 2621440 | tf_op jit(solution)/shard_map/all_to_all | solution.py:490
  81.3 0.7 pad_maximum_fusion.4.mid_ref
  82.0 0.7 pad_add_fusion.4
  82.7 0.7 pad_maximum_fusion.low_ref
  83.4 0.7 pad_add_fusion
  84.1 0.8 fusion.4
  84.9 26.0 %leaf_b.1 = f32[64,512]{1,0:T(8,128)} custom-call(bf16[16,512,1024]{2,1,0:T(8,128)(2,1)} %get-tuple-element.7.u_ref, f32[8,4,32,64,128]{4,3,2,1,0:T(8,128)} %get-tuple-element.8.y_ref, bf16[64,2,8,1024]{3,2,1,0:T(8,128)(2,1)} %bitcast.60, f32[8,128]{1,0:T(8,128)} %get-tuple-element.9.occ_ref, bf16[256,256]{1,0:T(8,128)(2,1)} %get-tuple-element.10.t0, ...), custom_call_target="tpu_custom_call" | custom-call | flops 6442450944 | bytes 52428800 | tf_op jit(solution)/shard_map/leaf_b/pallas_call | solution.py:353
  111.0 1.1 copy-done.1
  112.1 5.0 %finish.1 = bf16[256,1024]{1,0:T(8,128)(2,1)} custom-call(bf16[1024,640]{1,0:T(8,128)(2,1)} %bitcast.61, bf16[256,1024]{1,0:T(8,128)(2,1)} %feat_ref.3, s32[1,256]{1,0:T(1,128)} %bitcast.79, f32[16,128]{1,0:T(8,128)} %copy.55.up2_ref, f32[64,16]{1,0:T(8,128)} %bitcast.70, f32[64,64]{1,0:T(8,128)} %reshape.71.root_ref, f32[64,64]{1,0:T(8,128)} %pad_maximum_fusion.4.mid_ref, ...), custom_call_target="tpu_custom_call" | custom-call | tf_op jit(solution)/shard_map/finish/pallas_call | solution.py:450
  (39 shorter events, 0.1 us)
Async XLA Ops:
  4.9 11.2 %copy-start.7 = (f32[4,16,16]{2,1,0:T(8,128)S(1)}, f32[4,16,16]{2,1,0:T(8,128)}, u32[]{:S(2)}) copy-start(f32[4,16,16]{2,1,0:T(8,128)} %param.33) | copy-start | bytes 12292
  4.9 11.9 %copy-start.12 = (bf16[192,192]{1,0:T(8,128)(2,1)S(1)}, bf16[192,192]{1,0:T(8,128)(2,1)}, u32[]{:S(2)}) copy-start(bf16[192,192]{1,0:T(8,128)(2,1)} %param.25) | copy-start | bytes 221188
  4.9 13.4 %copy-start.11 = (bf16[256,256]{1,0:T(8,128)(2,1)S(1)}, bf16[256,256]{1,0:T(8,128)(2,1)}, u32[]{:S(2)}) copy-start(bf16[256,256]{1,0:T(8,128)(2,1)} %param.24) | copy-start | bytes 393220
  4.9 15.0 %copy-start.16 = (bf16[128,128]{1,0:T(8,128)(2,1)S(1)}, bf16[128,128]{1,0:T(8,128)(2,1)}, u32[]{:S(2)}) copy-start(bf16[128,128]{1,0:T(8,128)(2,1)} %param.26) | copy-start | bytes 98308
  4.9 41.5 %all-to-all-start = ((bf16[128,8,1024]{2,1,0:T(8,128)(2,1)}), bf16[128,8,1024]{2,1,0:T(8,128)(2,1)S(1)}, u32[]{:S(2)}, u32[]{:S(2)}) async-start(bf16[128,8,1024]{2,1,0:T(8,128)(2,1)} %bitcast.58), calls=%async_computation | async-start | bytes 4194304 | tf_op jit(solution)/shard_map/all_to_all | solution.py:490
  16.1 4.7 %copy-start.17 = (bf16[64,64]{1,0:T(8,128)(2,1)S(1)}, bf16[64,64]{1,0:T(8,128)(2,1)}, u32[]{:S(2)}) copy-start(bf16[64,64]{1,0:T(8,128)(2,1)} %param.27) | copy-start | bytes 24580
  16.1 6.2 %copy-start.8 = (f32[64,512]{1,0:T(8,128)S(1)}, f32[64,512]{1,0:T(8,128)}, u32[]{:S(2)}) copy-start(f32[64,512]{1,0:T(8,128)} %param.23) | copy-start | bytes 393220
  16.1 6.4 %copy-start.2 = (f32[8,8,16,16]{3,2,1,0:T(8,128)S(1)}, f32[8,8,16,16]{3,2,1,0:T(8,128)}, u32[]{:S(2)}) copy-start(f32[8,8,16,16]{3,2,1,0:T(8,128)} %param.36) | copy-start | bytes 196612
  23.4 6.9 %copy-start.3 = (bf16[192,192]{1,0:T(8,128)(2,1)S(1)}, bf16[192,192]{1,0:T(8,128)(2,1)}, u32[]{:S(2)}) copy-start(bf16[192,192]{1,0:T(8,128)(2,1)} %param.29) | copy-start | bytes 221188
  23.4 7.9 %copy-start.14 = (bf16[64,64]{1,0:T(8,128)(2,1)S(1)}, bf16[64,64]{1,0:T(8,128)(2,1)}, u32[]{:S(2)}) copy-start(bf16[64,64]{1,0:T(8,128)(2,1)} %param.31) | copy-start | bytes 24580
  25.9 8.5 %copy-start.13 = (f32[4,4,16,16]{3,2,1,0:T(8,128)S(1)}, f32[4,4,16,16]{3,2,1,0:T(8,128)}, u32[]{:S(2)}) copy-start(f32[4,4,16,16]{3,2,1,0:T(8,128)} %param.35) | copy-start | bytes 49156
  25.9 8.6 %copy-start.9 = (bf16[128,128]{1,0:T(8,128)(2,1)S(1)}, bf16[128,128]{1,0:T(8,128)(2,1)}, u32[]{:S(2)}) copy-start(bf16[128,128]{1,0:T(8,128)(2,1)} %param.30) | copy-start | bytes 98308
  25.9 9.2 %copy-start.4 = (bf16[192,192]{1,0:T(8,128)(2,1)S(1)}, bf16[192,192]{1,0:T(8,128)(2,1)}, u32[]{:S(2)}) copy-start(bf16[192,192]{1,0:T(8,128)(2,1)} %copy.60) | copy-start | bytes 221188
  46.4 1.3 %copy-start = (bf16[128,8,1024]{2,1,0:T(8,128)(2,1)}, bf16[128,8,1024]{2,1,0:T(8,128)(2,1)S(1)}, u32[]{:S(2)}) copy-start(bf16[128,8,1024]{2,1,0:T(8,128)(2,1)S(1)} %all-to-all-done) | copy-start | bytes 6291460
  76.2 5.0 %copy-start.10 = (f32[4,16,16]{2,1,0:T(8,128)S(1)}, f32[4,16,16]{2,1,0:T(8,128)}, u32[]{:S(2)}) copy-start(f32[4,16,16]{2,1,0:T(8,128)} %copy.52) | copy-start | bytes 12292
  76.2 5.7 %copy-start.15 = (bf16[64,64]{1,0:T(8,128)(2,1)S(1)}, bf16[64,64]{1,0:T(8,128)(2,1)}, u32[]{:S(2)}) copy-start(bf16[64,64]{1,0:T(8,128)(2,1)} %get-tuple-element.36) | copy-start | bytes 24580
  76.3 6.4 %copy-start.6 = (f32[128,128]{1,0:T(8,128)S(1)}, f32[128,128]{1,0:T(8,128)}, u32[]{:S(2)}) copy-start(f32[128,128]{1,0:T(8,128)} %reshape.76) | copy-start | bytes 196612
  76.3 7.8 %copy-start.5 = (bf16[192,192]{1,0:T(8,128)(2,1)S(1)}, bf16[192,192]{1,0:T(8,128)(2,1)}, u32[]{:S(2)}) copy-start(bf16[192,192]{1,0:T(8,128)(2,1)} %get-tuple-element.28) | copy-start | bytes 221188
  76.3 34.7 %all-to-all-start.1 = ((bf16[128,8,640]{2,1,0:T(8,128)(2,1)}), bf16[128,8,640]{2,1,0:T(8,128)(2,1)S(1)}, u32[]{:S(2)}, u32[]{:S(2)}) async-start(bf16[128,8,640]{2,1,0:T(8,128)(2,1)} %bitcast.62), calls=%async_computation.1 | async-start | bytes 2621440 | tf_op jit(solution)/shard_map/all_to_all | solution.py:490
  111.0 1.1 copy-start.1

commit v5 on v4

--- a/solution.py
+++ b/solution.py
@@ -91,7 +91,7 @@
         for which in range(2):
             start = pl.multiple_of(index[which][i >> 7, i & 127], 8)
             row = own + table_ref[pl.ds(start, 8), :]
-            out_ref[0, part, (which * TILE + j) >> 3, pl.ds(j & 7, 8, stride=8), :] = row
+            out_ref[(which * TILE + j) >> 3, pl.ds(j & 7, 8, stride=8), :] = row
 
 
 def both(a, b):
@@ -110,24 +110,28 @@
     return [p01, p23, p12, p31, p23, p23, p23, r3]
 
 
-def mix_blocks(piece, w0, w1a, w1b, w2, w3, use):
-    out = dot(jnp.concatenate([piece(0), piece(1)], axis=1), w0[...])
+def mix_blocks(piece, w0, w1a, w1b, w2, w3, use, flip=False):
+    def times(x, w):
+        dims = (((1,), (1 if flip else 0,)), ((), ()))
+        return lax.dot_general(x, w[...], dims, preferred_element_type=F32)
+
+    out = times(jnp.concatenate([piece(0), piece(1)], axis=1), w0)
     use(0, out[:, :128])
     use(1, out[:, 128:])
     middle = piece(3)
-    a = dot(jnp.concatenate([piece(2), middle], axis=1), w1a[...])
-    b = dot(jnp.concatenate([middle, piece(4)], axis=1), w1b[...])
+    a = times(jnp.concatenate([piece(2), middle], axis=1), w1a)
+    b = times(jnp.concatenate([middle, piece(4)], axis=1), w1b)
     use(2, a[:, :128])
     use(3, a[:, 128:] + b[:, :128])
     use(4, b[:, 128:])
-    out = dot(jnp.concatenate([piece(5), piece(6)], axis=1), w2[...])
+    out = times(jnp.concatenate([piece(5), piece(6)], axis=1), w2)
     use(5, out[:, :128])
     use(6, out[:, 128:])
-    use(7, dot(piece(7), w3[...]))
+    use(7, times(piece(7), w3))
 
 
 def leaf_a_kernel(
-    got_hbm,
+    got_ref,
     nbr_ref,
     rad_ref,
     f0, f1a, f1b, f2, f3,
@@ -136,12 +140,15 @@
     y_ref,
     back_ref,
     occ_ref,
-    got_ref,
     own_ref,
     table_ref,
     index_ref,
     acc_ref,
     tile_ref,
+    buf0,
+    buf1,
+    buf2,
+    buf3,
     rank_ref,
     rank_smem,
     index_smem,
@@ -152,7 +159,6 @@
 
     @pl.when(step == 0)
     def _():
-        pltpu.sync_copy(got_hbm, got_ref)
         first = jnp.where(iota((8, 128), 1) == 0, 1.0, 0.0).astype(BF16)
         got0 = got_ref[:, :, :, 0:128].reshape(1024, 128)
         lead = lax.dot_general(first, got0, (((1,), (1,)), ((), ())), preferred_element_type=F32)
@@ -193,17 +199,19 @@
             to = pl.multiple_of(rank_smem[s >> 7, s & 127], 8)
             table_ref[pl.ds(to, 8), :] = own_ref[i * 8 : (i + 1) * 8, :]
         index_to_smem.wait()
-
-    gather(index_smem, step, 0, own_ref, table_ref, y_ref)
+        gather(index_smem, 0, 0, own_ref, table_ref, buf0)
+
+    bufs = (buf0, buf1, buf2, buf3)
     for turn in range(4):
-        if turn < 3:
-            gather(index_smem, step, turn + 1, own_ref, table_ref, y_ref)
+        after = jnp.minimum(step + (turn + 1) // 4, NBR // 2 - 1)
+        gather(index_smem, after, (turn + 1) % 4, own_ref, table_ref, bufs[(turn + 1) % 4])
         rows = pl.ds(turn * TILE, TILE)
         pats = scales(rad_ref, rows, step)
 
         def piece(g):
-            y = y_ref[0, turn, :, g * 8 : (g + 1) * 8, :].reshape(2 * TILE, 128)
-            return (y * pats[g]).astype(BF16)
+            y = bufs[turn][:, g * 8 : (g + 1) * 8, :]
+            y_ref[0, turn, :, g * 8 : (g + 1) * 8, :] = y.astype(BF16)
+            return (y.reshape(2 * TILE, 128) * pats[g]).astype(BF16)
 
         def use(g, w):
             cols = slice(g * 128, (g + 1) * 128)
@@ -239,7 +247,7 @@
     return pl.BlockSpec(x.shape, lambda k, n=len(x.shape): (0,) * n)
 
 
-HBM = pl.BlockSpec(memory_space=pltpu.HBM)
+WHOLE = pl.BlockSpec(memory_space=pltpu.VMEM)
 Y_BLOCK = (1, 4, TILE // 4, 64, 128)
 
 
@@ -247,14 +255,14 @@
     args = (nbr, rad, *firsts, *seconds)
     out_shape = [
         jax.ShapeDtypeStruct((NBR, POOL, WIDTH), BF16),
-        jax.ShapeDtypeStruct((NBR // 2,) + Y_BLOCK[1:], F32),
+        jax.ShapeDtypeStruct((NBR // 2,) + Y_BLOCK[1:], BF16),
         jax.ShapeDtypeStruct((64, 2, 8, 640), BF16),
         jax.ShapeDtypeStruct((8, 128), F32),
     ]
     return pl.pallas_call(
         leaf_a_kernel,
         grid=(NBR // 2,),
-        in_specs=[HBM] + [full(x) for x in args],
+        in_specs=[WHOLE] + [full(x) for x in args],
         out_specs=[
             pl.BlockSpec((2, POOL, WIDTH), lambda k: (k, 0, 0)),
             pl.BlockSpec(Y_BLOCK, lambda k: (k, 0, 0, 0, 0)),
@@ -263,35 +271,36 @@
         ],
         out_shape=out_shape,
         scratch_shapes=[
-            pltpu.VMEM((64, 2, 8, WIDTH), BF16),
             pltpu.VMEM((POOL * 8, 128), F32),
             pltpu.VMEM((POOL * 8 + 8, 128), F32),
             pltpu.VMEM((NBR, 4, 128), jnp.int32),
             pltpu.VMEM((POOL, WIDTH), F32),
             pltpu.VMEM((8, WIDTH), F32),
+        ]
+        + [pltpu.VMEM((TILE // 4, 64, 128), F32)] * 4
+        + [
             pltpu.VMEM((8, 128), jnp.int32),
             pltpu.SMEM((8, 128), jnp.int32),
             pltpu.SMEM((NBR, 4, 128), jnp.int32),
             pltpu.SemaphoreType.DMA,
             pltpu.SemaphoreType.DMA,
         ],
-        compiler_params=pltpu.CompilerParams(vmem_limit_bytes=56 << 20),
-        cost_estimate=pl.CostEstimate(flops=6 << 30, bytes_accessed=50 << 20, transcendentals=8 << 20),
+        compiler_params=pltpu.CompilerParams(vmem_limit_bytes=44 << 20),
+        cost_estimate=pl.CostEstimate(flops=6 << 30, bytes_accessed=34 << 20, transcendentals=8 << 20),
         name="leaf_a",
     )(got, *args)
 
 
 def leaf_b_kernel(
-    u_ref, y_ref, got_hbm, occ_ref,
+    u_ref, y_ref, got_ref, occ_ref,
     t0, t1a, t1b, t2, t3,
     s0, s1a, s1b, s2, s3,
-    sum_ref, out_ref, acc_ref, half_t_ref, got_ref,
+    sum_ref, out_ref, acc_ref, half_t_ref,
 ):
     step = pl.program_id(0)
 
     @pl.when(step == 0)
     def _():
-        pltpu.sync_copy(got_hbm, got_ref)
         acc_ref[...] = jnp.zeros_like(acc_ref)
         top = iota((8, WIDTH), 0) < 4
         for part in range(POOL // TILE):
@@ -305,7 +314,7 @@
             def use(g, value):
                 half_t_ref[rows, g * 128 : (g + 1) * 128] = 0.5 * value
 
-            mix_blocks(lambda g: grad[:, g * 128 : (g + 1) * 128], s0, s1a, s1b, s2, s3, use)
+            mix_blocks(lambda g: grad[:, g * 128 : (g + 1) * 128], s0, s1a, s1b, s2, s3, use, True)
 
     for turn in range(4):
         rows = pl.ds(turn * TILE, TILE)
@@ -323,7 +332,8 @@
             return both(*out)
 
         def use(g, s):
-            prods[g] = s * y_ref[0, turn, :, g * 8 : (g + 1) * 8, :].reshape(2 * TILE, 128)
+            y = y_ref[0, turn, :, g * 8 : (g + 1) * 8, :].astype(F32)
+            prods[g] = s * y.reshape(2 * TILE, 128)
 
         mix_blocks(piece, t0, t1a, t1b, t2, t3, use)
         low = iota((2 * TILE, 128), 1) < 64
@@ -348,15 +358,15 @@
         out_ref[...] = 0.5 * occ * jnp.transpose(acc_ref[...])[0:64, :]
 
 
-def leaf_b(u, y, got, occ, firsts_t, seconds_t, sums):
-    args = (occ, *firsts_t, *seconds_t, sums)
+def leaf_b(u, y, got, occ, firsts_t, seconds, sums):
+    args = (occ, *firsts_t, *seconds, sums)
     return pl.pallas_call(
         leaf_b_kernel,
         grid=(NBR // 2,),
         in_specs=[
             pl.BlockSpec((2, POOL, WIDTH), lambda k: (k, 0, 0)),
             pl.BlockSpec(Y_BLOCK, lambda k: (k, 0, 0, 0, 0)),
-            HBM,
+            WHOLE,
         ]
         + [full(x) for x in args],
         out_specs=pl.BlockSpec((64, POOL), lambda k: (0, 0)),
@@ -364,10 +374,9 @@
         scratch_shapes=[
             pltpu.VMEM((POOL, 128), F32),
             pltpu.VMEM((POOL, WIDTH), F32),
-            pltpu.VMEM((64, 2, 8, WIDTH), BF16),
         ],
-        compiler_params=pltpu.CompilerParams(vmem_limit_bytes=56 << 20),
-        cost_estimate=pl.CostEstimate(flops=6 << 30, bytes_accessed=50 << 20, transcendentals=8 << 20),
+        compiler_params=pltpu.CompilerParams(vmem_limit_bytes=44 << 20),
+        cost_estimate=pl.CostEstimate(flops=6 << 30, bytes_accessed=34 << 20, transcendentals=8 << 20),
         name="leaf_b",
     )(u, y, got, *args)
 
@@ -517,14 +526,13 @@
     firsts = (first_zero, first_one, first_two, first_three)
     seconds = (second_zero, second_one, second_two, second_three)
     got = got.reshape(64, 2, 8, WIDTH)
-    u, y, back, occ = leaf_a(
-        got, neighbours, rad, blocks(firsts, 0.5, False), blocks(seconds, 1.0, False)
-    )
+    firsts_t = blocks(firsts, 0.5, True)
+    seconds = blocks(seconds, 1.0, False)
+    mats = tree_mats(lift_leaf, lift_branch, couple_root, couple_branch, couple_leaf)
+    got, firsts_t, mats = lax.optimization_barrier((got, firsts_t, mats))
+    u, y, back, occ = leaf_a(got, neighbours, rad, blocks(firsts, 0.5, False), seconds)
     ret = swap(back.reshape(128, 8, 640))
-    grads = leaf_b(
-        u, y, got, occ, blocks(firsts, 0.5, True), blocks(seconds, 1.0, True), degree_table()
-    )
-    mats = tree_mats(lift_leaf, lift_branch, couple_root, couple_branch, couple_leaf)
+    grads = leaf_b(u, y, got, occ, firsts_t, seconds, degree_table())
     updated = finish(ret.reshape(1024, 640), features, leaf_row, mats)
     return updated, grads
 

time: 118 us -> 110 us (0.932)
  Pallas kernels: 63.7 us -> 56.5 us
  local copies, waits for them, and re-layouts: 17.6 us -> 16 us
    pallas_call x1, Pallas kernels: 26 us -> 21 us  [leaf_b(): pl.pallas_call(leaf_b_kernel, grid=(NBR // 2,), in_specs=[pl.BlockSpec((2...]
    pallas_call x1, Pallas kernels: 28.5 us -> 26.4 us  [leaf_a(): pl.pallas_call(leaf_a_kernel, grid=(NBR // 2,), in_specs=[WHOLE] + [full(...]
    add x3, other arithmetic: 1.46 us -> 0.24 us  [blocks(): w3 = jnp.pad(m3, ((0, 64), (0, 64))) + jnp.pad(m3, ((64, 0), (64, 0)))]
  transfers between devices with their start and end apart: 2 -> 2, of which waited for: 1 -> 1; matrix products, arithmetic and copies ran while one was open for 20% -> 18% of each run, Pallas kernels for 22% -> 19%
where the time goes in v5:
time: 110 us; the launch traced here: 109 us
  Pallas kernels  56.5 us (51%)
  starting transfers between devices  17.2 us (16%)
  local copies, waits for them, and re-layouts  16 us (15%)
  waiting for transfers between devices  11 us (10%)
  other arithmetic  7.49 us (7%)
    pallas_call x1, Pallas kernels, leaf_a(): pl.pallas_call(leaf_a_kernel, grid=(NBR // 2,), in_specs=[WHOLE] + [full(...  26.4 us
    pallas_call x1, Pallas kernels, leaf_b(): pl.pallas_call(leaf_b_kernel, grid=(NBR // 2,), in_specs=[pl.BlockSpec((2...  21 us
    all_to_all x2, starting transfers between devices, swap(): return lax.all_to_all(x, AXES, split_axis=0, concat_axis=0, tiled=True)  17.2 us
    all_to_all x2, waiting for transfers between devices, swap(): return lax.all_to_all(x, AXES, split_axis=0, concat_axis=0, tiled=True)  11 us
    unnamed x46, local copies, waits for them, and re-layouts  5.69 us
    pallas_call x1, Pallas kernels, finish(): pl.pallas_call(finish_kernel, out_shape=jax.ShapeDtypeStruct((ROWS, WIDTH...  4.95 us
    pallas_call x1, Pallas kernels, pack(): pl.pallas_call(pack_kernel, out_shape=jax.ShapeDtypeStruct((128 * 8, WIDT...  4.26 us
  transfers between devices with their start and end apart: 2, of which 1 were waited for; matrix products, arithmetic and copies ran while one was open for 18% of the time, Pallas kernels for 19%

profile of v5, /device:TPU:0, one launch (start us, length us, event | category | flops | bytes accessed | tf_op | source)
XLA Modules:
  0.0 109.1 jit_solution(16365310912365754412)
XLA Ops:
  0.6 4.3 %pack.1 = bf16[1024,1024]{1,0:T(8,128)(2,1)} custom-call(s32[1,256]{1,0:T(1,128)} %bitcast.68, bf16[256,1024]{1,0:T(8,128)(2,1)} %feat_ref.3, bf16[256,1024]{1,0:T(8,128)(2,1)} %grad_ref.1), custom_call_target="tpu_custom_call" | custom-call | tf_op jit(solution)/shard_map/pack/pallas_call | solution.py:61
  4.9 0.0 copy-start.15
  4.9 0.0 copy-start.13
  4.9 11.2 %all-to-all-start = ((bf16[128,8,1024]{2,1,0:T(8,128)(2,1)}), bf16[128,8,1024]{2,1,0:T(8,128)(2,1)S(1)}, u32[]{:S(2)}, u32[]{:S(2)}) async-start(bf16[128,8,1024]{2,1,0:T(8,128)(2,1)} %bitcast.56), calls=%async_computation | async-start | bytes 4194304 | tf_op jit(solution)/shard_map/all_to_all | solution.py:499
  16.1 0.0 copy-start.14
  16.1 0.0 copy-start.12
  16.2 0.1 copy.39
  16.3 0.1 pad_add_fusion.4
  16.4 0.1 copy.50.f3
  16.5 0.1 copy.38
  16.6 0.7 copy.42
  17.3 0.6 broadcast_multiply_fusion.2
  17.9 0.7 copy.40
  18.6 0.7 copy.44
  19.4 0.7 copy.49.f2
  20.1 0.1 copy.37
  20.2 0.7 broadcast_multiply_fusion.1
  20.9 0.7 copy.52
  21.6 0.1 multiply_bitcast_fusion.1
  21.7 0.1 copy.41
  21.8 0.7 reshape.69.root_ref
  22.5 0.1 copy.36
  22.7 0.8 copy.46.f0
  23.4 0.8 copy.45
  24.3 0.9 multiply_bitcast_fusion
  25.2 1.4 %copy.43 = f32[16,8,16,8]{3,2,1,0:T(8,128)S(1)} copy(f32[16,8,16,8]{2,0,3,1:T(8,128)} %multiply_bitcast_fusion) | data formatting | bytes 131072 | tf_op jit(solution)/shard_map/transpose | solution.py:486
  26.6 0.0 copy-start.6
  26.7 1.1 reshape.74
  27.7 1.0 pad.70.rad_ref
  28.8 0.1 pad_add_fusion.3.s3
  28.8 0.1 pad_add_fusion.5.t3
  28.9 0.9 slice_bitcast_fusion.11
  29.8 1.5 %pad_maximum_fusion.4.mid_ref = f32[64,64]{1,0:T(8,128)} fusion(f32[64,16]{1,0:T(8,128)S(1)} %bitcast.65, f32[64,16]{1,0:T(8,128)S(1)} %bitcast.67, f32[64,16]{1,0:T(8,128)S(1)} %bitcast.66, f32[64,16]{1,0:T(8,128)} %bitcast.64), kind=kLoop, calls=%fused_computation.11 | loop fusion | flops 12288 | bytes 32768 | tf_op jit(solution)/shard_map/concatenate | solution.py:485
  31.3 0.8 pad_add_fusion.s2
  32.1 1.5 %pad_maximum_fusion.low_ref = f32[128,144]{1,0:T(8,128)} fusion(f32[128,16]{1,0:T(8,128)} %bitcast.61, f32[128,128]{1,0:T(8,128)} %reshape.74), kind=kLoop, calls=%fused_computation.1 | loop fusion | flops 18432 | bytes 147456 | tf_op jit(solution)/shard_map/concatenate | solution.py:488
  33.6 1.1 fusion.6
  34.7 0.8 fusion.4
  35.5 11.0 %all-to-all-done = bf16[128,8,1024]{2,1,0:T(8,128)(2,1)S(1)} async-done(((bf16[128,8,1024]{2,1,0:T(8,128)(2,1)}), bf16[128,8,1024]{2,1,0:T(8,128)(2,1)S(1)}, u32[]{:S(2)}, u32[]{:S(2)}) %all-to-all-start) | async-done | bytes 2097184 | tf_op jit(solution)/shard_map/all_to_all | solution.py:499
  46.5 0.9 copy-done.1
  47.4 0.9 copy-done.2
  48.3 0.9 copy-done.3
  49.2 0.9 copy-done.4
  50.1 26.4 %leaf_a.1 = (bf16[16,512,1024]{2,1,0:T(8,128)(2,1)}, bf16[8,4,32,64,128]{4,3,2,1,0:T(8,128)(2,1)}, bf16[64,2,8,640]{3,2,1,0:T(8,128)(2,1)}, f32[8,128]{1,0:T(8,128)S(1)}) custom-call(bf16[64,2,8,1024]{3,2,1,0:T(8,128)(2,1)S(1)} %bitcast.54, s32[16,512]{1,0:T(8,128)S(1)} %copy-done.6, f32[512,128]{1,0:T(8,128)S(1)} %pad.70.rad_ref, ...), custom_call_target="tpu_custom_call" | custom-call | flops 6442450944 | bytes 35651584 | tf_op jit(solution)/shard_map/leaf_a/pallas_call | solution.py:262
  76.5 0.0 copy-start.5
  76.5 6.0 %all-to-all-start.1 = ((bf16[128,8,640]{2,1,0:T(8,128)(2,1)}), bf16[128,8,640]{2,1,0:T(8,128)(2,1)}, u32[]{:S(2)}, u32[]{:S(2)}) async-start(bf16[128,8,640]{2,1,0:T(8,128)(2,1)} %bitcast.32), calls=%async_computation.1 | async-start | bytes 2621440 | tf_op jit(solution)/shard_map/all_to_all | solution.py:499
  82.5 0.7 copy.51.up2_ref
  83.2 21.0 %leaf_b.1 = f32[64,512]{1,0:T(8,128)} custom-call(bf16[16,512,1024]{2,1,0:T(8,128)(2,1)} %get-tuple-element.24.u_ref, bf16[8,4,32,64,128]{4,3,2,1,0:T(8,128)(2,1)} %get-tuple-element.25.y_ref, bf16[64,2,8,1024]{3,2,1,0:T(8,128)(2,1)S(1)} %bitcast.55, f32[8,128]{1,0:T(8,128)S(1)} %get-tuple-element.26.occ_ref, bf16[256,256]{1,0:T(8,128)(2,1)S(1)} %get-tuple-element.27.t0, ...), custom_call_target="tpu_custom_call" | custom-call | flops 6442450944 | bytes 35651584 | tf_op jit(solution)/shard_map/leaf_b/pallas_call | solution.py:363
  104.2 5.0 %finish.1 = bf16[256,1024]{1,0:T(8,128)(2,1)} custom-call(bf16[1024,640]{1,0:T(8,128)(2,1)} %bitcast.33.ret_ref, bf16[256,1024]{1,0:T(8,128)(2,1)} %feat_ref.3, s32[1,256]{1,0:T(1,128)} %bitcast.69, f32[16,128]{1,0:T(8,128)} %copy.51.up2_ref, f32[64,16]{1,0:T(8,128)} %bitcast.62, f32[64,64]{1,0:T(8,128)} %reshape.69.root_ref, ...), custom_call_target="tpu_custom_call" | custom-call | tf_op jit(solution)/shard_map/finish/pallas_call | solution.py:459
  (38 shorter events, 0.1 us)
Async XLA Ops:
  4.9 11.3 %copy-start.19 = (bf16[64,64]{1,0:T(8,128)(2,1)S(1)}, bf16[64,64]{1,0:T(8,128)(2,1)}, u32[]{:S(2)}) copy-start(bf16[64,64]{1,0:T(8,128)(2,1)} %param.27) | copy-start | bytes 24580
  4.9 11.6 %copy-start.17 = (bf16[128,128]{1,0:T(8,128)(2,1)S(1)}, bf16[128,128]{1,0:T(8,128)(2,1)}, u32[]{:S(2)}) copy-start(bf16[128,128]{1,0:T(8,128)(2,1)} %param.26) | copy-start | bytes 98308
  4.9 11.7 %copy-start.11 = (f32[4,16,16]{2,1,0:T(8,128)S(1)}, f32[4,16,16]{2,1,0:T(8,128)}, u32[]{:S(2)}) copy-start(f32[4,16,16]{2,1,0:T(8,128)} %param.33) | copy-start | bytes 12292
  4.9 13.0 %copy-start.9 = (f32[8,16,16]{2,1,0:T(8,128)S(1)}, f32[8,16,16]{2,1,0:T(8,128)}, u32[]{:S(2)}) copy-start(f32[8,16,16]{2,1,0:T(8,128)} %param.32) | copy-start | bytes 24580
  4.9 15.2 %copy-start.15 = (bf16[192,192]{1,0:T(8,128)(2,1)S(1)}, bf16[192,192]{1,0:T(8,128)(2,1)}, u32[]{:S(2)}) copy-start(bf16[192,192]{1,0:T(8,128)(2,1)} %param.25) | copy-start | bytes 221188
  4.9 16.7 %copy-start.13 = (f32[4,4,16,16]{3,2,1,0:T(8,128)S(1)}, f32[4,4,16,16]{3,2,1,0:T(8,128)}, u32[]{:S(2)}) copy-start(f32[4,4,16,16]{3,2,1,0:T(8,128)} %param.34) | copy-start | bytes 49156
  4.9 41.5 %all-to-all-start = ((bf16[128,8,1024]{2,1,0:T(8,128)(2,1)}), bf16[128,8,1024]{2,1,0:T(8,128)(2,1)S(1)}, u32[]{:S(2)}, u32[]{:S(2)}) async-start(bf16[128,8,1024]{2,1,0:T(8,128)(2,1)} %bitcast.56), calls=%async_computation | async-start | bytes 4194304 | tf_op jit(solution)/shard_map/all_to_all | solution.py:499
  16.1 6.4 %copy-start.14 = (bf16[256,256]{1,0:T(8,128)(2,1)S(1)}, bf16[256,256]{1,0:T(8,128)(2,1)}, u32[]{:S(2)}) copy-start(bf16[256,256]{1,0:T(8,128)(2,1)} %param.24) | copy-start | bytes 393220
  16.1 7.3 %copy-start.12 = (f32[64,512]{1,0:T(8,128)S(1)}, f32[64,512]{1,0:T(8,128)}, u32[]{:S(2)}) copy-start(f32[64,512]{1,0:T(8,128)} %param.23) | copy-start | bytes 393220
  16.1 8.1 %copy-start.7 = (f32[8,8,16,16]{3,2,1,0:T(8,128)S(1)}, f32[8,8,16,16]{3,2,1,0:T(8,128)}, u32[]{:S(2)}) copy-start(f32[8,8,16,16]{3,2,1,0:T(8,128)} %param.36) | copy-start | bytes 196612
  25.2 3.5 %copy-start.18 = (bf16[64,64]{1,0:T(8,128)(2,1)S(1)}, bf16[64,64]{1,0:T(8,128)(2,1)}, u32[]{:S(2)}) copy-start(bf16[64,64]{1,0:T(8,128)(2,1)} %param.31) | copy-start | bytes 24580
  26.6 19.8 %copy-start = (bf16[256,256]{1,0:T(8,128)(2,1)S(1)}, bf16[256,256]{1,0:T(8,128)(2,1)}, u32[]{:S(2)}) copy-start(bf16[256,256]{1,0:T(8,128)(2,1)} %s0.3) | copy-start | bytes 393220
  26.6 19.8 %copy-start.6 = (s32[16,512]{1,0:T(8,128)S(1)}, s32[16,512]{1,0:T(8,128)}, u32[]{:S(2)}) copy-start(s32[16,512]{1,0:T(8,128)} %nbr_ref.1) | copy-start | bytes 98308
  27.7 7.0 %copy-start.8 = (bf16[192,192]{1,0:T(8,128)(2,1)S(1)}, bf16[192,192]{1,0:T(8,128)(2,1)}, u32[]{:S(2)}) copy-start(bf16[192,192]{1,0:T(8,128)(2,1)} %copy.52) | copy-start | bytes 221188
  27.7 7.0 %copy-start.16 = (bf16[192,192]{1,0:T(8,128)(2,1)S(1)}, bf16[192,192]{1,0:T(8,128)(2,1)}, u32[]{:S(2)}) copy-start(bf16[192,192]{1,0:T(8,128)(2,1)} %param.29) | copy-start | bytes 221188
  46.5 0.9 copy-start.1
  47.4 0.9 copy-start.2
  48.3 0.9 copy-start.3
  49.2 0.9 copy-start.4
  76.5 6.1 %copy-start.10 = (f32[16,16,8]{0,2,1:T(8,128)S(1)}, f32[16,16,8]{0,2,1:T(8,128)}, u32[]{:S(2)}) copy-start(f32[16,16,8]{0,2,1:T(8,128)} %copy.40) | copy-start | bytes 24580
  76.5 6.7 %copy-start.5 = (bf16[256,128]{1,0:T(8,128)(2,1)S(1)}, bf16[256,128]{1,0:T(8,128)(2,1)}, u32[]{:S(2)}) copy-start(bf16[256,128]{1,0:T(8,128)(2,1)} %constant.4.clone.sum_ref) | copy-start | bytes 196612
  76.5 27.7 %all-to-all-start.1 = ((bf16[128,8,640]{2,1,0:T(8,128)(2,1)}), bf16[128,8,640]{2,1,0:T(8,128)(2,1)}, u32[]{:S(2)}, u32[]{:S(2)}) async-start(bf16[128,8,640]{2,1,0:T(8,128)(2,1)} %bitcast.32), calls=%async_computation.1 | async-start | bytes 2621440 | tf_op jit(solution)/shard_map/all_to_all | solution.py:499

commit v6 on v5

--- a/solution.py
+++ b/solution.py
@@ -38,31 +38,40 @@
     return high, (x - high.astype(F32)).astype(BF16)
 
 
-def pack_kernel(leaf_ref, feat_ref, grad_ref, send_ref):
-    row = leaf_ref[...]
-    col = col_of(row)[:, 0:1]
+def pack_kernel(leaf_ref, feat_ref, grad_ref, send_ref, slot_ref):
+    part = pl.program_id(0)
     n = ROWS
-    same = (col == row) & (iota((n, n), 0) < iota((n, n), 1))
-    rank = jnp.sum(jnp.where(same, 1.0, 0.0), axis=0, keepdims=True).astype(jnp.int32)
-    slot = row * 8 + rank
-    ones = jnp.ones((n, 128), BF16)
-    for part in range(4):
-        index = iota((n, n), 0) + part * n
-        pick_f = jnp.where(index == slot, 1.0, 0.0).astype(BF16)
-        pick_g = jnp.where(index == slot + 4, 1.0, 0.0).astype(BF16)
-        there = dot(pick_f, ones)
-        gone = (there < 0.5) & ((iota((n, 128), 0) & 7) < 4)
-        out = dot(pick_f, feat_ref[...]) + dot(pick_g, grad_ref[...])
-        send_ref[part * n : (part + 1) * n, 128:] = out[:, 128:].astype(BF16)
-        send_ref[part * n : (part + 1) * n, :128] = jnp.where(gone, EMPTY, out[:, :128]).astype(BF16)
+
+    @pl.when(part == 0)
+    def _():
+        row = leaf_ref[...]
+        col = col_of(row)[:, 0:1]
+        same = (col == row) & (iota((n, n), 0) < iota((n, n), 1))
+        rank = jnp.sum(jnp.where(same, 1.0, 0.0), axis=0, keepdims=True).astype(jnp.int32)
+        slot_ref[...] = jnp.broadcast_to(row * 8 + rank, (8, n))
+
+    slot = slot_ref[0:1, :]
+    index = iota((n, n), 0) + part * n
+    pick_f = jnp.where(index == slot, 1.0, 0.0).astype(BF16)
+    pick_g = jnp.where(index == slot + 4, 1.0, 0.0).astype(BF16)
+    there = dot(pick_f, jnp.ones((n, 128), BF16))
+    gone = (there < 0.5) & ((iota((n, 128), 0) & 7) < 4)
+    out = dot(pick_f, feat_ref[...]) + dot(pick_g, grad_ref[...])
+    send_ref[:, 128:] = out[:, 128:].astype(BF16)
+    send_ref[:, :128] = jnp.where(gone, EMPTY, out[:, :128]).astype(BF16)
 
 
 def pack(leaf_row, features, cotangent):
+    args = (leaf_row, features, cotangent)
     return pl.pallas_call(
         pack_kernel,
+        grid=(4,),
+        in_specs=[full(x) for x in args],
+        out_specs=pl.BlockSpec((ROWS, WIDTH), lambda k: (k, 0)),
         out_shape=jax.ShapeDtypeStruct((128 * 8, WIDTH), BF16),
+        scratch_shapes=[pltpu.VMEM((8, ROWS), jnp.int32)],
         name="pack",
-    )(leaf_row, features, cotangent)
+    )(*args)
 
 
 def mix(x, w0, w1a, w1b, w2, w3):
@@ -134,7 +143,7 @@
     got_ref,
     nbr_ref,
     rad_ref,
-    f0, f1a, f1b, f2, f3,
+    f0_hbm, f1a_hbm, f1b_hbm, f2_hbm, f3_hbm,
     s0, s1a, s1b, s2, s3,
     u_ref,
     y_ref,
@@ -152,13 +161,19 @@
     rank_ref,
     rank_smem,
     index_smem,
+    f0, f1a, f1b, f2, f3,
     sem0,
     sem1,
+    sems,
 ):
     step = pl.program_id(0)
+    pairs = ((f0_hbm, f0), (f1a_hbm, f1a), (f1b_hbm, f1b), (f2_hbm, f2), (f3_hbm, f3))
+    weights = [pltpu.make_async_copy(a, b, sems.at[i]) for i, (a, b) in enumerate(pairs)]
 
     @pl.when(step == 0)
     def _():
+        for copy in weights:
+            copy.start()
         first = jnp.where(iota((8, 128), 1) == 0, 1.0, 0.0).astype(BF16)
         got0 = got_ref[:, :, :, 0:128].reshape(1024, 128)
         lead = lax.dot_general(first, got0, (((1,), (1,)), ((), ())), preferred_element_type=F32)
@@ -200,6 +215,8 @@
             table_ref[pl.ds(to, 8), :] = own_ref[i * 8 : (i + 1) * 8, :]
         index_to_smem.wait()
         gather(index_smem, 0, 0, own_ref, table_ref, buf0)
+        for copy in weights:
+            copy.wait()
 
     bufs = (buf0, buf1, buf2, buf3)
     for turn in range(4):
@@ -248,11 +265,11 @@
 
 
 WHOLE = pl.BlockSpec(memory_space=pltpu.VMEM)
+HBM = pl.BlockSpec(memory_space=pltpu.HBM)
 Y_BLOCK = (1, 4, TILE // 4, 64, 128)
 
 
 def leaf_a(got, nbr, rad, firsts, seconds):
-    args = (nbr, rad, *firsts, *seconds)
     out_shape = [
         jax.ShapeDtypeStruct((NBR, POOL, WIDTH), BF16),
         jax.ShapeDtypeStruct((NBR // 2,) + Y_BLOCK[1:], BF16),
@@ -262,7 +279,7 @@
     return pl.pallas_call(
         leaf_a_kernel,
         grid=(NBR // 2,),
-        in_specs=[WHOLE] + [full(x) for x in args],
+        in_specs=[WHOLE, full(nbr), full(rad)] + [HBM] * 5 + [full(x) for x in seconds],
         out_specs=[
             pl.BlockSpec((2, POOL, WIDTH), lambda k: (k, 0, 0)),
             pl.BlockSpec(Y_BLOCK, lambda k: (k, 0, 0, 0, 0)),
@@ -282,13 +299,17 @@
             pltpu.VMEM((8, 128), jnp.int32),
             pltpu.SMEM((8, 128), jnp.int32),
             pltpu.SMEM((NBR, 4, 128), jnp.int32),
+        ]
+        + [pltpu.VMEM(x.shape, BF16) for x in firsts]
+        + [
             pltpu.SemaphoreType.DMA,
             pltpu.SemaphoreType.DMA,
+            pltpu.SemaphoreType.DMA((5,)),
         ],
-        compiler_params=pltpu.CompilerParams(vmem_limit_bytes=44 << 20),
+        compiler_params=pltpu.CompilerParams(vmem_limit_bytes=60 << 20),
         cost_estimate=pl.CostEstimate(flops=6 << 30, bytes_accessed=34 << 20, transcendentals=8 << 20),
         name="leaf_a",
-    )(got, *args)
+    )(got, nbr, rad, *firsts, *seconds)
 
 
 def leaf_b_kernel(

time: 110 us -> 110 us (level)
  local copies, waits for them, and re-layouts: 16 us -> 13.3 us
  Pallas kernels: 56.5 us -> 59 us
  other arithmetic: 7.49 us -> 9.53 us
  waiting for transfers between devices: 11 us -> 9.34 us
    unnamed x46 -> x48, local copies, waits for them, and re-layouts: 5.69 us -> 2.66 us
    pallas_call x2, Pallas kernels: 30.6 us -> 33 us  [the longest x1 28.5 us: leaf_a(): pl.pallas_call(leaf_a_kernel, grid=(NBR // 2,), in_specs=[WHOLE, full(nbr...]
    all_to_all x2, waiting for transfers between devices: 11 us -> 9.34 us  [swap(): return lax.all_to_all(x, AXES, split_axis=0, concat_axis=0, tiled=True)]
    add x3, other arithmetic: 0.24 us -> 1.64 us  [blocks(): w3 = jnp.pad(m3, ((0, 64), (0, 64))) + jnp.pad(m3, ((64, 0), (64, 0)))]
  transfers between devices with their start and end apart: 2 -> 2, of which waited for: 1 -> 1; matrix products, arithmetic and copies ran while one was open for 18% -> 20% of each run, Pallas kernels for 19% -> 19%
where the time goes in v6:
time: 110 us; the launch traced here: 109 us
  Pallas kernels  59 us (54%)
  starting transfers between devices  17.2 us (16%)
  local copies, waits for them, and re-layouts  13.3 us (12%)
  other arithmetic  9.53 us (9%)
  waiting for transfers between devices  9.34 us (8%)
    pallas_call x1, Pallas kernels, leaf_a(): pl.pallas_call(leaf_a_kernel, grid=(NBR // 2,), in_specs=[WHOLE, full(nbr...  28.5 us
    pallas_call x1, Pallas kernels, leaf_b(): pl.pallas_call(leaf_b_kernel, grid=(NBR // 2,), in_specs=[pl.BlockSpec((2...  21 us
    all_to_all x2, starting transfers between devices, swap(): return lax.all_to_all(x, AXES, split_axis=0, concat_axis=0, tiled=True)  17.2 us
    all_to_all x2, waiting for transfers between devices, swap(): return lax.all_to_all(x, AXES, split_axis=0, concat_axis=0, tiled=True)  9.34 us
    pallas_call x1, Pallas kernels, finish(): pl.pallas_call(finish_kernel, out_shape=jax.ShapeDtypeStruct((ROWS, WIDTH...  4.95 us
    pallas_call x1, Pallas kernels, pack(): pl.pallas_call(pack_kernel, grid=(4,), in_specs=[full(x) for x in args],...  4.56 us
    unnamed x48, local copies, waits for them, and re-layouts  2.66 us
  transfers between devices with their start and end apart: 2, of which 1 were waited for; matrix products, arithmetic and copies ran while one was open for 20% of the time, Pallas kernels for 19%

profile of v6, /device:TPU:0, one launch (start us, length us, event | category | flops | bytes accessed | tf_op | source)
XLA Modules:
  0.0 109.3 jit_solution(2053812460369392960)
XLA Ops:
  0.6 4.6 %pack.1 = bf16[1024,1024]{1,0:T(8,128)(2,1)} custom-call(s32[1,256]{1,0:T(1,128)} %bitcast.69, bf16[256,1024]{1,0:T(8,128)(2,1)} %feat_ref.3, bf16[256,1024]{1,0:T(8,128)(2,1)} %grad_ref.1), custom_call_target="tpu_custom_call" | custom-call | tf_op jit(solution)/shard_map/pack/pallas_call | solution.py:66
  5.2 0.0 copy-start.17
  5.2 0.0 copy-start.15
  5.2 11.2 %all-to-all-start = ((bf16[128,8,1024]{2,1,0:T(8,128)(2,1)}), bf16[128,8,1024]{2,1,0:T(8,128)(2,1)S(1)}, u32[]{:S(2)}, u32[]{:S(2)}) async-start(bf16[128,8,1024]{2,1,0:T(8,128)(2,1)} %bitcast.56), calls=%async_computation | async-start | bytes 4194304 | tf_op jit(solution)/shard_map/all_to_all | solution.py:520
  16.4 0.0 copy-start.16
  16.4 0.0 copy-start.14
  16.4 0.0 copy-start.9
  16.5 0.0 copy-done.20
  16.5 0.1 copy.39
  16.6 0.1 pad_add_fusion.4
  16.6 0.7 copy.50.f3_hbm
  17.4 0.0 copy-done.19
  17.4 0.1 copy.38
  17.5 0.7 copy.42
  18.2 0.6 broadcast_multiply_fusion.2
  18.8 0.7 copy.40
  19.5 0.7 copy.44
  20.2 0.8 copy.49.f2_hbm
  21.0 0.1 copy.37
  21.1 0.7 broadcast_multiply_fusion.1
  21.7 0.8 copy.52
  22.5 0.1 multiply_bitcast_fusion.1
  22.6 0.1 copy.41
  22.6 0.7 reshape.69.root_ref
  23.4 0.1 copy.36
  23.5 0.8 copy.46.f0_hbm
  24.3 0.1 copy.45
  24.4 0.9 multiply_bitcast_fusion
  25.3 1.4 %copy.43 = f32[16,8,16,8]{3,2,1,0:T(8,128)S(1)} copy(f32[16,8,16,8]{2,0,3,1:T(8,128)} %multiply_bitcast_fusion) | data formatting | bytes 131072 | tf_op jit(solution)/shard_map/transpose | solution.py:507
  26.7 1.1 reshape.74
  27.8 0.7 pad.70.rad_ref
  28.5 1.5 %pad_add_fusion.3.s3 = bf16[128,128]{1,0:T(8,128)(2,1)} fusion(bf16[64,64]{1,0:T(8,128)(2,1)} %param.31), kind=kLoop, calls=%fused_computation.12 | loop fusion | flops 65536 | bytes 40960 | tf_op jit(solution)/shard_map/add | solution.py:493
  30.0 0.1 pad_add_fusion.5.t3
  30.1 0.9 slice_bitcast_fusion.11
  31.0 1.5 %pad_maximum_fusion.4.mid_ref = f32[64,64]{1,0:T(8,128)} fusion(f32[64,16]{1,0:T(8,128)S(1)} %bitcast.66, f32[64,16]{1,0:T(8,128)S(1)} %bitcast.68, f32[64,16]{1,0:T(8,128)S(1)} %bitcast.67, f32[64,16]{1,0:T(8,128)} %bitcast.65), kind=kLoop, calls=%fused_computation.11 | loop fusion | flops 12288 | bytes 32768 | tf_op jit(solution)/shard_map/concatenate | solution.py:506
  32.4 1.5 %pad_add_fusion.s2 = bf16[256,256]{1,0:T(8,128)(2,1)} fusion(bf16[128,128]{1,0:T(8,128)(2,1)} %param.30), kind=kLoop, calls=%fused_computation.2 | loop fusion | flops 262144 | bytes 163840 | tf_op jit(solution)/shard_map/add | solution.py:492
  33.9 1.5 %pad_maximum_fusion.low_ref = f32[128,144]{1,0:T(8,128)} fusion(f32[128,16]{1,0:T(8,128)} %bitcast.62, f32[128,128]{1,0:T(8,128)} %reshape.74), kind=kLoop, calls=%fused_computation.1 | loop fusion | flops 18432 | bytes 147456 | tf_op jit(solution)/shard_map/concatenate | solution.py:509
  35.5 1.1 fusion.6
  36.6 0.9 fusion.4
  37.4 9.3 %all-to-all-done = bf16[128,8,1024]{2,1,0:T(8,128)(2,1)S(1)} async-done(((bf16[128,8,1024]{2,1,0:T(8,128)(2,1)}), bf16[128,8,1024]{2,1,0:T(8,128)(2,1)S(1)}, u32[]{:S(2)}, u32[]{:S(2)}) %all-to-all-start) | async-done | bytes 2097184 | tf_op jit(solution)/shard_map/all_to_all | solution.py:520
  46.8 1.3 %copy-done = bf16[128,8,1024]{2,1,0:T(8,128)(2,1)} copy-done((bf16[128,8,1024]{2,1,0:T(8,128)(2,1)}, bf16[128,8,1024]{2,1,0:T(8,128)(2,1)S(1)}, u32[]{:S(2)}) %copy-start) | copy-done | bytes 2097176
  48.1 28.5 %leaf_a.1 = (bf16[16,512,1024]{2,1,0:T(8,128)(2,1)}, bf16[8,4,32,64,128]{4,3,2,1,0:T(8,128)(2,1)}, bf16[64,2,8,640]{3,2,1,0:T(8,128)(2,1)}, f32[8,128]{1,0:T(8,128)}) custom-call(bf16[64,2,8,1024]{3,2,1,0:T(8,128)(2,1)} %bitcast.54, s32[16,512]{1,0:T(8,128)} %nbr_ref.1, f32[512,128]{1,0:T(8,128)} %pad.70.rad_ref, bf16[256,256]{1,0:T(8,128)(2,1)} %copy.46.f0_hbm, ...), custom_call_target="tpu_custom_call" | custom-call | flops 6442450944 | bytes 35651584 | tf_op jit(solution)/shard_map/leaf_a/pallas_call | solution.py:279
  76.6 0.0 copy-start.5
  76.6 6.0 %all-to-all-start.1 = ((bf16[128,8,640]{2,1,0:T(8,128)(2,1)}), bf16[128,8,640]{2,1,0:T(8,128)(2,1)}, u32[]{:S(2)}, u32[]{:S(2)}) async-start(bf16[128,8,640]{2,1,0:T(8,128)(2,1)} %bitcast.57), calls=%async_computation.1 | async-start | bytes 2621440 | tf_op jit(solution)/shard_map/all_to_all | solution.py:520
  82.7 0.7 copy.51.up2_ref
  83.4 21.0 %leaf_b.1 = f32[64,512]{1,0:T(8,128)} custom-call(bf16[16,512,1024]{2,1,0:T(8,128)(2,1)} %get-tuple-element.24.u_ref, bf16[8,4,32,64,128]{4,3,2,1,0:T(8,128)(2,1)} %get-tuple-element.25.y_ref, bf16[64,2,8,1024]{3,2,1,0:T(8,128)(2,1)S(1)} %bitcast.55, f32[8,128]{1,0:T(8,128)S(1)} %copy-done.8, bf16[256,256]{1,0:T(8,128)(2,1)S(1)} %get-tuple-element.27.t0, ...), custom_call_target="tpu_custom_call" | custom-call | flops 6442450944 | bytes 35651584 | tf_op jit(solution)/shard_map/leaf_b/pallas_call | solution.py:384
  104.4 0.0 all-to-all-done.1
  104.4 5.0 %finish.1 = bf16[256,1024]{1,0:T(8,128)(2,1)} custom-call(bf16[1024,640]{1,0:T(8,128)(2,1)} %bitcast.33.ret_ref, bf16[256,1024]{1,0:T(8,128)(2,1)} %feat_ref.3, s32[1,256]{1,0:T(1,128)} %bitcast.70, f32[16,128]{1,0:T(8,128)} %copy.51.up2_ref, f32[64,16]{1,0:T(8,128)} %bitcast.63, f32[64,64]{1,0:T(8,128)} %reshape.69.root_ref, ...), custom_call_target="tpu_custom_call" | custom-call | tf_op jit(solution)/shard_map/finish/pallas_call | solution.py:480
  (40 shorter events, 0.1 us)
Async XLA Ops:
  5.2 11.3 %copy-start.20 = (bf16[64,64]{1,0:T(8,128)(2,1)S(1)}, bf16[64,64]{1,0:T(8,128)(2,1)}, u32[]{:S(2)}) copy-start(bf16[64,64]{1,0:T(8,128)(2,1)} %param.27) | copy-start | bytes 24580
  5.2 12.2 %copy-start.19 = (bf16[128,128]{1,0:T(8,128)(2,1)S(1)}, bf16[128,128]{1,0:T(8,128)(2,1)}, u32[]{:S(2)}) copy-start(bf16[128,128]{1,0:T(8,128)(2,1)} %param.26) | copy-start | bytes 98308
  5.2 12.3 %copy-start.13 = (f32[4,16,16]{2,1,0:T(8,128)S(1)}, f32[4,16,16]{2,1,0:T(8,128)}, u32[]{:S(2)}) copy-start(f32[4,16,16]{2,1,0:T(8,128)} %param.33) | copy-start | bytes 12292
  5.2 13.6 %copy-start.11 = (f32[8,16,16]{2,1,0:T(8,128)S(1)}, f32[8,16,16]{2,1,0:T(8,128)}, u32[]{:S(2)}) copy-start(f32[8,16,16]{2,1,0:T(8,128)} %param.32) | copy-start | bytes 24580
  5.2 15.8 %copy-start.17 = (bf16[192,192]{1,0:T(8,128)(2,1)S(1)}, bf16[192,192]{1,0:T(8,128)(2,1)}, u32[]{:S(2)}) copy-start(bf16[192,192]{1,0:T(8,128)(2,1)} %param.25) | copy-start | bytes 221188
  5.2 17.3 %copy-start.15 = (f32[4,4,16,16]{3,2,1,0:T(8,128)S(1)}, f32[4,4,16,16]{3,2,1,0:T(8,128)}, u32[]{:S(2)}) copy-start(f32[4,4,16,16]{3,2,1,0:T(8,128)} %param.34) | copy-start | bytes 49156
  5.2 41.5 %all-to-all-start = ((bf16[128,8,1024]{2,1,0:T(8,128)(2,1)}), bf16[128,8,1024]{2,1,0:T(8,128)(2,1)S(1)}, u32[]{:S(2)}, u32[]{:S(2)}) async-start(bf16[128,8,1024]{2,1,0:T(8,128)(2,1)} %bitcast.56), calls=%async_computation | async-start | bytes 4194304 | tf_op jit(solution)/shard_map/all_to_all | solution.py:520
  16.4 7.0 %copy-start.16 = (bf16[256,256]{1,0:T(8,128)(2,1)S(1)}, bf16[256,256]{1,0:T(8,128)(2,1)}, u32[]{:S(2)}) copy-start(bf16[256,256]{1,0:T(8,128)(2,1)} %param.24) | copy-start | bytes 393220
  16.4 7.8 %copy-start.14 = (f32[64,512]{1,0:T(8,128)S(1)}, f32[64,512]{1,0:T(8,128)}, u32[]{:S(2)}) copy-start(f32[64,512]{1,0:T(8,128)} %param.23) | copy-start | bytes 393220
  16.4 8.0 %copy-start.9 = (f32[8,8,16,16]{3,2,1,0:T(8,128)S(1)}, f32[8,8,16,16]{3,2,1,0:T(8,128)}, u32[]{:S(2)}) copy-start(f32[8,8,16,16]{3,2,1,0:T(8,128)} %param.36) | copy-start | bytes 196612
  27.8 8.7 %copy-start.10 = (bf16[192,192]{1,0:T(8,128)(2,1)S(1)}, bf16[192,192]{1,0:T(8,128)(2,1)}, u32[]{:S(2)}) copy-start(bf16[192,192]{1,0:T(8,128)(2,1)} %copy.52) | copy-start | bytes 221188
  27.8 8.7 %copy-start.18 = (bf16[192,192]{1,0:T(8,128)(2,1)S(1)}, bf16[192,192]{1,0:T(8,128)(2,1)}, u32[]{:S(2)}) copy-start(bf16[192,192]{1,0:T(8,128)(2,1)} %param.29) | copy-start | bytes 221188
  46.8 1.3 %copy-start = (bf16[128,8,1024]{2,1,0:T(8,128)(2,1)}, bf16[128,8,1024]{2,1,0:T(8,128)(2,1)S(1)}, u32[]{:S(2)}) copy-start(bf16[128,8,1024]{2,1,0:T(8,128)(2,1)S(1)} %all-to-all-done) | copy-start | bytes 6291460
  48.1 34.6 %copy-start.12 = (f32[16,16,8]{0,2,1:T(8,128)S(1)}, f32[16,16,8]{0,2,1:T(8,128)}, u32[]{:S(2)}) copy-start(f32[16,16,8]{0,2,1:T(8,128)} %copy.40) | copy-start | bytes 24580
  48.1 35.2 %copy-start.7 = (bf16[256,128]{1,0:T(8,128)(2,1)S(1)}, bf16[256,128]{1,0:T(8,128)(2,1)}, u32[]{:S(2)}) copy-start(bf16[256,128]{1,0:T(8,128)(2,1)} %constant.4.clone.sum_ref) | copy-start | bytes 196612
  76.5 6.8 %copy-start.1 = (bf16[128,8,1024]{2,1,0:T(8,128)(2,1)S(1)}, bf16[128,8,1024]{2,1,0:T(8,128)(2,1)}, u32[]{:S(2)}) copy-start(bf16[128,8,1024]{2,1,0:T(8,128)(2,1)} %copy-done) | copy-start | bytes 6291460
  76.5 6.8 %copy-start.2 = (bf16[256,256]{1,0:T(8,128)(2,1)S(1)}, bf16[256,256]{1,0:T(8,128)(2,1)}, u32[]{:S(2)}) copy-start(bf16[256,256]{1,0:T(8,128)(2,1)} %pad_add_fusion.s2) | copy-start | bytes 393220
  76.6 6.8 %copy-start.3 = (bf16[256,256]{1,0:T(8,128)(2,1)S(1)}, bf16[256,256]{1,0:T(8,128)(2,1)}, u32[]{:S(2)}) copy-start(bf16[256,256]{1,0:T(8,128)(2,1)} %get-tuple-element.46.s1b) | copy-start | bytes 393220
  76.6 6.8 %copy-start.4 = (bf16[256,256]{1,0:T(8,128)(2,1)S(1)}, bf16[256,256]{1,0:T(8,128)(2,1)}, u32[]{:S(2)}) copy-start(bf16[256,256]{1,0:T(8,128)(2,1)} %get-tuple-element.47.s1a) | copy-start | bytes 393220
  76.6 6.8 %copy-start.5 = (bf16[256,256]{1,0:T(8,128)(2,1)S(1)}, bf16[256,256]{1,0:T(8,128)(2,1)}, u32[]{:S(2)}) copy-start(bf16[256,256]{1,0:T(8,128)(2,1)} %s0.3) | copy-start | bytes 393220
  76.6 6.8 %copy-start.6 = (bf16[128,128]{1,0:T(8,128)(2,1)S(1)}, bf16[128,128]{1,0:T(8,128)(2,1)}, u32[]{:S(2)}) copy-start(bf16[128,128]{1,0:T(8,128)(2,1)} %pad_add_fusion.3.s3) | copy-start | bytes 98308
  76.6 6.8 %copy-start.8 = (f32[8,128]{1,0:T(8,128)S(1)}, f32[8,128]{1,0:T(8,128)}, u32[]{:S(2)}) copy-start(f32[8,128]{1,0:T(8,128)} %get-tuple-element.26.occ_ref) | copy-start | bytes 12292
  76.6 27.8 %all-to-all-start.1 = ((bf16[128,8,640]{2,1,0:T(8,128)(2,1)}), bf16[128,8,640]{2,1,0:T(8,128)(2,1)}, u32[]{:S(2)}, u32[]{:S(2)}) async-start(bf16[128,8,640]{2,1,0:T(8,128)(2,1)} %bitcast.57), calls=%async_computation.1 | async-start | bytes 2621440 | tf_op jit(solution)/shard_map/all_to_all | solution.py:520
